TPU v7x, 32 devices: a whole 2x2x4 slice. The times are simulated.
32 devices in a mesh: frames: 8 (over z, x), rows: 4 (over y, core).
Axes of the slice: x: 2, y: 2, z: 4, core: 2. Of those that a mesh axis runs over, the one named last changes fastest.
Arguments:
- latent: bfloat16 [8, 32, 128, 512], P('frames', 'rows'), may hold values from -20 to 20, as said below
- norm_gain: float32 [512], replicated, may hold values from 0.1 to 1.9
- norm_shift: float32 [512], replicated, may hold values from -3 to 3
- conv_one: bfloat16 [3, 3, 512, 512], replicated, may hold values from -0.09375 to 0.09375
- bias_one: float32 [512], replicated, may hold values from -3 to 3
- conv_two: bfloat16 [3, 3, 512, 256], replicated, may hold values from -0.09375 to 0.09375
- bias_two: float32 [256], replicated, may hold values from -3 to 3
- temporal_weight: bfloat16 [3, 256, 256], replicated, may hold values from -0.21875 to 0.21875
- bias_temporal: float32 [256], replicated, may hold values from -3 to 3
- clip_ids: int32 [8], replicated, may hold values from 0 to 3, never falling along the last dimension, each value on 1 to 4 neighbouring positions
Outputs:
- decoded: bfloat16 [8, 64, 256, 256], P(None, 'rows', 'frames')
Inputs may be any that keep to these rules, and one draw needn't show every extreme that they name: latent is of order one; its scale varies over rows and channels. `clip_ids`: clip numbers never fall along the frames; each clip has 1 to 4 frames and one has exactly 4.
All inputs are finite; a program needn't handle non-finite values.
Results may differ from a plain program's by a relative error of at most 0.006.
Values may be sent and summed in bfloat16 or wider, within the bound.
No kernel may reach another device: no remote copies, remote signals or barrier semaphores. Data moves between devices by JAX's collectives and lax.ppermute only.
A program may use at most 64 MiB of HBM per device.

v0:
```python
import jax
import jax.numpy as jnp
from jax import lax
from jax.sharding import PartitionSpec as P

GROUPS = 32
TEMPORAL_TAPS = 3
FRAME_DILATION = 2


GN_EPS = 1e-06


def with_halo(value, sides, width):
    for axis, dim in sides:
        peers, length = (lax.axis_size(axis), value.shape[dim])
        up = [(i, (i + 1) % peers) for i in range(peers - 1)]
        down = [(j, i) for i, j in up]
        last = lax.slice_in_dim(value, length - width, length, axis=dim)
        leading = lax.slice_in_dim(value, 0, width, axis=dim)
        before = lax.ppermute(last, axis, up)
        after = lax.ppermute(leading, axis, down)
        value = jnp.concatenate([before, value, after], axis=dim)
    return value


def convolve_rows(padded, weights):
    return lax.conv_general_dilated(
        padded,
        weights,
        (1, 1),
        ((0, 0), (1, 1)),
        dimension_numbers=("NHWC", "HWIO", "NHWC"),
        preferred_element_type=jnp.float32,
    )


def clip_starts(clip_ids):
    frame_positions = jnp.arange(clip_ids.shape[0], dtype=jnp.int32)
    same_clip = clip_ids[:, None] == clip_ids[None, :]
    return jnp.min(jnp.where(same_clip, frame_positions[None, :], clip_ids.shape[0]), axis=1)


def enlarge(features):
    return jnp.repeat(jnp.repeat(features, 2, axis=1), 2, axis=2)


def per_device(
    latent,
    norm_gain,
    norm_shift,
    conv_one,
    bias_one,
    conv_two,
    bias_two,
    temporal_weight,
    bias_temporal,
    clip_ids,
):
    frames_here, height, width, channels = latent.shape
    value_rows = latent.astype(jnp.float32).reshape(
        frames_here, height * width, GROUPS, channels // GROUPS
    )
    part_sum = jnp.sum(value_rows, axis=(1, 3))
    part_squares = jnp.sum(value_rows * value_rows, axis=(1, 3))
    summed, summed_sq = lax.psum((part_sum, part_squares), "rows")
    cell_count = height * width * (channels // GROUPS) * lax.axis_size("rows")
    group_average = summed / cell_count
    variance = summed_sq / cell_count - group_average * group_average
    normed = (value_rows - group_average[:, None, :, None]) * lax.rsqrt(variance + GN_EPS)[
        :, None, :, None
    ]
    normed = normed.reshape(frames_here, height, width, channels) * norm_gain + norm_shift
    hidden = jax.nn.silu(normed).astype(jnp.bfloat16)
    padded = with_halo(hidden, (("rows", 1),), 1)
    first = (convolve_rows(padded, conv_one) + bias_one).astype(jnp.bfloat16)
    widened = with_halo(enlarge(first), (("rows", 1),), 1)
    second = (convolve_rows(widened, conv_two) + bias_two).astype(jnp.bfloat16)
    start_offsets = clip_starts(clip_ids)
    total_frames = clip_ids.shape[0]
    frame_positions = jnp.arange(total_frames, dtype=jnp.int32)
    source_frames = [
        jnp.maximum(frame_positions - tap_index * FRAME_DILATION, start_offsets)
        for tap_index in range(TEMPORAL_TAPS)
    ]
    gathered = lax.all_to_all(second, "frames", split_axis=2, concat_axis=0, tiled=True)
    activated = jax.nn.silu(gathered.astype(jnp.float32)).astype(jnp.bfloat16)
    branch = jnp.zeros(gathered.shape, jnp.float32)
    for tap_index in range(TEMPORAL_TAPS):
        chosen = jnp.take(activated, source_frames[tap_index], axis=0)
        branch = branch + jnp.einsum(
            "fnwc,cd->fnwd", chosen, temporal_weight[tap_index], preferred_element_type=jnp.float32
        )
    return (gathered.astype(jnp.float32) + bias_temporal + branch).astype(jnp.bfloat16)


def solution(mesh):
    in_specs = (P("frames", "rows", None, None), P(), P(), P(), P(), P(), P(), P(), P(), P())
    out_specs = P(None, "rows", "frames", None)
    return jax.shard_map(
        per_device, mesh=mesh, in_specs=in_specs, out_specs=out_specs, check_vma=False
    )
```

profile of v0, /device:TPU:1, one launch (start us, length us, event | category | flops | bytes accessed | tf_op | source)
XLA Modules:
  0.0 159.5 jit_solution(1795622648644085035)
XLA Ops:
  0.0 1.7 %convert_reduce_fusion = (f32[512]{0:T(512)S(1)}, f32[512]{0:T(512)S(1)}) fusion(bf16[1,8,128,512]{3,2,1,0:T(8,128)(2,1)} %param.12), kind=kLoop, calls=%fused_computation.24 | loop fusion | flops 2096128 | bytes 1052672 | tf_op jit(solution)/shard_map/reduce_sum | solution.py:64
  2.1 6.4 %all-reduce = (f32[1,32]{1,0:T(1,128)S(1)}, f32[1,32]{1,0:T(1,128)S(1)}) all-reduce(f32[1,32]{1,0:T(1,128)S(1)} %bitcast.88, f32[1,32]{1,0:T(1,128)S(1)} %bitcast.87), channel_id=1, replica_groups=mesh['frames'=8,'rows'=4] {'rows'}, use_global_device_ids=true, to_apply=%region_5.6 | all-reduce | flops 64 | bytes 512 | tf_op jit(solution)/shard_map/psum | solution.py:66
  8.8 2.0 %fusion.24 = bf16[1,8,128,512]{3,2,1,0:T(8,128)(2,1)S(1)} fusion(bf16[1,8,128,512]{3,2,1,0:T(8,128)(2,1)} %param.12, f32[512]{0:T(512)} %param.14, f32[512]{0:T(512)} %param.13, f32[512]{0:T(512)S(1)} %mul.51, f32[512]{0:T(512)S(1)} %sub.29), kind=kLoop, calls=%fused_computation.37 | loop fusion | flops 5242880 | bytes 2105344 | tf_op jit(solution)/shard_map/convert_element_type | solution.py:74
  10.8 3.9 %collective-permute-start = (bf16[1,1,128,512]{3,2,1,0:T(8,128)(2,1)S(1)}, bf16[1,1,128,512]{3,2,1,0:T(8,128)(2,1)S(1)}, u32[]{:S(2)}, u32[]{:S(2)}) collective-permute-start(bf16[1,1,128,512]{3,2,1,0:T(8,128)(2,1)S(1)} %get-tuple-element.16), channel_id=1, source_target_pairs={{0,1},{1,2},{2,3},{4,5},{5,6},{6,7},{8,9},{9,10},{10,11},{12,13},{... | collective-permute-start | bytes 393224 | tf_op jit(solution)/shard_map/ppermute | solution.py:21
  14.7 1.9 %collective-permute-start.1 = (bf16[1,1,128,512]{3,2,1,0:T(8,128)(2,1)S(1)}, bf16[1,1,128,512]{3,2,1,0:T(8,128)(2,1)S(1)}, u32[]{:S(2)}, u32[]{:S(2)}) collective-permute-start(bf16[1,1,128,512]{3,2,1,0:T(8,128)(2,1)S(1)} %get-tuple-element.17), channel_id=1, source_target_pairs={{1,0},{2,1},{3,2},{5,4},{6,5},{7,6},{9,8},{10,9},{11,10},{13,12},{... | collective-permute-start | bytes 393224 | tf_op jit(solution)/shard_map/ppermute | solution.py:22
  16.7 4.3 %collective-permute-done.1 = bf16[1,1,128,512]{3,2,1,0:T(8,128)(2,1)S(1)} collective-permute-done((bf16[1,1,128,512]{3,2,1,0:T(8,128)(2,1)S(1)}, bf16[1,1,128,512]{3,2,1,0:T(8,128)(2,1)S(1)}, u32[]{:S(2)}, u32[]{:S(2)}) %collective-permute-start.1) | collective-permute-done | bytes 131104 | tf_op jit(solution)/shard_map/ppermute | solution.py:22
  21.2 1.5 pad
  22.7 3.3 %reshape.68 = bf16[10,1,8,17,512]{4,3,2,0,1:T(8,128)(2,1)} reshape(bf16[10,1,136,512]{3,2,0,1:T(8,128)(2,1)} %pad) | data formatting | bytes 2785280 | tf_op jit(solution)/shard_map/conv_general_dilated | solution.py:28
  26.0 2.1 %copy.31 = bf16[10,1,8,17,512]{4,2,3,0,1:T(8,128)(2,1)S(1)} copy(bf16[10,1,8,17,512]{4,3,2,0,1:T(8,128)(2,1)} %reshape.68) | data formatting | bytes 2785280 | tf_op jit(solution)/shard_map/conv_general_dilated | solution.py:28
  28.1 7.3 %add_convert_fusion.1 = bf16[8,8,17,512]{3,1,2,0:T(8,128)(2,1)S(1)} fusion(bf16[3,3,512,512]{3,2,1,0:T(8,128)(2,1)} %param.15, bf16[10,1,7,2,512]{4,2,3,0,1:T(8,128)(2,1)S(1)} %slice.40, bf16[10,1,8,17,512]{4,2,3,0,1:T(8,128)(2,1)S(1)} %copy.31, f32[512]{0:T(512)S(1)} %copy-done.8, pred[8,17]{0,1:T(8,128)(4,1)S(1)} %copy-done.12), kind=kOutput, calls=%fused_computation.28 | convolution fusion | flops 5140168704 | bytes 7370888 | tf_op jit(solution)/shard_map/conv_general_dilated | solution.py:28
  36.3 3.5 %broadcast_in_dim.43 = bf16[16,128,2,512]{3,2,1,0:T(2,128)(2,1)} broadcast(bf16[16,128,512]{2,1,0:T(8,128)(2,1)S(1)} %bitcast.85), dimensions={0,1,3} | broadcast | bytes 6291456 | tf_op jit(solution)/shard_map/broadcast_in_dim | solution.py:45
  39.9 7.2 %broadcast_in_dim.44 = bf16[1,16,256,512]{3,2,1,0:T(8,128)(2,1)} reshape(bf16[16,128,2,512]{3,2,1,0:T(2,128)(2,1)} %broadcast_in_dim.43) | data formatting | bytes 8388608 | tf_op jit(solution)/shard_map/broadcast_in_dim | solution.py:45
  47.1 1.1 fusion.64
  48.2 1.9 %collective-permute-start.2 = (bf16[1,1,256,512]{3,2,1,0:T(8,128)(2,1)S(1)}, bf16[1,1,256,512]{3,2,1,0:T(8,128)(2,1)S(1)}, u32[]{:S(2)}, u32[]{:S(2)}) collective-permute-start(bf16[1,1,256,512]{3,2,1,0:T(8,128)(2,1)S(1)} %get-tuple-element.14), channel_id=1, source_target_pairs={{0,1},{1,2},{2,3},{4,5},{5,6},{6,7},{8,9},{9,10},{10,11},{12,13},{... | collective-permute-start | bytes 786440 | tf_op jit(solution)/shard_map/ppermute | solution.py:21
  50.1 2.6 %collective-permute-start.3 = (bf16[1,1,256,512]{3,2,1,0:T(8,128)(2,1)S(1)}, bf16[1,1,256,512]{3,2,1,0:T(8,128)(2,1)S(1)}, u32[]{:S(2)}, u32[]{:S(2)}) collective-permute-start(bf16[1,1,256,512]{3,2,1,0:T(8,128)(2,1)S(1)} %get-tuple-element.15), channel_id=1, source_target_pairs={{1,0},{2,1},{3,2},{5,4},{6,5},{7,6},{9,8},{10,9},{11,10},{13,12},{... | collective-permute-start | bytes 786440 | tf_op jit(solution)/shard_map/ppermute | solution.py:22
  53.4 4.4 %collective-permute-done.3 = bf16[1,1,256,512]{3,2,1,0:T(8,128)(2,1)S(1)} collective-permute-done((bf16[1,1,256,512]{3,2,1,0:T(8,128)(2,1)S(1)}, bf16[1,1,256,512]{3,2,1,0:T(8,128)(2,1)S(1)}, u32[]{:S(2)}, u32[]{:S(2)}) %collective-permute-start.3) | collective-permute-done | bytes 262176 | tf_op jit(solution)/shard_map/ppermute | solution.py:22
  57.8 2.5 %maximum_bitcast_fusion = bf16[18,1,256,512]{3,2,0,1:T(8,128)(2,1)S(1)} fusion(bf16[1,1,256,512]{3,2,1,0:T(8,128)(2,1)S(1)} %collective-permute-done.3, bf16[1,16,256,512]{3,2,1,0:T(8,128)(2,1)} %broadcast_in_dim.44, bf16[1,1,256,512]{3,2,1,0:T(8,128)(2,1)S(1)} %collective-permute-done.2), kind=kLoop, calls=%fused_computation.11 | loop fusion | flops 4718592 | bytes 9437184 | tf_op jit(solution)/shard_map/concatenate | solution.py:23
  60.3 4.7 %pad.2 = bf16[18,1,264,512]{3,2,0,1:T(8,128)(2,1)} pad(bf16[18,1,256,512]{3,2,0,1:T(8,128)(2,1)S(1)} %maximum_bitcast_fusion, bf16[]{:T(256)} %constant.34), padding=0_0x0_0x1_7x0_0 | pad | bytes 9584642 | tf_op jit(solution)/shard_map/concatenate | solution.py:23
  65.0 8.2 %reshape.75 = bf16[18,1,8,33,512]{4,3,2,0,1:T(8,128)(2,1)} reshape(bf16[18,1,264,512]{3,2,0,1:T(8,128)(2,1)} %pad.2) | data formatting | bytes 9732096 | tf_op jit(solution)/shard_map/conv_general_dilated | solution.py:28
  73.2 4.8 %copy.35 = bf16[18,1,8,33,512]{4,2,3,0,1:T(8,128)(2,1)S(1)} copy(bf16[18,1,8,33,512]{4,3,2,0,1:T(8,128)(2,1)} %reshape.75) | data formatting | bytes 9732096 | tf_op jit(solution)/shard_map/conv_general_dilated | solution.py:28
  78.1 11.1 %add_convert_fusion = bf16[16,8,33,256]{3,1,2,0:T(8,128)(2,1)S(1)} fusion(f32[256]{0:T(256)S(1)} %copy-done.9, pred[8,33]{0,1:T(8,128)(4,1)S(1)} %copy-done.11, bf16[3,3,512,256]{3,2,1,0:T(8,128)(2,1)S(1)} %copy-done, bf16[18,1,7,2,512]{4,2,3,0,1:T(8,128)(2,1)S(1)} %slice.44, bf16[18,1,8,33,512]{4,2,3,0,1:T(8,128)(2,1)S(1)} %copy.35), kind=kOutput, calls=%fused_computation.12 | convolution fusion | flops 9984393216 | bytes 9647368 | tf_op jit(solution)/shard_map/conv_general_dilated | solution.py:28
  89.7 1.5 slice_bitcast_fusion
  91.1 5.8 %all-to-all-start = ((bf16[1,16,256,256]{3,1,0,2:T(8,128)(2,1)}), bf16[1,16,256,256]{3,1,0,2:T(8,128)(2,1)S(1)}, u32[]{:S(2)}, u32[]{:S(2)}) async-start(bf16[1,16,256,256]{3,1,0,2:T(8,128)(2,1)} %slice_bitcast_fusion), calls=%async_computation | async-start | bytes 4194304 | tf_op jit(solution)/shard_map/all_to_all | solution.py:86
  97.1 45.8 %all-to-all-done = bf16[1,16,256,256]{3,1,0,2:T(8,128)(2,1)S(1)} async-done(((bf16[1,16,256,256]{3,1,0,2:T(8,128)(2,1)}), bf16[1,16,256,256]{3,1,0,2:T(8,128)(2,1)S(1)}, u32[]{:S(2)}, u32[]{:S(2)}) %all-to-all-start) | async-done | bytes 2097184 | tf_op jit(solution)/shard_map/all_to_all | solution.py:86
  143.7 1.3 copy-done.2
  145.0 1.3 fusion.13
  146.2 2.0 %gather_fusion.2 = bf16[8,16,32,256]{3,2,1,0:T(8,128)(2,1)} fusion(bf16[8,16,32,256]{3,2,1,0:T(8,128)(2,1)S(1)} %fusion.13, s32[1024]{0:T(1024)S(1)} %pad_clamp_fusion), kind=kCustom, calls=%fused_computation.2.clone | custom fusion | bytes 4194336 | tf_op jit(solution)/shard_map/jit(_take)/gather | solution.py:90
  148.2 2.0 %gather_fusion.1 = bf16[8,16,32,256]{3,2,1,0:T(8,128)(2,1)} fusion(bf16[8,16,32,256]{3,2,1,0:T(8,128)(2,1)S(1)} %fusion.13, s32[1024]{0:T(1024)S(1)} %pad_clamp_fusion.1), kind=kCustom, calls=%fused_computation.1.clone | custom fusion | bytes 4194336 | tf_op jit(solution)/shard_map/jit(_take)/gather | solution.py:90
  150.3 2.0 %gather_fusion = bf16[8,16,32,256]{3,2,1,0:T(8,128)(2,1)} fusion(bf16[8,16,32,256]{3,2,1,0:T(8,128)(2,1)S(1)} %fusion.13, s32[1024]{0:T(1024)S(1)} %pad_clamp_fusion.2), kind=kCustom, calls=%fused_computation.clone | custom fusion | bytes 4194336 | tf_op jit(solution)/shard_map/jit(_take)/gather | solution.py:90
  152.3 2.5 %fusion.29 = f32[8,16,32,256]{3,2,1,0:T(8,128)S(1)} fusion(bf16[8,16,32,256]{3,2,1,0:T(8,128)(2,1)} %gather_fusion, pred[8]{0:T(512)(128)(4,1)S(1)} %get-tuple-element.18, bf16[3,256,256]{2,1,0:T(8,128)(2,1)S(1)} %copy-done.6), kind=kOutput, calls=%fused_computation.43 | convolution fusion | flops 537919488 | bytes 6423040 | tf_op jit(solution)/shard_map/fnwc,cd->fnwd/dot_general | solution.py:91
  155.6 0.8 copy-done.3
  157.0 2.5 %fusion.9 = bf16[8,16,32,256]{3,2,1,0:T(8,128)(2,1)} fusion(f32[8,16,32,256]{3,2,1,0:T(8,128)S(1)} %fusion.29, f32[8,16,32,256]{3,2,1,0:T(8,128)S(1)} %fusion.27, bf16[8,16,32,256]{3,2,1,0:T(8,128)(2,1)S(1)} %copy-done.5, f32[256]{0:T(256)S(1)} %copy-done.7, pred[8]{0:T(512)(128)(4,1)S(1)} %get-tuple-element.10, bf16[3,256,256]{2,1,0:T(8,128)(2,1)S(1)} %copy-done.6, ...), kind=kOutput, calls=%fused_computation.17 | convolution fusion | flops 544210944 | bytes 14812672 | tf_op jit(solution)/shard_map/fnwc,cd->fnwd/dot_general | solution.py:91
  (52 shorter events, 5.4 us)
Async XLA Ops:
  0.0 78.1 %copy-start = (bf16[3,3,512,256]{3,2,1,0:T(8,128)(2,1)S(1)}, bf16[3,3,512,256]{3,2,1,0:T(8,128)(2,1)}, u32[]{:S(2)}) copy-start(bf16[3,3,512,256]{3,2,1,0:T(8,128)(2,1)} %param.17) | copy-start | bytes 7077892
  10.8 5.8 %collective-permute-start = (bf16[1,1,128,512]{3,2,1,0:T(8,128)(2,1)S(1)}, bf16[1,1,128,512]{3,2,1,0:T(8,128)(2,1)S(1)}, u32[]{:S(2)}, u32[]{:S(2)}) collective-permute-start(bf16[1,1,128,512]{3,2,1,0:T(8,128)(2,1)S(1)} %get-tuple-element.16), channel_id=1, source_target_pairs={{0,1},{1,2},{2,3},{4,5},{5,6},{6,7},{8,9},{9,10},{10,11},{12,13},{... | collective-permute-start | bytes 393224 | tf_op jit(solution)/shard_map/ppermute | solution.py:21
  14.7 6.3 %collective-permute-start.1 = (bf16[1,1,128,512]{3,2,1,0:T(8,128)(2,1)S(1)}, bf16[1,1,128,512]{3,2,1,0:T(8,128)(2,1)S(1)}, u32[]{:S(2)}, u32[]{:S(2)}) collective-permute-start(bf16[1,1,128,512]{3,2,1,0:T(8,128)(2,1)S(1)} %get-tuple-element.17), channel_id=1, source_target_pairs={{1,0},{2,1},{3,2},{5,4},{6,5},{7,6},{9,8},{10,9},{11,10},{13,12},{... | collective-permute-start | bytes 393224 | tf_op jit(solution)/shard_map/ppermute | solution.py:22
  26.0 2.1 %copy-start.8 = (f32[512]{0:T(512)S(1)}, f32[512]{0:T(512)}, u32[]{:S(2)}) copy-start(f32[512]{0:T(512)} %param.16) | copy-start | bytes 6148
  26.0 2.1 %copy-start.12 = (pred[8,17]{0,1:T(8,128)(4,1)S(1)}, pred[8,17]{0,1:T(8,128)(4,1)}, u32[]{:S(2)}) copy-start(pred[8,17]{0,1:T(8,128)(4,1)} %constant.43) | copy-start | bytes 412
  48.2 5.2 %collective-permute-start.2 = (bf16[1,1,256,512]{3,2,1,0:T(8,128)(2,1)S(1)}, bf16[1,1,256,512]{3,2,1,0:T(8,128)(2,1)S(1)}, u32[]{:S(2)}, u32[]{:S(2)}) collective-permute-start(bf16[1,1,256,512]{3,2,1,0:T(8,128)(2,1)S(1)} %get-tuple-element.14), channel_id=1, source_target_pairs={{0,1},{1,2},{2,3},{4,5},{5,6},{6,7},{8,9},{9,10},{10,11},{12,13},{... | collective-permute-start | bytes 786440 | tf_op jit(solution)/shard_map/ppermute | solution.py:21
  50.1 7.7 %collective-permute-start.3 = (bf16[1,1,256,512]{3,2,1,0:T(8,128)(2,1)S(1)}, bf16[1,1,256,512]{3,2,1,0:T(8,128)(2,1)S(1)}, u32[]{:S(2)}, u32[]{:S(2)}) collective-permute-start(bf16[1,1,256,512]{3,2,1,0:T(8,128)(2,1)S(1)} %get-tuple-element.15), channel_id=1, source_target_pairs={{1,0},{2,1},{3,2},{5,4},{6,5},{7,6},{9,8},{10,9},{11,10},{13,12},{... | collective-permute-start | bytes 786440 | tf_op jit(solution)/shard_map/ppermute | solution.py:22
  73.2 4.9 %copy-start.9 = (f32[256]{0:T(256)S(1)}, f32[256]{0:T(256)}, u32[]{:S(2)}) copy-start(f32[256]{0:T(256)} %param.18) | copy-start | bytes 3076
  73.2 4.9 %copy-start.11 = (pred[8,33]{0,1:T(8,128)(4,1)S(1)}, pred[8,33]{0,1:T(8,128)(4,1)}, u32[]{:S(2)}) copy-start(pred[8,33]{0,1:T(8,128)(4,1)} %constant.42) | copy-start | bytes 796
  91.1 5.8 %copy-start.10 = (s32[8]{0:T(128)S(1)}, s32[8]{0:T(128)}, u32[]{:S(2)}) copy-start(s32[8]{0:T(128)} %param.21) | copy-start | bytes 100
  91.1 51.8 %all-to-all-start = ((bf16[1,16,256,256]{3,1,0,2:T(8,128)(2,1)}), bf16[1,16,256,256]{3,1,0,2:T(8,128)(2,1)S(1)}, u32[]{:S(2)}, u32[]{:S(2)}) async-start(bf16[1,16,256,256]{3,1,0,2:T(8,128)(2,1)} %slice_bitcast_fusion), calls=%async_computation | async-start | bytes 4194304 | tf_op jit(solution)/shard_map/all_to_all | solution.py:86
  143.7 1.3 copy-start.2
  150.3 2.0 %copy-start.6 = (bf16[3,256,256]{2,1,0:T(8,128)(2,1)S(1)}, bf16[3,256,256]{2,1,0:T(8,128)(2,1)}, u32[]{:S(2)}) copy-start(bf16[3,256,256]{2,1,0:T(8,128)(2,1)} %param.19) | copy-start | bytes 1179652
  152.3 2.5 %copy-start.4 = (bf16[8,16,32,256]{3,2,1,0:T(8,128)(2,1)S(1)}, bf16[8,16,32,256]{3,2,1,0:T(8,128)(2,1)}, u32[]{:S(2)}) copy-start(bf16[8,16,32,256]{3,2,1,0:T(8,128)(2,1)} %gather_fusion.1) | copy-start | bytes 6291460
  154.8 1.6 copy-start.3
  154.8 2.2 %copy-start.5 = (bf16[8,16,32,256]{3,2,1,0:T(8,128)(2,1)S(1)}, bf16[8,16,32,256]{3,2,1,0:T(8,128)(2,1)}, u32[]{:S(2)}) copy-start(bf16[8,16,32,256]{3,2,1,0:T(8,128)(2,1)} %gather_fusion.2) | copy-start | bytes 6291460
  154.8 2.2 %copy-start.7 = (f32[256]{0:T(256)S(1)}, f32[256]{0:T(256)}, u32[]{:S(2)}) copy-start(f32[256]{0:T(256)} %param.20) | copy-start | bytes 3076
  157.0 2.5 %copy-start.1 = (bf16[3,3,512,256]{3,2,1,0:T(8,128)(2,1)S(1)}, bf16[3,3,512,256]{3,2,1,0:T(8,128)(2,1)}, u32[]{:S(2)}) copy-start(bf16[3,3,512,256]{3,2,1,0:T(8,128)(2,1)} %param.17) | copy-start | bytes 7077892
where the time goes:
time: 160 us
  waiting for transfers between devices  55.2 us (34%)
  local copies, waits for them, and re-layouts  49.3 us (31%)
  matrix products  24.1 us (15%)
  starting transfers between devices  16.1 us (10%)
  other arithmetic  8.1 us (5%)
  blocking collectives  6.42 us (4%)
    all_to_all x1, waiting for transfers between devices, per_device(): lax.all_to_all(second, 'frames', split_axis=2, concat_axis=0, tiled=True)  45.8 us
    conv_general_dilated x6, local copies, waits for them, and re-layouts, convolve_rows(): lax.conv_general_dilated(padded, weights, (1, 1), ((0, 0), (1, 1)), dimen...  18.5 us
    conv_general_dilated x2, matrix products, convolve_rows(): lax.conv_general_dilated(padded, weights, (1, 1), ((0, 0), (1, 1)), dimen...  18.4 us
    broadcast_in_dim x3, local copies, waits for them, and re-layouts, enlarge(): return jnp.repeat(jnp.repeat(features, 2, axis=1), 2, axis=2)  11 us
    ppermute x2, waiting for transfers between devices, with_halo(): after = lax.ppermute(leading, axis, down)  8.74 us
    psum x1, blocking collectives, per_device(): summed, summed_sq = lax.psum((part_sum, part_squares), 'rows')  6.42 us
    concatenate x2, local copies, waits for them, and re-layouts, with_halo(): value = jnp.concatenate([before, value, after], axis=dim)  6.11 us
    gather x3, local copies, waits for them, and re-layouts, per_device(): chosen = jnp.take(activated, source_frames[tap_index], axis=0)  6.03 us
  transfers between devices with their start and end apart: 5, of which 4 were waited for; matrix products, arithmetic and copies ran while one was open for 0% of the time, Pallas kernels for 0%

commit v1 on v0

v1 whole, which is shorter than its diff:
```python
import functools

import jax
import jax.numpy as jnp
from jax import lax
from jax.experimental import pallas as pl
from jax.experimental.pallas import tpu as pltpu
from jax.sharding import PartitionSpec as P

GROUPS = 32
TAPS = 3
DILATION = 2
GN_EPS = 1e-06
BF16, F32 = jnp.bfloat16, jnp.float32


class Plan:
    def __init__(self, frames, rows, cols, c1, c2):
        self.F, self.R, self.C, self.c1, self.c2 = frames, rows, cols, c1, c2
        self.CH = cols + 4
        self.G = max(1, 16 // frames)
        self.S = self.G * frames
        self.halo = -(-2 * self.CH // 16) * 16
        self.q = max(1, 16 // (2 * cols))
        self.cells = 2 * rows * 2 * cols


def silu(v):
    return v / (1.0 + jnp.exp(-v))


def dot(a, b):
    return jnp.dot(a, b, preferred_element_type=F32)


def stage_kernel(
    p, src, edge, recv, top, bot, w1_hbm, w2_hbm, wt, b1, b2, bt, pin, pout, out,
    cells, even, odd, feven, fodd, phase, second, act, w1, w2, sems,
):
    F, R, C, CH, G, S, c1, c2 = p.F, p.R, p.C, p.CH, p.G, p.S, p.c1, p.c2
    copy1 = pltpu.make_async_copy(w1_hbm, w1, sems.at[0])
    copy2 = pltpu.make_async_copy(w2_hbm, w2, sems.at[1])
    copy1.start()
    copy2.start()

    def turn(ref, first, count, at):
        for j in range(count // 16):
            block = jnp.concatenate([ref[f, 16 * j : 16 * j + 16, :] for f in range(F)], axis=0)
            turned = dot(pin[...], block).reshape(16, F, c1)
            lo = max(first - 16 * j, 0)
            cells[at + 16 * j + lo - first : at + 16 * j + 16 - first] = turned[lo:]

    skip = p.halo - 2 * CH
    turn(bot, 0, p.halo, (R + 2) * CH)
    turn(recv, 0, R * CH, 2 * CH)
    turn(top, skip, p.halo, 0)

    def split(r, carry):
        row = cells[pl.ds(r * CH, CH)]
        even[r] = row.reshape(CH // G, S, c1).astype(BF16)
        if G == 2:
            odd[r] = row[1 : CH - 1].reshape(CH // G - 1, S, c1).astype(BF16)
        return carry

    lax.fori_loop(0, R + 4, split, 0)

    def piece(e, o, r, nr, dc, n):
        if G == 1:
            v = e[pl.ds(r, nr), dc : dc + n]
        elif dc == 1:
            v = o[pl.ds(r, nr), 0:n]
        else:
            v = e[pl.ds(r, nr), dc // 2 : dc // 2 + n]
        return v.reshape(nr * n * S, v.shape[-1])

    n1 = (C + 2) // G
    nr1 = 2
    copy1.wait()
    left = edge[2]
    right = edge[3]

    def conv_one(i, carry):
        r = i * nr1
        acc = None
        for dr in range(3):
            for dc in range(3):
                t = dot(piece(even, odd, r + dr, nr1, dc, n1), w1[dr * 3 + dc])
                acc = t if acc is None else acc + t
        v = (acc + b1[...]).reshape(nr1, C + 2, F, c1)
        for k in range(nr1):
            row_in = jnp.logical_and(r + k >= edge[0], r + k < edge[1])
            col = lax.broadcasted_iota(jnp.int32, (C + 2, F, c1), 0)
            keep = jnp.logical_and(jnp.logical_and(col >= left, col < right), row_in)
            row = jnp.where(keep, v[k], 0.0)
            feven[r + k] = row.reshape(n1, S, c1).astype(BF16)
            if G == 2:
                fodd[r + k] = row[1 : C + 1].reshape(n1 - 1, S, c1).astype(BF16)
        return carry

    lax.fori_loop(0, (R + 2) // nr1, conv_one, 0)

    n2 = C // G
    nr2 = min(R, 4)
    copy2.wait()

    def conv_two(i, carry):
        r = i * nr2
        for a in range(2):
            for b in range(2):
                acc = None
                for da in range(2):
                    for db in range(2):
                        lhs = piece(feven, fodd, r + a + da, nr2, b + db, n2)
                        t = dot(lhs, w2[((a * 2 + b) * 2 + da) * 2 + db])
                        acc = t if acc is None else acc + t
                phase[a, b, pl.ds(r, nr2)] = (acc + b2[...]).astype(BF16).reshape(nr2, C * F, c2)
        return carry

    lax.fori_loop(0, R // nr2, conv_two, 0)

    for blk in range(2 * R // p.q):
        rows = range(blk * p.q, blk * p.q + p.q)
        x = jnp.concatenate([phase[o % 2, b, o // 2] for o in rows for b in range(2)], axis=0)
        turned = dot(pout[...], x)
        at = blk * p.q * 2 * C
        n = p.q * 2 * C
        second[:, at : at + n, :] = turned.astype(BF16).reshape(F, n, c2)
        act[:, at : at + n, :] = silu(turned).astype(BF16).reshape(F, n, c2)

    def temporal(t, carry):
        lhs = jnp.concatenate([act[src[k, t]] for k in range(TAPS)], axis=-1)
        out[t] = (dot(lhs, wt[...]) + second[t].astype(F32) + bt[...]).astype(BF16)
        return carry

    lax.fori_loop(0, F, temporal, 0)


def fused(p, src, edge, recv, top, bot, w1, w2, wt, b1, b2, bt):
    F, R, C, CH, G, S, c1, c2 = p.F, p.R, p.C, p.CH, p.G, p.S, p.c1, p.c2
    ri = jnp.arange(16 * F)
    pin = ((ri[:, None] // F == ri[None, :] % 16) & (ri[:, None] % F == ri[None, :] // 16)).astype(BF16)
    q = p.q
    ro = jnp.arange(q * 2 * C * F)
    of, orow, oc = ro // (q * 2 * C), ro // (2 * C) % q, ro % (2 * C)
    irow, ib, ic, if_ = ro // (2 * C * F), ro // (C * F) % 2, ro // F % C, ro % F
    pout = (
        (of[:, None] == if_[None, :]) & (orow[:, None] == irow[None, :])
        & (oc[:, None] == (2 * ic + ib)[None, :])
    ).astype(BF16)
    vm = pl.BlockSpec(memory_space=pltpu.VMEM)
    sm = pl.BlockSpec(memory_space=pltpu.SMEM)
    hbm = pl.BlockSpec(memory_space=pl.ANY)
    odd_rows = 1 if G == 1 else R + 4
    fodd_rows = 1 if G == 1 else R + 2
    return pl.pallas_call(
        functools.partial(stage_kernel, p),
        out_shape=jax.ShapeDtypeStruct((F, p.cells, c2), BF16),
        in_specs=[sm, sm, vm, vm, vm, hbm, hbm, vm, vm, vm, vm, vm, vm],
        out_specs=vm,
        scratch_shapes=[
            pltpu.VMEM(((R + 4) * CH + p.halo, F, c1), F32),
            pltpu.VMEM((R + 4, CH // G, S, c1), BF16),
            pltpu.VMEM((odd_rows, CH // G - 1, S, c1), BF16),
            pltpu.VMEM((R + 2, (C + 2) // G, S, c1), BF16),
            pltpu.VMEM((fodd_rows, max(1, (C + 2) // G - 1), S, c1), BF16),
            pltpu.VMEM((2, 2, R, C * F, c2), BF16),
            pltpu.VMEM((F, p.cells, c2), BF16),
            pltpu.VMEM((F, p.cells, c2), BF16),
            pltpu.VMEM(w1.shape, BF16),
            pltpu.VMEM(w2.shape, BF16),
            pltpu.SemaphoreType.DMA((2,)),
        ],
        compiler_params=pltpu.CompilerParams(vmem_limit_bytes=60 * 2**20),
    )(src, edge, recv, top, bot, w1, w2, wt, b1, b2, bt, pin, pout)


def clip_starts(clip_ids):
    frame_positions = jnp.arange(clip_ids.shape[0], dtype=jnp.int32)
    same_clip = clip_ids[:, None] == clip_ids[None, :]
    return jnp.min(jnp.where(same_clip, frame_positions[None, :], clip_ids.shape[0]), axis=1)


def phase_weights(conv_two):
    w = conv_two.astype(F32)
    rows = [[w[0], w[1] + w[2]], [w[0] + w[1], w[2]]]
    out = []
    for a in range(2):
        for b in range(2):
            for da in range(2):
                u = rows[a][da]
                pair = [u[0], u[1] + u[2]] if b == 0 else [u[0] + u[1], u[2]]
                out += pair
    return jnp.stack(out).astype(BF16)


def per_device(
    latent, norm_gain, norm_shift, conv_one, bias_one, conv_two, bias_two,
    temporal_weight, bias_temporal, clip_ids,
):
    frames_here, height, width, channels = latent.shape
    c2 = conv_two.shape[-1]
    peers, row_peers = lax.axis_size("frames"), lax.axis_size("rows")
    total_frames = clip_ids.shape[0]
    p = Plan(total_frames, height, width // peers, channels, c2)
    x = latent.astype(F32)
    sums = jnp.sum(x, axis=(1, 2)).reshape(frames_here, GROUPS, -1).sum(-1)
    squares = jnp.sum(x * x, axis=(1, 2)).reshape(frames_here, GROUPS, -1).sum(-1)
    sums, squares = lax.psum((sums, squares), "rows")
    count = height * width * (channels // GROUPS) * row_peers
    mean = sums / count
    inv = lax.rsqrt(squares / count - mean * mean + GN_EPS)
    mean = jnp.repeat(mean, channels // GROUPS, axis=1)[:, None, None, :]
    inv = jnp.repeat(inv, channels // GROUPS, axis=1)[:, None, None, :]
    hidden = jax.nn.silu((x - mean) * inv * norm_gain + norm_shift).astype(BF16)
    padded = jnp.pad(hidden, ((0, 0), (0, 0), (2, 2), (0, 0)))
    send = jnp.stack([padded[:, :, d * p.C : d * p.C + p.CH] for d in range(peers)])
    send = send.reshape(peers * frames_here, height * p.CH, channels)
    recv = lax.all_to_all(send, "frames", split_axis=0, concat_axis=0, tiled=True)
    n = height * p.CH
    top = lax.ppermute(recv[:, n - p.halo :], "rows", [(i, i + 1) for i in range(row_peers - 1)])
    bot = lax.ppermute(recv[:, : p.halo], "rows", [(i + 1, i) for i in range(row_peers - 1)])
    start = clip_starts(clip_ids)
    at = jnp.arange(total_frames, dtype=jnp.int32)
    src = jnp.stack([jnp.maximum(at - k * DILATION, start) for k in range(TAPS)])
    d, r = lax.axis_index("frames"), lax.axis_index("rows")
    edge = jnp.stack([
        jnp.where(r == 0, 1, 0), jnp.where(r == row_peers - 1, height + 1, height + 2),
        jnp.where(d == 0, 1, 0), jnp.where(d == peers - 1, p.C + 1, p.C + 2),
    ]).astype(jnp.int32)
    out = fused(
        p, src, edge, recv, top, bot, conv_one.reshape(9, channels, channels),
        phase_weights(conv_two), temporal_weight.reshape(TAPS * c2, c2),
        bias_one[None], bias_two[None], bias_temporal[None],
    )
    return out.reshape(total_frames, 2 * height, 2 * p.C, c2)


def solution(mesh):
    in_specs = (P("frames", "rows", None, None), P(), P(), P(), P(), P(), P(), P(), P(), P())
    out_specs = P(None, "rows", "frames", None)
    return jax.shard_map(
        per_device, mesh=mesh, in_specs=in_specs, out_specs=out_specs, check_vma=False
    )
```

time: 160 us -> 91.8 us (0.57)
  waiting for transfers between devices: 55.2 us -> 16.1 us
  local copies, waits for them, and re-layouts: 49.3 us -> 16.8 us
  matrix products: 24.1 us -> 0 us
  Pallas kernels: 0 us -> 22.1 us
  other arithmetic: 8.1 us -> 16.3 us
  starting transfers between devices: 16.1 us -> 13.5 us
    all_to_all x1, waiting for transfers between devices: 45.8 us -> 11.8 us  [per_device(): lax.all_to_all(send, 'frames', split_axis=0, concat_axis=0, tiled=True)]
    pallas_call x0 -> x1, Pallas kernels: none -> 22.1 us  [fused(): pl.pallas_call(functools.partial(stage_kernel, p), out_shape=jax.ShapeDty...]
    conv_general_dilated x6 -> x0, local copies, waits for them, and re-layouts: 18.5 us -> none  [convolve_rows(): lax.conv_general_dilated(padded, weights, (1, 1), ((0, 0), (1, 1)), dimen...]
    conv_general_dilated x2 -> x0, matrix products: 18.4 us -> none  [convolve_rows(): lax.conv_general_dilated(padded, weights, (1, 1), ((0, 0), (1, 1)), dimen...]
    broadcast_in_dim x3 -> x4, local copies, waits for them, and re-layouts: 11 us -> 0.3 us  [the longest x2 0.15 us: per_device(): mean = jnp.repeat(mean, channels // GROUPS, axis=1)[:, None, None, :]]
    unnamed x26 -> x24, local copies, waits for them, and re-layouts: 2.78 us -> 11.8 us
    unnamed x0 -> x8, other arithmetic: none -> 8.88 us
    concatenate x2 -> x0, local copies, waits for them, and re-layouts: 6.11 us -> none  [with_halo(): value = jnp.concatenate([before, value, after], axis=dim)]
  transfers between devices with their start and end apart: 5 -> 3, of which waited for: 4 -> 2; matrix products, arithmetic and copies ran while one was open for 0% -> 22% of each run, Pallas kernels for 0% -> 0%
where the time goes in v1:
time: 91.8 us; the launch traced here: 91.4 us
  Pallas kernels  22.1 us (24%)
  local copies, waits for them, and re-layouts  16.8 us (18%)
  other arithmetic  16.3 us (18%)
  waiting for transfers between devices  16.1 us (18%)
  starting transfers between devices  13.5 us (15%)
  blocking collectives  6.42 us (7%)
    pallas_call x1, Pallas kernels, fused(): pl.pallas_call(functools.partial(stage_kernel, p), out_shape=jax.ShapeDty...  22.1 us
    all_to_all x1, waiting for transfers between devices, per_device(): lax.all_to_all(send, 'frames', split_axis=0, concat_axis=0, tiled=True)  11.8 us
    unnamed x24, local copies, waits for them, and re-layouts  11.8 us
    unnamed x8, other arithmetic  8.88 us
    psum x1, blocking collectives, per_device(): sums, squares = lax.psum((sums, squares), 'rows')  6.42 us
    ppermute x1, starting transfers between devices, per_device(): lax.ppermute(recv[:, n - p.halo:], 'rows', [(i, i + 1) for i in range(row...  5.98 us
    all_to_all x1, starting transfers between devices, per_device(): lax.all_to_all(send, 'frames', split_axis=0, concat_axis=0, tiled=True)  5.63 us
    ppermute x1, waiting for transfers between devices, per_device(): lax.ppermute(recv[:, :p.halo], 'rows', [(i + 1, i) for i in range(row_pee...  4.23 us
  transfers between devices with their start and end apart: 3, of which 2 were waited for; matrix products, arithmetic and copies ran while one was open for 22% of the time, Pallas kernels for 0%

profile of v1, /device:TPU:1, one launch (start us, length us, event | category | flops | bytes accessed | tf_op | source)
XLA Modules:
  0.0 91.4 jit_solution(17877037656313638225)
XLA Ops:
  0.0 1.6 %convert_reduce_fusion = (f32[512]{0:T(512)S(1)}, f32[512]{0:T(512)S(1)}) fusion(bf16[1,8,128,512]{3,2,1,0:T(8,128)(2,1)} %param.10), kind=kLoop, calls=%fused_computation.2 | loop fusion | flops 2096128 | bytes 1052672 | tf_op jit(solution)/shard_map/reduce_sum | solution.py:206
  2.0 6.4 %all-reduce.1 = (f32[1,32]{1,0:T(1,128)S(1)}, f32[1,32]{1,0:T(1,128)S(1)}) all-reduce(f32[1,32]{1,0:T(1,128)S(1)} %bitcast.90, f32[1,32]{1,0:T(1,128)S(1)} %bitcast.89), channel_id=1, replica_groups=mesh['frames'=8,'rows'=4] {'rows'}, use_global_device_ids=true, to_apply=%region_6.7 | all-reduce | flops 64 | bytes 512 | tf_op jit(solution)/shard_map/psum | solution.py:208
  8.7 2.0 %fusion.8 = bf16[1,8,128,512]{3,2,1,0:T(8,128)(2,1)S(1)} fusion(bf16[1,8,128,512]{3,2,1,0:T(8,128)(2,1)} %param.10, f32[512]{0:T(512)} %param.12, f32[512]{0:T(512)} %param.11, f32[512]{0:T(512)S(1)} %broadcast_in_dim.51, f32[512]{0:T(512)S(1)} %broadcast_in_dim.49), kind=kLoop, calls=%fused_computation.11 | loop fusion | flops 5242880 | bytes 2105344 | tf_op jit(solution)/shard_map/convert_element_type | solution.py:214
  11.4 0.7 constant_dynamic-update-slice_fusion.7
  12.4 0.7 constant_dynamic-update-slice_fusion.6
  13.1 0.7 constant_dynamic-update-slice_fusion.5
  17.1 5.6 %all-to-all-start = ((bf16[8,160,512]{2,1,0:T(8,128)(2,1)}), bf16[8,160,512]{2,1,0:T(8,128)(2,1)}, u32[]{:S(2)}, u32[]{:S(2)}) async-start(bf16[8,160,512]{2,1,0:T(8,128)(2,1)} %constant_dynamic-update-slice_fusion), calls=%async_computation | async-start | bytes 2621440 | tf_op jit(solution)/shard_map/all_to_all | solution.py:218
  23.2 0.8 fusion.11
  24.4 1.1 %fusion.27 = bf16[16,512,256]{2,1,0:T(8,128)(2,1)} fusion(bf16[16,512,256]{2,1,0:T(8,128)(2,1)} %fusion.11, f32[3,3,512,256]{3,2,1,0:T(8,128)S(1)} %convert_element_type.20), kind=kLoop, calls=%fused_computation.50 | loop fusion | flops 262144 | bytes 1310720
  25.5 0.7 fusion.15
  26.2 0.8 fusion.29
  27.0 0.8 fusion.31
  27.8 0.7 fusion.13
  28.7 0.7 and_convert_fusion.1.pin
  29.4 0.8 and_convert_fusion.pout
  30.2 0.8 fusion.33
  31.0 0.7 fusion.17
  31.7 0.7 fusion.19
  32.5 0.8 fusion.35
  33.3 1.8 %fusion.23 = bf16[16,512,256]{2,1,0:T(8,128)(2,1)} fusion(bf16[16,512,256]{2,1,0:T(8,128)(2,1)} %fusion.35, f32[3,3,512,256]{3,2,1,0:T(8,128)} %copy-done), kind=kLoop, calls=%fused_computation.46 | loop fusion | bytes 524288
  35.0 1.9 %fusion.37 = bf16[16,512,256]{2,1,0:T(8,128)(2,1)} fusion(bf16[16,512,256]{2,1,0:T(8,128)(2,1)} %fusion.23, f32[3,3,512,256]{3,2,1,0:T(8,128)} %copy-done), kind=kLoop, calls=%fused_computation.60 | loop fusion | flops 262144 | bytes 1310720
  37.0 0.8 fusion.39
  37.7 0.8 fusion.21
  38.5 2.0 %fusion.41 = bf16[16,512,256]{2,1,0:T(8,128)(2,1)} fusion(bf16[16,512,256]{2,1,0:T(8,128)(2,1)} %fusion.21, f32[3,3,512,256]{3,2,1,0:T(8,128)} %copy-done), kind=kLoop, calls=%fused_computation.64 | loop fusion | flops 262144 | bytes 1310720
  40.5 11.8 %all-to-all-done.recv = bf16[8,160,512]{2,1,0:T(8,128)(2,1)} async-done(((bf16[8,160,512]{2,1,0:T(8,128)(2,1)}), bf16[8,160,512]{2,1,0:T(8,128)(2,1)}, u32[]{:S(2)}, u32[]{:S(2)}) %all-to-all-start) | async-done | bytes 1310752 | tf_op jit(solution)/shard_map/all_to_all | solution.py:218
  52.3 1.2 %fusion.51 = (bf16[8,48,512]{2,1,0:T(8,128)(2,1)S(1)}, bf16[8,48,512]{2,1,0:T(8,128)(2,1)S(1)}) fusion(bf16[8,160,512]{2,1,0:T(8,128)(2,1)} %all-to-all-done.recv), kind=kLoop, calls=%fused_computation.121 | loop fusion | bytes 1572864 | tf_op jit(solution)/shard_map/slice | solution.py:221
  53.5 6.0 %collective-permute-start = (bf16[8,48,512]{2,1,0:T(8,128)(2,1)S(1)}, bf16[8,48,512]{2,1,0:T(8,128)(2,1)S(1)}, u32[]{:S(2)}, u32[]{:S(2)}) collective-permute-start(bf16[8,48,512]{2,1,0:T(8,128)(2,1)S(1)} %get-tuple-element.12), channel_id=1, source_target_pairs={{0,1},{1,2},{2,3},{4,5},{5,6},{6,7},{8,9},{9,10},{10,11},{12,13},{... | collective-permute-start | bytes 1179656 | tf_op jit(solution)/shard_map/ppermute | solution.py:220
  59.5 1.9 %collective-permute-start.1 = (bf16[8,48,512]{2,1,0:T(8,128)(2,1)S(1)}, bf16[8,48,512]{2,1,0:T(8,128)(2,1)S(1)}, u32[]{:S(2)}, u32[]{:S(2)}) collective-permute-start(bf16[8,48,512]{2,1,0:T(8,128)(2,1)S(1)} %get-tuple-element.11), channel_id=1, source_target_pairs={{1,0},{2,1},{3,2},{5,4},{6,5},{7,6},{9,8},{10,9},{11,10},{13,12},{... | collective-permute-start | bytes 1179656 | tf_op jit(solution)/shard_map/ppermute | solution.py:221
  62.5 1.8 %fusion.25.w2_hbm = bf16[16,512,256]{2,1,0:T(8,128)(2,1)} fusion(bf16[16,512,256]{2,1,0:T(8,128)(2,1)} %fusion.41, f32[3,3,512,256]{3,2,1,0:T(8,128)} %copy-done), kind=kLoop, calls=%fused_computation.48 | loop fusion | bytes 524288 | tf_op jit(solution)/shard_map/stack | solution.py:193
  64.3 4.2 %collective-permute-done.1.bot = bf16[8,48,512]{2,1,0:T(8,128)(2,1)S(1)} collective-permute-done((bf16[8,48,512]{2,1,0:T(8,128)(2,1)S(1)}, bf16[8,48,512]{2,1,0:T(8,128)(2,1)S(1)}, u32[]{:S(2)}, u32[]{:S(2)}) %collective-permute-start.1) | collective-permute-done | bytes 393248 | tf_op jit(solution)/shard_map/ppermute | solution.py:221
  68.6 0.7 copy-done.3
  69.3 22.1 %shard_map.100 = bf16[8,512,256]{2,1,0:T(8,128)(2,1)} custom-call(s32[3,8]{1,0:T(4,128)} %pad_add_fusion.src, s32[4]{0:T(128)} %pad_add_fusion.1.edge, bf16[8,160,512]{2,1,0:T(8,128)(2,1)} %all-to-all-done.recv, bf16[8,48,512]{2,1,0:T(8,128)(2,1)} %copy-done.2, bf16[8,48,512]{2,1,0:T(8,128)(2,1)} %copy-done.3, bf16[9,512,512]{2,1,0:T(8,128)(2,1)} %bitcast.84, ...), custom_call_target="tpu_custom_call" | custom-call | tf_op jit(solution)/shard_map/pallas_call | solution.py:155
  (44 shorter events, 7.2 us)
Async XLA Ops:
  13.7 9.0 %copy-start.1 = (bf16[3,3,512,256]{3,2,1,0:T(8,128)(2,1)S(1)}, bf16[3,3,512,256]{3,2,1,0:T(8,128)(2,1)}, u32[]{:S(2)}) copy-start(bf16[3,3,512,256]{3,2,1,0:T(8,128)(2,1)} %param.15) | copy-start | bytes 7077892
  17.1 35.2 %all-to-all-start = ((bf16[8,160,512]{2,1,0:T(8,128)(2,1)}), bf16[8,160,512]{2,1,0:T(8,128)(2,1)}, u32[]{:S(2)}, u32[]{:S(2)}) async-start(bf16[8,160,512]{2,1,0:T(8,128)(2,1)} %constant_dynamic-update-slice_fusion), calls=%async_computation | async-start | bytes 2621440 | tf_op jit(solution)/shard_map/all_to_all | solution.py:218
  23.2 4.6 %copy-start = (f32[3,3,512,256]{3,2,1,0:T(8,128)}, f32[3,3,512,256]{3,2,1,0:T(8,128)S(1)}, u32[]{:S(2)}) copy-start(f32[3,3,512,256]{3,2,1,0:T(8,128)S(1)} %convert_element_type.20) | copy-start | bytes 14155780
  25.5 3.0 %copy-start.4 = (s32[8]{0:T(128)S(1)}, s32[8]{0:T(128)}, u32[]{:S(2)}) copy-start(s32[8]{0:T(128)} %param.19) | copy-start | bytes 100
  53.5 10.9 %collective-permute-start = (bf16[8,48,512]{2,1,0:T(8,128)(2,1)S(1)}, bf16[8,48,512]{2,1,0:T(8,128)(2,1)S(1)}, u32[]{:S(2)}, u32[]{:S(2)}) collective-permute-start(bf16[8,48,512]{2,1,0:T(8,128)(2,1)S(1)} %get-tuple-element.12), channel_id=1, source_target_pairs={{0,1},{1,2},{2,3},{4,5},{5,6},{6,7},{8,9},{9,10},{10,11},{12,13},{... | collective-permute-start | bytes 1179656 | tf_op jit(solution)/shard_map/ppermute | solution.py:220
  59.5 9.1 %collective-permute-start.1 = (bf16[8,48,512]{2,1,0:T(8,128)(2,1)S(1)}, bf16[8,48,512]{2,1,0:T(8,128)(2,1)S(1)}, u32[]{:S(2)}, u32[]{:S(2)}) collective-permute-start(bf16[8,48,512]{2,1,0:T(8,128)(2,1)S(1)} %get-tuple-element.11), channel_id=1, source_target_pairs={{1,0},{2,1},{3,2},{5,4},{6,5},{7,6},{9,8},{10,9},{11,10},{13,12},{... | collective-permute-start | bytes 1179656 | tf_op jit(solution)/shard_map/ppermute | solution.py:221
  64.3 4.2 %copy-start.2 = (bf16[8,48,512]{2,1,0:T(8,128)(2,1)}, bf16[8,48,512]{2,1,0:T(8,128)(2,1)S(1)}, u32[]{:S(2)}) copy-start(bf16[8,48,512]{2,1,0:T(8,128)(2,1)S(1)} %collective-permute-done.top) | copy-start | bytes 1179652
  68.6 0.7 copy-start.3

commit v2 on v1

v2 whole, which is shorter than its diff:
```python
import functools

import jax
import jax.numpy as jnp
from jax import lax
from jax.experimental import pallas as pl
from jax.experimental.pallas import tpu as pltpu
from jax.sharding import PartitionSpec as P

GROUPS = 32
TAPS = 3
DILATION = 2
GN_EPS = 1e-06
BF16, F32 = jnp.bfloat16, jnp.float32


def up_to(n, m):
    return -(-n // m) * m


class Plan:
    def __init__(self, frames, rows, cols, width, c1, c2, row_peers):
        self.F, self.R, self.C, self.W, self.c1, self.c2 = frames, rows, cols, width, c1, c2
        self.row_peers = row_peers
        self.peers = width // cols
        self.CH = cols + 4
        self.G = max(1, 16 // frames)
        self.S = self.G * frames
        self.T = up_to(2 * self.CH, 8)
        self.NA = 2 * self.T + 8
        self.NB = up_to((rows - 4) * self.CH, 16)
        self.q = max(1, 16 // (2 * cols))
        self.cells = 2 * rows * 2 * cols
        self.swap = self.peers <= 8 and cols % 16 == 0


def silu(v):
    h = 0.5 * v
    return h + h * jnp.tanh(h)


def dot(a, b, **kw):
    return jnp.dot(a, b, preferred_element_type=F32, **kw)


def log2(n):
    assert n & (n - 1) == 0
    return n.bit_length() - 1


def div(x, n):
    return lax.shift_right_logical(x, log2(n))


def mod(x, n):
    return x & (n - 1)


def pack_kernel(p, lat, outer, *inner):
    R, C, W, CH, T = p.R, p.C, p.W, p.CH, p.T

    def row_static(r, dest):
        lo, hi = dest * C - 2, dest * C - 2 + CH
        v = lat[r, max(lo, 0) : min(hi, W), :]
        parts = []
        if lo < 0:
            parts.append(jnp.zeros((-lo, p.c1), BF16))
        parts.append(v)
        if hi > W:
            parts.append(jnp.zeros((hi - W, p.c1), BF16))
        return jnp.concatenate(parts, axis=0) if len(parts) > 1 else v

    def row_dynamic(r, dest):
        at = pl.multiple_of(dest * C, 16)
        before = pl.multiple_of(jnp.maximum(at - 16, 0), 16)
        after = pl.multiple_of(jnp.minimum(at + C, W - 16), 16)
        return jnp.concatenate(
            [lat[r, pl.ds(before, 16), :][14:], lat[r, pl.ds(at, C), :], lat[r, pl.ds(after, 16), :][:2]],
            axis=0,
        )

    total = jnp.zeros((1, p.c1), F32)
    square = jnp.zeros((1, p.c1), F32)
    for r in range(R):
        x = lat[r].astype(F32)
        total = total + jnp.sum(x, axis=0, keepdims=True)
        square = square + jnp.sum(x * x, axis=0, keepdims=True)
    parts = []
    for s in (total, square):
        high = s.astype(BF16).astype(F32)
        middle = (s - high).astype(BF16).astype(F32)
        parts += [high, middle, s - high - middle]
    parts = jnp.concatenate(parts + [jnp.zeros((2, p.c1), F32)], axis=0).astype(BF16)
    for dest in range(p.peers):
        for r, at in ((0, 0), (1, CH), (R - 2, T + 8), (R - 1, T + 8 + CH)):
            outer[dest, at : at + CH, :] = row_static(r, dest)
        if 2 * CH < T:
            for at in (2 * CH, T + 8 + 2 * CH):
                outer[dest, at : at + T - 2 * CH, :] = jnp.zeros((T - 2 * CH, p.c1), BF16)
        outer[dest, T : T + 8, :] = parts
    me = lax.axis_index("frames")
    for s in range(p.peers):
        for i in range(R - 4):
            if p.swap:
                inner[s][i * CH : i * CH + CH, :] = row_dynamic(2 + i, lax.bitwise_xor(me, s))
            else:
                inner[0][s, i * CH : i * CH + CH, :] = row_static(2 + i, s)
        rest = (R - 4) * CH
        if not p.swap and rest < p.NB:
            inner[0][s, rest : p.NB, :] = jnp.zeros((p.NB - rest, p.c1), BF16)


def pack(p, latent):
    vm = pl.BlockSpec(memory_space=pltpu.VMEM)
    outs = [jax.ShapeDtypeStruct((p.peers, p.NA, p.c1), BF16)]
    if p.swap:
        outs += [jax.ShapeDtypeStruct((p.NB, p.c1), BF16)] * p.peers
    else:
        outs += [jax.ShapeDtypeStruct((p.peers, p.NB, p.c1), BF16)]
    outer, *inner = pl.pallas_call(
        functools.partial(pack_kernel, p),
        out_shape=outs,
        in_specs=[vm],
        out_specs=[vm] * len(outs),
        compiler_params=pltpu.CompilerParams(vmem_limit_bytes=32 * 2**20),
    )(latent)
    return outer, inner


def weights_kernel(w, out):
    u = [[w[3 * i + j].astype(F32) for j in range(3)] for i in range(3)]
    for a in range(2):
        for da in range(2):
            if a == 0:
                row = u[0] if da == 0 else [x + y for x, y in zip(u[1], u[2])]
            else:
                row = u[2] if da == 1 else [x + y for x, y in zip(u[0], u[1])]
            for b in range(2):
                pair = (row[0], row[1] + row[2]) if b == 0 else (row[0] + row[1], row[2])
                for db in range(2):
                    out[((a * 2 + b) * 2 + da) * 2 + db] = pair[db].astype(BF16)


def phase_weights(w):
    taps, c1, c2 = w.shape
    step = 64
    return pl.pallas_call(
        weights_kernel,
        grid=(c1 // step,),
        out_shape=jax.ShapeDtypeStruct((16, c1, c2), BF16),
        in_specs=[pl.BlockSpec((taps, step, c2), lambda i: (0, i, 0))],
        out_specs=pl.BlockSpec((16, step, c2), lambda i: (0, i, 0)),
        compiler_params=pltpu.CompilerParams(vmem_limit_bytes=16 * 2**20),
        cost_estimate=pl.CostEstimate(
            flops=20 * c1 * c2, transcendentals=0, bytes_accessed=50 * c1 * c2
        ),
    )(w)


def main_kernel(p, n_inner, clip, *refs):
    outer, inner = refs[0], refs[1 : 1 + n_inner]
    (above, below, across, gain, shift, w1_hbm, w2_hbm, wt, b1, b2, bt, out,
     cells, even, odd, feven, fodd, phase, second, act, w1, w2, start, sems) = refs[1 + n_inner :]
    F, R, C, CH, G, S, T, c1, c2 = p.F, p.R, p.C, p.CH, p.G, p.S, p.T, p.c1, p.c2
    copy1 = pltpu.make_async_copy(w1_hbm, w1, sems.at[0])
    copy2 = pltpu.make_async_copy(w2_hbm, w2, sems.at[1])
    copy1.start()
    copy2.start()
    me = lax.axis_index("frames")
    my_row = lax.axis_index("rows")

    parts = jnp.concatenate(
        [outer[f, T : T + 8, :].astype(F32) for f in range(F)]
        + [above[f, 0:8, :].astype(F32) for f in range(F)]
        + [below[f, T : T + 8, :].astype(F32) for f in range(F)]
        + [across[k, f].astype(F32) for k in range(p.row_peers - 3) for f in range(F)],
        axis=0,
    ).astype(BF16)
    i = lax.broadcasted_iota(jnp.int32, (2 * F, parts.shape[0]), 0)
    j = lax.broadcasted_iota(jnp.int32, (2 * F, parts.shape[0]), 1)
    kind = mod(j, 8)
    wanted = jnp.where(i < F, jnp.where(kind < 3, 1, 0), jnp.where((kind >= 3) & (kind < 6), 1, 0))
    pick = jnp.where((mod(div(j, 8), F) == mod(i, F)) & (wanted == 1), 1.0, 0.0).astype(BF16)
    sums = dot(pick, parts)
    per_group = c1 // GROUPS
    i = lax.broadcasted_iota(jnp.int32, (c1, c1), 0)
    j = lax.broadcasted_iota(jnp.int32, (c1, c1), 1)
    same = jnp.where(div(i, per_group) == div(j, per_group), 1.0, 0.0).astype(BF16)
    grouped = jnp.zeros((2 * F, c1), F32)
    for _ in range(3):
        term = sums.astype(BF16)
        grouped = grouped + dot(term, same)
        sums = sums - term.astype(F32)
    count = p.row_peers * R * p.W * per_group
    mean = grouped[:F] / count
    variance = grouped[F:] / count - mean * mean
    scale = lax.rsqrt(variance + GN_EPS) * gain[...]
    offset = shift[...] - mean * scale

    def turner(first):
        i = lax.broadcasted_iota(jnp.int32, (16 * F, 16 * F), 0)
        j = lax.broadcasted_iota(jnp.int32, (16 * F, 16 * F), 1)
        frame = lax.bitwise_xor(div(j, 16), first)
        return jnp.where((div(i, F) == mod(j, 16)) & (mod(i, F) == frame), 1.0, 0.0).astype(BF16)

    def turn(load, matrix, block, runs):
        lo_b = block
        turned = None
        for first, count, row in runs:
            lo, hi = max(first, lo_b), min(first + count, lo_b + 16)
            if lo >= hi:
                continue
            if turned is None:
                data = jnp.concatenate([load(f, lo_b) for f in range(F)], axis=0)
                turned = dot(matrix, data).reshape(16, F, c1)
                turned = silu(turned * scale[None] + offset[None])
            at = lo
            while at < hi:
                r, c = divmod(at - first, CH)
                n = min(hi - at, CH - c)
                cells[row + r, c : c + n] = turned[at - lo_b : at - lo_b + n]
                at += n

    plain = turner(0)
    inner_turn = turner(me) if n_inner > 1 else plain
    span = 2 * CH
    for block in sorted({min(b, p.NA - 16) for b in range(0, p.NA, 16)}):
        turn(lambda f, b: outer[f, b : b + 16, :], plain, block, [(0, span, 2), (T + 8, span, R)])
    for block in sorted({min(b, T + 8 - 16) for b in range(0, T + 8, 16)}):
        turn(lambda f, b: above[f, b : b + 16, :], plain, block, [(8, span, 0)])
        turn(lambda f, b: below[f, b : b + 16, :], plain, block, [(0, span, R + 2)])
    for block in range(0, p.NB, 16):
        if n_inner > 1:
            load = lambda f, b: inner[f][b : b + 16, :]
        else:
            load = lambda f, b: inner[0][f, b : b + 16, :]
        turn(load, inner_turn, block, [(0, (R - 4) * CH, 4)])

    @pl.when(me == 0)
    def _():
        cells[:, 0:2] = jnp.zeros((R + 4, 2, F, c1), F32)

    @pl.when(me == p.peers - 1)
    def _():
        cells[:, CH - 2 : CH] = jnp.zeros((R + 4, 2, F, c1), F32)

    @pl.when(my_row == 0)
    def _():
        cells[0:2] = jnp.zeros((2, CH, F, c1), F32)

    @pl.when(my_row == p.row_peers - 1)
    def _():
        cells[R + 2 : R + 4] = jnp.zeros((2, CH, F, c1), F32)

    def split(r, carry):
        even[r] = cells[r].reshape(CH // G, S, c1).astype(BF16)
        if G == 2:
            odd[r] = cells[r, 1 : CH - 1].reshape(CH // G - 1, S, c1).astype(BF16)
        return carry

    lax.fori_loop(0, R + 4, split, 0)

    def piece(e, o, r, nr, dc, n):
        if G == 1:
            v = e[pl.ds(r, nr), dc : dc + n]
        elif dc == 1:
            v = o[pl.ds(r, nr), 0:n]
        else:
            v = e[pl.ds(r, nr), dc // 2 : dc // 2 + n]
        return v.reshape(nr * n * S, v.shape[-1])

    n1 = (C + 2) // G
    nr1 = 2
    copy1.wait()
    left = jnp.where(me == 0, 1, 0)
    right = jnp.where(me == p.peers - 1, C + 1, C + 2)
    upper = jnp.where(my_row == 0, 1, 0)
    lower = jnp.where(my_row == p.row_peers - 1, R + 1, R + 2)

    def conv_one(i, carry):
        r = i * nr1
        acc = None
        for dr in range(3):
            for dc in range(3):
                t = dot(piece(even, odd, r + dr, nr1, dc, n1), w1[dr * 3 + dc])
                acc = t if acc is None else acc + t
        v = (acc + b1[...]).reshape(nr1, C + 2, F, c1)
        for k in range(nr1):
            row_in = jnp.logical_and(r + k >= upper, r + k < lower)
            col = lax.broadcasted_iota(jnp.int32, (C + 2, F, c1), 0)
            keep = jnp.logical_and(jnp.logical_and(col >= left, col < right), row_in)
            row = jnp.where(keep, v[k], 0.0)
            feven[r + k] = row.reshape(n1, S, c1).astype(BF16)
            if G == 2:
                fodd[r + k] = row[1 : C + 1].reshape(n1 - 1, S, c1).astype(BF16)
        return carry

    lax.fori_loop(0, (R + 2) // nr1, conv_one, 0)

    n2 = C // G
    nr2 = min(R, 4)
    copy2.wait()

    def conv_two(i, carry):
        r = i * nr2
        for a in range(2):
            for b in range(2):
                acc = None
                for da in range(2):
                    for db in range(2):
                        lhs = piece(feven, fodd, r + a + da, nr2, b + db, n2)
                        t = dot(lhs, w2[((a * 2 + b) * 2 + da) * 2 + db])
                        acc = t if acc is None else acc + t
                phase[a, b, pl.ds(r, nr2)] = (acc + b2[...]).astype(BF16).reshape(nr2, C * F, c2)
        return carry

    lax.fori_loop(0, R // nr2, conv_two, 0)

    q = p.q
    n = q * 2 * C
    i = lax.broadcasted_iota(jnp.int32, (n * F, n * F), 0)
    j = lax.broadcasted_iota(jnp.int32, (n * F, n * F), 1)
    source_cell = div(j, 2 * C * F) * (2 * C) + 2 * mod(div(j, F), C) + mod(div(j, C * F), 2)
    back = jnp.where((div(i, n) == mod(j, F)) & (mod(i, n) == source_cell), 1.0, 0.0).astype(BF16)
    for blk in range(2 * R // q):
        rows = range(blk * q, blk * q + q)
        x = jnp.concatenate([phase[o % 2, b, o // 2] for o in rows for b in range(2)], axis=0)
        turned = dot(back, x)
        second[:, blk * n : blk * n + n, :] = turned.astype(BF16).reshape(F, n, c2)
        act[:, blk * n : blk * n + n, :] = silu(turned).astype(BF16).reshape(F, n, c2)

    start[0] = 0

    def find(t, carry):
        start[t] = jnp.where(clip[t] == clip[t - 1], start[t - 1], t)
        return carry

    lax.fori_loop(1, F, find, 0)

    def temporal(t, carry):
        taps = [act[jnp.maximum(t - k * DILATION, start[t])] for k in range(TAPS)]
        lhs = jnp.concatenate(taps, axis=-1)
        out[t] = (dot(lhs, wt[...]) + second[t].astype(F32) + bt[...]).astype(BF16)
        return carry

    lax.fori_loop(0, F, temporal, 0)


def main(p, clip, outer, inner, above, below, across, gain, shift, w1, w2, wt, b1, b2, bt):
    F, R, C, CH, G, S, c1, c2 = p.F, p.R, p.C, p.CH, p.G, p.S, p.c1, p.c2
    vm = pl.BlockSpec(memory_space=pltpu.VMEM)
    sm = pl.BlockSpec(memory_space=pltpu.SMEM)
    hbm = pl.BlockSpec(memory_space=pl.ANY)
    odd_rows = 1 if G == 1 else R + 4
    fodd_rows = 1 if G == 1 else R + 2
    return pl.pallas_call(
        functools.partial(main_kernel, p, len(inner)),
        out_shape=jax.ShapeDtypeStruct((F, p.cells, c2), BF16),
        in_specs=[sm] + [vm] * (1 + len(inner) + 5) + [hbm, hbm] + [vm] * 4,
        out_specs=vm,
        scratch_shapes=[
            pltpu.VMEM((R + 4, CH, F, c1), F32),
            pltpu.VMEM((R + 4, CH // G, S, c1), BF16),
            pltpu.VMEM((odd_rows, CH // G - 1, S, c1), BF16),
            pltpu.VMEM((R + 2, (C + 2) // G, S, c1), BF16),
            pltpu.VMEM((fodd_rows, max(1, (C + 2) // G - 1), S, c1), BF16),
            pltpu.VMEM((2, 2, R, C * F, c2), BF16),
            pltpu.VMEM((F, p.cells, c2), BF16),
            pltpu.VMEM((F, p.cells, c2), BF16),
            pltpu.VMEM(w1.shape, BF16),
            pltpu.VMEM(w2.shape, BF16),
            pltpu.SMEM((F,), jnp.int32),
            pltpu.SemaphoreType.DMA((2,)),
        ],
        compiler_params=pltpu.CompilerParams(vmem_limit_bytes=60 * 2**20),
    )(clip, outer, *inner, above, below, across, gain, shift, w1, w2, wt, b1, b2, bt)


def per_device(
    latent, norm_gain, norm_shift, conv_one, bias_one, conv_two, bias_two,
    temporal_weight, bias_temporal, clip_ids,
):
    _, height, width, c1 = latent.shape
    c2 = conv_two.shape[-1]
    peers, row_peers = lax.axis_size("frames"), lax.axis_size("rows")
    p = Plan(clip_ids.shape[0], height, width // peers, width, c1, c2, row_peers)
    outer, inner = pack(p, latent[0])
    outer = lax.all_to_all(outer, "frames", split_axis=0, concat_axis=0, tiled=True)
    if p.swap:
        order = sorted(range(1, peers), key=lambda s: -(s // 4))
        got = {
            s: lax.ppermute(inner[s], "frames", [(i, i ^ s) for i in range(peers)]) for s in order
        }
        inner = [inner[0]] + [got[s] for s in range(1, peers)]
    else:
        inner = [lax.all_to_all(inner[0], "frames", split_axis=0, concat_axis=0, tiled=True)]

    def over_rows(v, by):
        return lax.ppermute(v, "rows", [(i, (i + by) % row_peers) for i in range(row_peers)])

    above = over_rows(outer[:, p.T :], 1)
    below = over_rows(outer[:, : p.T + 8], -1)
    sums = outer[:, p.T : p.T + 8]
    across = jnp.stack([over_rows(sums, by) for by in range(2, row_peers - 1)])
    out = main(
        p, clip_ids, outer, inner, above, below, across, norm_gain[None], norm_shift[None],
        conv_one.reshape(9, c1, c1), phase_weights(conv_two.reshape(9, c1, c2)),
        temporal_weight.reshape(TAPS * c2, c2), bias_one[None], bias_two[None], bias_temporal[None],
    )
    return out.reshape(p.F, 2 * height, 2 * p.C, c2)


def solution(mesh):
    in_specs = (P("frames", "rows", None, None), P(), P(), P(), P(), P(), P(), P(), P(), P())
    out_specs = P(None, "rows", "frames", None)
    return jax.shard_map(
        per_device, mesh=mesh, in_specs=in_specs, out_specs=out_specs, check_vma=False
    )
```

time: 91.8 us -> 75.3 us (0.82)
  the two profiles are of different devices: /device:TPU:1 before, /device:TPU:0 now
where the time goes in v2:
time: 75.3 us; the launch traced here: 75.1 us
  blocking collectives  25.9 us (34%)
  Pallas kernels  23.8 us (32%)
  starting transfers between devices  11.8 us (16%)
  waiting for transfers between devices  9.18 us (12%)
  local copies, waits for them, and re-layouts  4.27 us (6%)
    all_to_all x1, blocking collectives, per_device(): lax.all_to_all(outer, 'frames', split_axis=0, concat_axis=0, tiled=True)  25.9 us
    pallas_call x1, Pallas kernels, main(): pl.pallas_call(functools.partial(main_kernel, p, len(inner)), out_shape=j...  22 us
    ppermute x7, starting transfers between devices, per_device(): lax.ppermute(inner[s], 'frames', [(i, i ^ s) for i in range(peers)])  10.5 us
    ppermute x7, waiting for transfers between devices, per_device(): lax.ppermute(inner[s], 'frames', [(i, i ^ s) for i in range(peers)])  9.18 us
    unnamed x30, local copies, waits for them, and re-layouts  4.19 us
  transfers between devices with their start and end apart: 10, of which 4 were waited for; matrix products, arithmetic and copies ran while one was open for 0% of the time, Pallas kernels for 2%

profile of v2, /device:TPU:0, one launch (start us, length us, event | category | flops | bytes accessed | tf_op | source)
XLA Modules:
  0.0 75.1 jit_solution(18237610561012503931)
XLA Ops:
  0.0 1.4 %copy-done.2 = bf16[1,8,128,512]{3,2,1,0:T(8,128)(2,1)S(1)} copy-done((bf16[1,8,128,512]{3,2,1,0:T(8,128)(2,1)S(1)}, bf16[1,8,128,512]{3,2,1,0:T(8,128)(2,1)}, u32[]{:S(2)}) %copy-start.2) | copy-done | bytes 1048600
  1.4 0.6 shard_map.100
  1.9 0.0 copy-start.3
  1.9 25.9 %all_to_all.5.refs_0_ = bf16[8,88,512]{2,1,0:T(8,128)(2,1)S(1)} all-to-all(bf16[8,88,512]{2,1,0:T(8,128)(2,1)S(1)} %get-tuple-element.14), channel_id=1, replica_groups=mesh['frames'=8,'rows'=4] {'frames'}, dimensions={0} | all-to-all | bytes 1441792 | tf_op jit(solution)/shard_map/all_to_all | solution.py:388
  27.8 0.1 fusion
  27.9 0.1 collective-permute-start.8
  28.0 0.5 collective-permute-start.7
  28.5 1.4 %collective-permute-start = (bf16[80,512]{1,0:T(8,128)(2,1)S(1)}, bf16[80,512]{1,0:T(8,128)(2,1)S(1)}, u32[]{:S(2)}, u32[]{:S(2)}) collective-permute-start(bf16[80,512]{1,0:T(8,128)(2,1)S(1)} %get-tuple-element.16), channel_id=1, source_target_pairs={{0,4},{4,0},{8,12},{12,8},{16,20},{20,16},{24,28},{28,24},{1,5},{5... | collective-permute-start | bytes 245768 | tf_op jit(solution)/shard_map/ppermute | solution.py:392
  29.8 0.0 collective-permute-start.1
  29.9 2.1 %collective-permute-start.2 = (bf16[80,512]{1,0:T(8,128)(2,1)S(1)}, bf16[80,512]{1,0:T(8,128)(2,1)S(1)}, u32[]{:S(2)}, u32[]{:S(2)}) collective-permute-start(bf16[80,512]{1,0:T(8,128)(2,1)S(1)} %get-tuple-element.18), channel_id=1, source_target_pairs={{0,12},{4,8},{8,4},{12,0},{16,28},{20,24},{24,20},{28,16},{1,13},{... | collective-permute-start | bytes 245768 | tf_op jit(solution)/shard_map/ppermute | solution.py:392
  32.0 1.6 %collective-permute-done.refs_2_ = bf16[80,512]{1,0:T(8,128)(2,1)S(1)} collective-permute-done((bf16[80,512]{1,0:T(8,128)(2,1)S(1)}, bf16[80,512]{1,0:T(8,128)(2,1)S(1)}, u32[]{:S(2)}, u32[]{:S(2)}) %collective-permute-start) | collective-permute-done | bytes 81952 | tf_op jit(solution)/shard_map/ppermute | solution.py:392
  33.6 1.0 %collective-permute-start.3 = (bf16[80,512]{1,0:T(8,128)(2,1)S(1)}, bf16[80,512]{1,0:T(8,128)(2,1)S(1)}, u32[]{:S(2)}, u32[]{:S(2)}) collective-permute-start(bf16[80,512]{1,0:T(8,128)(2,1)S(1)} %get-tuple-element.19), channel_id=1, source_target_pairs={{0,16},{4,20},{8,24},{12,28},{16,0},{20,4},{24,8},{28,12},{1,17},{... | collective-permute-start | bytes 245768 | tf_op jit(solution)/shard_map/ppermute | solution.py:392
  34.6 0.5 collective-permute-done.1.refs_3_
  35.2 2.1 %collective-permute-start.4 = (bf16[80,512]{1,0:T(8,128)(2,1)S(1)}, bf16[80,512]{1,0:T(8,128)(2,1)S(1)}, u32[]{:S(2)}, u32[]{:S(2)}) collective-permute-start(bf16[80,512]{1,0:T(8,128)(2,1)S(1)} %get-tuple-element.20), channel_id=1, source_target_pairs={{0,20},{4,16},{8,28},{12,24},{16,4},{20,0},{24,12},{28,8},{1,21},{... | collective-permute-start | bytes 245768 | tf_op jit(solution)/shard_map/ppermute | solution.py:392
  37.3 0.0 collective-permute-done.2.refs_4_
  37.3 1.8 %collective-permute-start.5 = (bf16[80,512]{1,0:T(8,128)(2,1)S(1)}, bf16[80,512]{1,0:T(8,128)(2,1)S(1)}, u32[]{:S(2)}, u32[]{:S(2)}) collective-permute-start(bf16[80,512]{1,0:T(8,128)(2,1)S(1)} %get-tuple-element.21), channel_id=1, source_target_pairs={{0,24},{4,28},{8,16},{12,20},{16,8},{20,12},{24,0},{28,4},{1,25},{... | collective-permute-start | bytes 245768 | tf_op jit(solution)/shard_map/ppermute | solution.py:392
  39.1 5.9 %collective-permute-done.3.refs_5_ = bf16[80,512]{1,0:T(8,128)(2,1)S(1)} collective-permute-done((bf16[80,512]{1,0:T(8,128)(2,1)S(1)}, bf16[80,512]{1,0:T(8,128)(2,1)S(1)}, u32[]{:S(2)}, u32[]{:S(2)}) %collective-permute-start.3) | collective-permute-done | bytes 81952 | tf_op jit(solution)/shard_map/ppermute | solution.py:392
  45.0 2.0 %collective-permute-start.6 = (bf16[80,512]{1,0:T(8,128)(2,1)S(1)}, bf16[80,512]{1,0:T(8,128)(2,1)S(1)}, u32[]{:S(2)}, u32[]{:S(2)}) collective-permute-start(bf16[80,512]{1,0:T(8,128)(2,1)S(1)} %get-tuple-element.22), channel_id=1, source_target_pairs={{0,28},{4,24},{8,20},{12,16},{16,12},{20,8},{24,4},{28,0},{1,29},{... | collective-permute-start | bytes 245768 | tf_op jit(solution)/shard_map/ppermute | solution.py:392
  47.0 0.0 collective-permute-done.4.refs_6_
  47.0 0.8 %collective-permute-start.9 = (bf16[8,8,512]{2,1,0:T(8,128)(2,1)S(1)}, bf16[8,8,512]{2,1,0:T(8,128)(2,1)S(1)}, u32[]{:S(2)}, u32[]{:S(2)}) collective-permute-start(bf16[8,8,512]{2,1,0:T(8,128)(2,1)S(1)} %slice.14), channel_id=1, source_target_pairs={{0,2},{1,3},{2,0},{3,1},{4,6},{5,7},{6,4},{7,5},{8,10},{9,11},{10,... | collective-permute-start | bytes 196616 | tf_op jit(solution)/shard_map/ppermute | solution.py:399
  47.8 1.3 %shard_map.101.refs_15_ = bf16[16,512,256]{2,1,0:T(8,128)(2,1)S(1)} custom-call(bf16[9,512,256]{2,1,0:T(8,128)(2,1)S(1)} %bitcast.11), custom_call_target="tpu_custom_call" | custom-call | flops 2621440 | bytes 6553600 | tf_op jit(solution)/shard_map/pallas_call | solution.py:147
  49.1 1.9 %copy-done = bf16[16,512,256]{2,1,0:T(8,128)(2,1)} copy-done((bf16[16,512,256]{2,1,0:T(8,128)(2,1)}, bf16[16,512,256]{2,1,0:T(8,128)(2,1)S(1)}, u32[]{:S(2)}) %copy-start) | copy-done | bytes 4194328
  51.0 0.0 collective-permute-done.5.refs_7_
  51.0 1.2 %collective-permute-done.6.refs_8_ = bf16[80,512]{1,0:T(8,128)(2,1)S(1)} collective-permute-done((bf16[80,512]{1,0:T(8,128)(2,1)S(1)}, bf16[80,512]{1,0:T(8,128)(2,1)S(1)}, u32[]{:S(2)}, u32[]{:S(2)}) %collective-permute-start.6) | collective-permute-done | bytes 81952 | tf_op jit(solution)/shard_map/ppermute | solution.py:392
  52.1 0.0 collective-permute-done.9
  52.1 0.0 collective-permute-done.8.refs_10_
  52.2 0.0 collective-permute-done.7.refs_9_
  52.3 0.5 copy-done.13
  52.8 0.0 copy-done.14
  52.8 0.1 copy-done.5
  52.9 0.2 copy-done.6
  53.1 22.0 %shard_map.102 = bf16[8,512,256]{2,1,0:T(8,128)(2,1)} custom-call(s32[8]{0:T(128)} %clip.1, bf16[8,88,512]{2,1,0:T(8,128)(2,1)} %copy-done.4, bf16[80,512]{1,0:T(8,128)(2,1)} %copy-done.3, bf16[80,512]{1,0:T(8,128)(2,1)} %copy-done.7, bf16[80,512]{1,0:T(8,128)(2,1)} %copy-done.8, bf16[80,512]{1,0:T(8,128)(2,1)} %copy-done.9, bf16[80,512]{1,0:T(8,128)(2,1)} %copy-done.10, ...), custom_call_target="tpu_custom_call" | custom-call | tf_op jit(solution)/shard_map/pallas_call | solution.py:356
  (24 shorter events, 0.0 us)
Async XLA Ops:
  0.0 47.8 %copy-start.1 = (bf16[3,3,512,256]{3,2,1,0:T(8,128)(2,1)S(1)}, bf16[3,3,512,256]{3,2,1,0:T(8,128)(2,1)}, u32[]{:S(2)}) copy-start(bf16[3,3,512,256]{3,2,1,0:T(8,128)(2,1)} %param.15) | copy-start | bytes 7077892
  0.0 1.4 %copy-start.2 = (bf16[1,8,128,512]{3,2,1,0:T(8,128)(2,1)S(1)}, bf16[1,8,128,512]{3,2,1,0:T(8,128)(2,1)}, u32[]{:S(2)}) copy-start(bf16[1,8,128,512]{3,2,1,0:T(8,128)(2,1)} %param.10) | copy-start | bytes 3145732
  1.9 47.1 %copy-start.3 = (bf16[80,512]{1,0:T(8,128)(2,1)}, bf16[80,512]{1,0:T(8,128)(2,1)S(1)}, u32[]{:S(2)}) copy-start(bf16[80,512]{1,0:T(8,128)(2,1)S(1)} %get-tuple-element.15.refs_1_) | copy-start | bytes 245764
  27.8 24.3 %copy-start.4 = (bf16[8,88,512]{2,1,0:T(8,128)(2,1)}, bf16[8,88,512]{2,1,0:T(8,128)(2,1)S(1)}, u32[]{:S(2)}) copy-start(bf16[8,88,512]{2,1,0:T(8,128)(2,1)S(1)} %all_to_all.5.refs_0_) | copy-start | bytes 2162692
  27.9 24.2 %collective-permute-start.8 = (bf16[8,48,512]{2,1,0:T(8,128)(2,1)S(1)}, bf16[8,48,512]{2,1,0:T(8,128)(2,1)S(1)}, u32[]{:S(2)}, u32[]{:S(2)}) collective-permute-start(bf16[8,48,512]{2,1,0:T(8,128)(2,1)S(1)} %get-tuple-element.23), channel_id=1, source_target_pairs={{0,3},{1,0},{2,1},{3,2},{4,7},{5,4},{6,5},{7,6},{8,11},{9,8},{10,9... | collective-permute-start | bytes 1179656 | tf_op jit(solution)/shard_map/ppermute | solution.py:399
  28.0 24.2 %collective-permute-start.7 = (bf16[8,48,512]{2,1,0:T(8,128)(2,1)S(1)}, bf16[8,48,512]{2,1,0:T(8,128)(2,1)S(1)}, u32[]{:S(2)}, u32[]{:S(2)}) collective-permute-start(bf16[8,48,512]{2,1,0:T(8,128)(2,1)S(1)} %get-tuple-element.24), channel_id=1, source_target_pairs={{0,1},{1,2},{2,3},{3,0},{4,5},{5,6},{6,7},{7,4},{8,9},{9,10},{10,1... | collective-permute-start | bytes 1179656 | tf_op jit(solution)/shard_map/ppermute | solution.py:399
  28.5 5.1 %collective-permute-start = (bf16[80,512]{1,0:T(8,128)(2,1)S(1)}, bf16[80,512]{1,0:T(8,128)(2,1)S(1)}, u32[]{:S(2)}, u32[]{:S(2)}) collective-permute-start(bf16[80,512]{1,0:T(8,128)(2,1)S(1)} %get-tuple-element.16), channel_id=1, source_target_pairs={{0,4},{4,0},{8,12},{12,8},{16,20},{20,16},{24,28},{28,24},{1,5},{5... | collective-permute-start | bytes 245768 | tf_op jit(solution)/shard_map/ppermute | solution.py:392
  29.8 5.3 %collective-permute-start.1 = (bf16[80,512]{1,0:T(8,128)(2,1)S(1)}, bf16[80,512]{1,0:T(8,128)(2,1)S(1)}, u32[]{:S(2)}, u32[]{:S(2)}) collective-permute-start(bf16[80,512]{1,0:T(8,128)(2,1)S(1)} %get-tuple-element.17), channel_id=1, source_target_pairs={{0,8},{4,12},{8,0},{12,4},{16,24},{20,28},{24,16},{28,20},{1,9},{5... | collective-permute-start | bytes 245768 | tf_op jit(solution)/shard_map/ppermute | solution.py:392
  29.9 7.4 %collective-permute-start.2 = (bf16[80,512]{1,0:T(8,128)(2,1)S(1)}, bf16[80,512]{1,0:T(8,128)(2,1)S(1)}, u32[]{:S(2)}, u32[]{:S(2)}) collective-permute-start(bf16[80,512]{1,0:T(8,128)(2,1)S(1)} %get-tuple-element.18), channel_id=1, source_target_pairs={{0,12},{4,8},{8,4},{12,0},{16,28},{20,24},{24,20},{28,16},{1,13},{... | collective-permute-start | bytes 245768 | tf_op jit(solution)/shard_map/ppermute | solution.py:392
  33.6 18.6 %copy-start.7 = (bf16[80,512]{1,0:T(8,128)(2,1)}, bf16[80,512]{1,0:T(8,128)(2,1)S(1)}, u32[]{:S(2)}) copy-start(bf16[80,512]{1,0:T(8,128)(2,1)S(1)} %collective-permute-done.refs_2_) | copy-start | bytes 245764
  33.6 11.4 %collective-permute-start.3 = (bf16[80,512]{1,0:T(8,128)(2,1)S(1)}, bf16[80,512]{1,0:T(8,128)(2,1)S(1)}, u32[]{:S(2)}, u32[]{:S(2)}) collective-permute-start(bf16[80,512]{1,0:T(8,128)(2,1)S(1)} %get-tuple-element.19), channel_id=1, source_target_pairs={{0,16},{4,20},{8,24},{12,28},{16,0},{20,4},{24,8},{28,12},{1,17},{... | collective-permute-start | bytes 245768 | tf_op jit(solution)/shard_map/ppermute | solution.py:392
  35.2 17.1 %copy-start.8 = (bf16[80,512]{1,0:T(8,128)(2,1)}, bf16[80,512]{1,0:T(8,128)(2,1)S(1)}, u32[]{:S(2)}) copy-start(bf16[80,512]{1,0:T(8,128)(2,1)S(1)} %collective-permute-done.1.refs_3_) | copy-start | bytes 245764
  35.2 11.8 %collective-permute-start.4 = (bf16[80,512]{1,0:T(8,128)(2,1)S(1)}, bf16[80,512]{1,0:T(8,128)(2,1)S(1)}, u32[]{:S(2)}, u32[]{:S(2)}) collective-permute-start(bf16[80,512]{1,0:T(8,128)(2,1)S(1)} %get-tuple-element.20), channel_id=1, source_target_pairs={{0,20},{4,16},{8,28},{12,24},{16,4},{20,0},{24,12},{28,8},{1,21},{... | collective-permute-start | bytes 245768 | tf_op jit(solution)/shard_map/ppermute | solution.py:392
  37.3 14.9 %copy-start.9 = (bf16[80,512]{1,0:T(8,128)(2,1)}, bf16[80,512]{1,0:T(8,128)(2,1)S(1)}, u32[]{:S(2)}) copy-start(bf16[80,512]{1,0:T(8,128)(2,1)S(1)} %collective-permute-done.2.refs_4_) | copy-start | bytes 245764
  37.3 13.7 %collective-permute-start.5 = (bf16[80,512]{1,0:T(8,128)(2,1)S(1)}, bf16[80,512]{1,0:T(8,128)(2,1)S(1)}, u32[]{:S(2)}, u32[]{:S(2)}) collective-permute-start(bf16[80,512]{1,0:T(8,128)(2,1)S(1)} %get-tuple-element.21), channel_id=1, source_target_pairs={{0,24},{4,28},{8,16},{12,20},{16,8},{20,12},{24,0},{28,4},{1,25},{... | collective-permute-start | bytes 245768 | tf_op jit(solution)/shard_map/ppermute | solution.py:392
  45.0 7.2 %copy-start.10 = (bf16[80,512]{1,0:T(8,128)(2,1)}, bf16[80,512]{1,0:T(8,128)(2,1)S(1)}, u32[]{:S(2)}) copy-start(bf16[80,512]{1,0:T(8,128)(2,1)S(1)} %collective-permute-done.3.refs_5_) | copy-start | bytes 245764
  45.0 7.1 %collective-permute-start.6 = (bf16[80,512]{1,0:T(8,128)(2,1)S(1)}, bf16[80,512]{1,0:T(8,128)(2,1)S(1)}, u32[]{:S(2)}, u32[]{:S(2)}) collective-permute-start(bf16[80,512]{1,0:T(8,128)(2,1)S(1)} %get-tuple-element.22), channel_id=1, source_target_pairs={{0,28},{4,24},{8,20},{12,16},{16,12},{20,8},{24,4},{28,0},{1,29},{... | collective-permute-start | bytes 245768 | tf_op jit(solution)/shard_map/ppermute | solution.py:392
  47.0 5.3 %copy-start.11 = (bf16[80,512]{1,0:T(8,128)(2,1)}, bf16[80,512]{1,0:T(8,128)(2,1)S(1)}, u32[]{:S(2)}) copy-start(bf16[80,512]{1,0:T(8,128)(2,1)S(1)} %collective-permute-done.4.refs_6_) | copy-start | bytes 245764
  47.0 5.2 %collective-permute-start.9 = (bf16[8,8,512]{2,1,0:T(8,128)(2,1)S(1)}, bf16[8,8,512]{2,1,0:T(8,128)(2,1)S(1)}, u32[]{:S(2)}, u32[]{:S(2)}) collective-permute-start(bf16[8,8,512]{2,1,0:T(8,128)(2,1)S(1)} %slice.14), channel_id=1, source_target_pairs={{0,2},{1,3},{2,0},{3,1},{4,6},{5,7},{6,4},{7,5},{8,10},{9,11},{10,... | collective-permute-start | bytes 196616 | tf_op jit(solution)/shard_map/ppermute | solution.py:399
  49.0 1.9 %copy-start = (bf16[16,512,256]{2,1,0:T(8,128)(2,1)}, bf16[16,512,256]{2,1,0:T(8,128)(2,1)S(1)}, u32[]{:S(2)}) copy-start(bf16[16,512,256]{2,1,0:T(8,128)(2,1)S(1)} %shard_map.101.refs_15_) | copy-start | bytes 12582916
  51.0 1.3 %copy-start.12 = (bf16[80,512]{1,0:T(8,128)(2,1)}, bf16[80,512]{1,0:T(8,128)(2,1)S(1)}, u32[]{:S(2)}) copy-start(bf16[80,512]{1,0:T(8,128)(2,1)S(1)} %collective-permute-done.5.refs_7_) | copy-start | bytes 245764
  52.1 0.6 copy-start.13
  52.1 0.7 copy-start.14
  52.2 0.8 %copy-start.5 = (bf16[8,48,512]{2,1,0:T(8,128)(2,1)}, bf16[8,48,512]{2,1,0:T(8,128)(2,1)S(1)}, u32[]{:S(2)}) copy-start(bf16[8,48,512]{2,1,0:T(8,128)(2,1)S(1)} %collective-permute-done.8.refs_10_) | copy-start | bytes 1179652
  52.2 0.9 %copy-start.6 = (bf16[8,48,512]{2,1,0:T(8,128)(2,1)}, bf16[8,48,512]{2,1,0:T(8,128)(2,1)S(1)}, u32[]{:S(2)}) copy-start(bf16[8,48,512]{2,1,0:T(8,128)(2,1)S(1)} %collective-permute-done.7.refs_9_) | copy-start | bytes 1179652

commit v3 on v2

v3 whole, which is shorter than its diff:
```python
import functools

import jax
import jax.numpy as jnp
from jax import lax
from jax.experimental import pallas as pl
from jax.experimental.pallas import tpu as pltpu
from jax.sharding import PartitionSpec as P

GROUPS = 32
TAPS = 3
DILATION = 2
GN_EPS = 1e-06
BF16, F32 = jnp.bfloat16, jnp.float32


def up_to(n, m):
    return -(-n // m) * m


class Plan:
    def __init__(self, frames, rows, cols, width, c1, c2, row_peers):
        self.F, self.R, self.C, self.W, self.c1, self.c2 = frames, rows, cols, width, c1, c2
        self.row_peers = row_peers
        self.peers = width // cols
        self.CH = cols + 4
        self.G = max(1, 16 // frames)
        self.S = self.G * frames
        self.T = up_to(2 * self.CH, 8)
        self.NA = 2 * self.T + 8
        self.NB = up_to((rows - 4) * self.CH, 16)
        self.q = max(1, 16 // (2 * cols))
        self.cells = 2 * rows * 2 * cols
        packed = (rows + 4) * self.CH * frames * c1
        self.vmem = 11 * packed + 24 * self.cells * frames * c2 // 2 + 4 * 2**20
        self.near = self.peers // 2
        self.swap = self.peers <= 8 and cols % 16 == 0


def silu(v):
    h = 0.5 * v
    return h + h * jnp.tanh(h)


def dot(a, b, **kw):
    return jnp.dot(a, b, preferred_element_type=F32, **kw)


def log2(n):
    assert n & (n - 1) == 0
    return n.bit_length() - 1


def div(x, n):
    return lax.shift_right_logical(x, log2(n))


def mod(x, n):
    return x & (n - 1)


def messages(p, refs):
    if not p.swap:
        whole = [refs[0].at[f] for f in range(p.peers)]
        return [r.at[: p.NA] for r in whole], [r.at[p.NA :] for r in whole]
    near, far = refs[: p.near], refs[p.near :]
    outer, inner = far[: p.peers - p.near], far[p.peers - p.near :]
    return (
        [r.at[: p.NA] for r in near] + list(outer),
        [r.at[p.NA :] for r in near] + list(inner),
    )


def pack_kernel(p, lat, *refs):
    R, C, W, CH, T = p.R, p.C, p.W, p.CH, p.T
    outer, inner = messages(p, refs)

    def row_static(r, dest):
        lo, hi = dest * C - 2, dest * C - 2 + CH
        v = lat[r, max(lo, 0) : min(hi, W), :]
        parts = []
        if lo < 0:
            parts.append(jnp.zeros((-lo, p.c1), BF16))
        parts.append(v)
        if hi > W:
            parts.append(jnp.zeros((hi - W, p.c1), BF16))
        return jnp.concatenate(parts, axis=0) if len(parts) > 1 else v

    def row_dynamic(r, dest):
        at = pl.multiple_of(dest * C, 16)
        before = pl.multiple_of(jnp.maximum(at - 16, 0), 16)
        after = pl.multiple_of(jnp.minimum(at + C, W - 16), 16)
        return jnp.concatenate(
            [lat[r, pl.ds(before, 16), :][14:], lat[r, pl.ds(at, C), :], lat[r, pl.ds(after, 16), :][:2]],
            axis=0,
        )

    total = jnp.zeros((1, p.c1), F32)
    square = jnp.zeros((1, p.c1), F32)
    for r in range(R):
        x = lat[r].astype(F32)
        total = total + jnp.sum(x, axis=0, keepdims=True)
        square = square + jnp.sum(x * x, axis=0, keepdims=True)
    parts = []
    for s in (total, square):
        high = s.astype(BF16).astype(F32)
        middle = (s - high).astype(BF16).astype(F32)
        parts += [high, middle, s - high - middle]
    parts = jnp.concatenate(parts + [jnp.zeros((2, p.c1), F32)], axis=0).astype(BF16)
    me = lax.axis_index("frames")
    for s in range(p.peers):
        a, b = outer[s], inner[s]
        if p.swap:
            load = functools.partial(row_dynamic, dest=lax.bitwise_xor(me, s))
        else:
            load = functools.partial(row_static, dest=s)
        for r, at in ((0, 0), (1, CH), (R - 2, T + 8), (R - 1, T + 8 + CH)):
            a[at : at + CH, :] = load(r)
        if 2 * CH < T:
            for at in (2 * CH, T + 8 + 2 * CH):
                a[at : at + T - 2 * CH, :] = jnp.zeros((T - 2 * CH, p.c1), BF16)
        a[T : T + 8, :] = parts
        for i in range(R - 4):
            b[i * CH : i * CH + CH, :] = load(2 + i)
        rest = (R - 4) * CH
        if rest < p.NB:
            b[rest : p.NB, :] = jnp.zeros((p.NB - rest, p.c1), BF16)


def pack(p, latent):
    vm = pl.BlockSpec(memory_space=pltpu.VMEM)
    n = p.NA + p.NB
    shapes = [(p.peers, n, p.c1)]
    if p.swap:
        far = p.peers - p.near
        shapes = [(n, p.c1)] * p.near + [(p.NA, p.c1)] * far + [(p.NB, p.c1)] * far
    outs = [jax.ShapeDtypeStruct(s, BF16) for s in shapes]
    return pl.pallas_call(
        functools.partial(pack_kernel, p),
        out_shape=outs,
        in_specs=[vm],
        out_specs=[vm] * len(outs),
        compiler_params=pltpu.CompilerParams(vmem_limit_bytes=32 * 2**20),
    )(latent)


def weights_kernel(w, out):
    u = [[w[3 * i + j].astype(F32) for j in range(3)] for i in range(3)]
    for a in range(2):
        for da in range(2):
            if a == 0:
                row = u[0] if da == 0 else [x + y for x, y in zip(u[1], u[2])]
            else:
                row = u[2] if da == 1 else [x + y for x, y in zip(u[0], u[1])]
            for b in range(2):
                pair = (row[0], row[1] + row[2]) if b == 0 else (row[0] + row[1], row[2])
                for db in range(2):
                    out[((a * 2 + b) * 2 + da) * 2 + db] = pair[db].astype(BF16)


def phase_weights(w):
    taps, c1, c2 = w.shape
    step = 64
    return pl.pallas_call(
        weights_kernel,
        grid=(c1 // step,),
        out_shape=jax.ShapeDtypeStruct((16, c1, c2), BF16),
        in_specs=[pl.BlockSpec((taps, step, c2), lambda i: (0, i, 0))],
        out_specs=pl.BlockSpec((16, step, c2), lambda i: (0, i, 0)),
        compiler_params=pltpu.CompilerParams(vmem_limit_bytes=16 * 2**20),
        cost_estimate=pl.CostEstimate(
            flops=20 * c1 * c2, transcendentals=0, bytes_accessed=50 * c1 * c2
        ),
    )(w)


def face_kernel(p, n, second, *refs):
    outer, _ = messages(p, list(refs[:n]) + [None] * (p.peers - p.near))
    T = p.T
    odd = lax.bitwise_and(lax.axis_index("rows"), 1)
    to_above = odd == (0 if second else 1)
    out = refs[-2] if second else refs[-1]

    @pl.when(to_above)
    def _():
        for f in range(p.F):
            out[f, 0:T] = outer[f][0:T, :]

    @pl.when(jnp.logical_not(to_above))
    def _():
        for f in range(p.F):
            out[f, 0:T] = outer[f][T + 8 : 2 * T + 8, :]

    for f in range(p.F):
        sums = outer[f][T : T + 8, :]
        out[f, T : T + 8] = sums
        if second:
            theirs = refs[n][f, T : T + 8]
            out[f, T + 8 : T + 16] = theirs
            refs[-1][f, 0:8] = sums
            refs[-1][f, 8:16] = theirs


def face(p, got, first=None):
    vm = pl.BlockSpec(memory_space=pltpu.VMEM)
    rows = [p.T + 8] if first is None else [p.T + 16, 16]
    args = list(got) + ([] if first is None else [first])
    out = pl.pallas_call(
        functools.partial(face_kernel, p, len(got), first is not None),
        out_shape=[jax.ShapeDtypeStruct((p.F, r, p.c1), BF16) for r in rows],
        in_specs=[vm] * len(args),
        out_specs=[vm] * len(rows),
        compiler_params=pltpu.CompilerParams(vmem_limit_bytes=16 * 2**20),
        cost_estimate=pl.CostEstimate(flops=1, transcendentals=0, bytes_accessed=1),
    )(*args)
    return out[0] if first is None else out


def turner(p, first):
    F = p.F
    i = lax.broadcasted_iota(jnp.int32, (16 * F, 16 * F), 0)
    j = lax.broadcasted_iota(jnp.int32, (16 * F, 16 * F), 1)
    frame = lax.bitwise_xor(div(j, 16), first)
    return jnp.where((div(i, F) == mod(j, 16)) & (mod(i, F) == frame), 1.0, 0.0).astype(BF16)


def turn(p, load, matrix, scale, offset, block, runs, cells):
    if not any(max(f, block) < min(f + n, block + 16) for f, n, _ in runs):
        return
    data = jnp.concatenate([load(f, block) for f in range(p.F)], axis=0)
    turned = dot(matrix, data).reshape(16, p.F, p.c1)
    turned = silu(turned * scale[None] + offset[None])
    for first, count, row in runs:
        at, hi = max(first, block), min(first + count, block + 16)
        while at < hi:
            r, c = divmod(at - first, p.CH)
            n = min(hi - at, p.CH - c)
            cells[row + r, c : c + n] = turned[at - block : at - block + n]
            at += n


def clear_columns(p, cells, me):
    rows = cells.shape[0]

    @pl.when(me == 0)
    def _():
        cells[:, 0:2] = jnp.zeros((rows, 2, p.F, p.c1), F32)

    @pl.when(me == p.peers - 1)
    def _():
        cells[:, p.CH - 2 : p.CH] = jnp.zeros((rows, 2, p.F, p.c1), F32)


def pair_cells(p, row, even, odd):
    n = row.shape[0]
    even[...] = row.reshape(n // p.G, p.S, p.c1).astype(BF16)
    if p.G == 2:
        odd[...] = row[1 : n - 1].reshape(n // 2 - 1, p.S, p.c1).astype(BF16)


def shifted(p, rows, first, count, dc, n):
    parts = []
    for r in range(first, first + count) if isinstance(first, int) else first:
        even, odd = rows[r]
        if p.G == 1:
            v = even[dc : dc + n]
        elif dc == 1:
            v = odd[0:n]
        else:
            v = even[dc // 2 : dc // 2 + n]
        parts.append(v.reshape(n * p.S, p.c1))
    return jnp.concatenate(parts, axis=0)


def conv_one(p, out_rows, hidden, w1, b1, me, my_row, store):
    F, R, C, c1 = p.F, p.R, p.C, p.c1
    acc = None
    for dr in range(3):
        for dc in range(3):
            lhs = shifted(p, hidden, [r + dr for r in out_rows], 0, dc, (C + 2) // p.G)
            u = dot(lhs, w1[dr, dc])
            acc = u if acc is None else acc + u
    v = (acc + b1[...]).reshape(len(out_rows), C + 2, F, c1)
    left = jnp.where(me == 0, 1, 0)
    right = jnp.where(me == p.peers - 1, C + 1, C + 2)
    col = lax.broadcasted_iota(jnp.int32, (C + 2, F, c1), 0)
    for k, r in enumerate(out_rows):
        keep = (col >= left) & (col < right)
        if r == 0:
            keep = keep & (my_row > 0)
        if r == R + 1:
            keep = keep & (my_row < p.row_peers - 1)
        even, odd = store[r]
        pair_cells(p, jnp.where(keep, v[k], 0.0), even, odd)


def outer_kernel(p, n, *refs):
    outer, _ = messages(p, list(refs[:n]) + [None] * (p.peers - p.near))
    (face1, face2, sums2, gain, shift, w1, b1,
     norm, heven, hodd, feven, fodd, cells, teven, todd) = refs[n:]
    F, R, CH, T, c1 = p.F, p.R, p.CH, p.T, p.c1
    me = lax.axis_index("frames")
    my_row = lax.axis_index("rows")
    xor = me if p.swap else 0

    parts = jnp.concatenate(
        [outer[f][T : T + 8, :].astype(F32) for f in range(F)]
        + [face1[f, T : T + 8, :].astype(F32) for f in range(F)]
        + [face2[f, at : at + 8, :].astype(F32) for at in (T, T + 8) for f in range(F)]
        + [sums2[f, at : at + 8, :].astype(F32) for at in (0, 8) for f in range(F)],
        axis=0,
    ).astype(BF16)
    i = lax.broadcasted_iota(jnp.int32, (2 * F, parts.shape[0]), 0)
    j = lax.broadcasted_iota(jnp.int32, (2 * F, parts.shape[0]), 1)
    kind = mod(j, 8)
    wanted = jnp.where(i < F, jnp.where(kind < 3, 1, 0), jnp.where((kind >= 3) & (kind < 6), 1, 0))
    sent = lax.bitwise_xor(mod(div(j, 8), F), xor)
    pick = jnp.where((sent == mod(i, F)) & (wanted == 1), 1.0, 0.0).astype(BF16)
    sums = dot(pick, parts)
    per_group = c1 // GROUPS
    i = lax.broadcasted_iota(jnp.int32, (c1, c1), 0)
    j = lax.broadcasted_iota(jnp.int32, (c1, c1), 1)
    same = jnp.where(div(i, per_group) == div(j, per_group), 1.0, 0.0).astype(BF16)
    grouped = jnp.zeros((2 * F, c1), F32)
    for _ in range(3):
        term = sums.astype(BF16)
        grouped = grouped + dot(term, same)
        sums = sums - term.astype(F32)
    count = p.row_peers * R * p.W * per_group
    mean = grouped[:F] / count
    variance = grouped[F:] / count - mean * mean
    scale = lax.rsqrt(variance + GN_EPS) * gain[...]
    offset = shift[...] - mean * scale
    norm[0] = scale
    norm[1] = offset

    matrix = turner(p, xor)
    span = 2 * CH
    for block in sorted({min(b, p.NA - 16) for b in range(0, p.NA, 16)}):
        turn(p, lambda f, b: outer[f][b : b + 16, :], matrix, scale, offset, block,
             [(0, span, 2), (T + 8, span, 4)], cells)
    odd = lax.bitwise_and(my_row, 1)
    for block in range(0, span, 16):
        turn(p, lambda f, b: face1[f, b : b + 16, :], matrix, scale, offset, block,
             [(0, span, 6 - 6 * odd)], cells)
        turn(p, lambda f, b: face2[f, b : b + 16, :], matrix, scale, offset, block,
             [(0, span, 6 * odd)], cells)
    clear_columns(p, cells, me)

    @pl.when(my_row == 0)
    def _():
        cells[0:2] = jnp.zeros((2, CH, F, c1), F32)

    @pl.when(my_row == p.row_peers - 1)
    def _():
        cells[6:8] = jnp.zeros((2, CH, F, c1), F32)

    hidden = {}
    for k in range(8):
        if 2 <= k < 6:
            even, odd = heven.at[k - 2], hodd.at[k - 2]
        else:
            even, odd = teven.at[k % 4], todd.at[k % 4]
        pair_cells(p, cells[k], even, odd)
        hidden[k if k < 4 else R + k - 4] = (even, odd)
    rows = [0, 1, R, R + 1]
    store = {r: (feven.at[k], fodd.at[k]) for k, r in enumerate(rows)}
    conv_one(p, rows, hidden, w1, b1, me, my_row, store)


def inner_kernel(p, n, clip, *refs):
    _, inner = messages(p, list(refs[: p.near]) + [None] * (p.peers - p.near) + list(refs[p.near : n])
                        if p.swap else refs[:n])
    (norm, heven, hodd, feven_in, fodd_in, w1, w2, wt, b1, b2, bt, out,
     cells, even, odd, feven, fodd, phase, second, act, start) = refs[n:]
    F, R, C, CH, S, c1, c2 = p.F, p.R, p.C, p.CH, p.S, p.c1, p.c2
    me = lax.axis_index("frames")
    my_row = lax.axis_index("rows")
    scale, offset = norm[0], norm[1]
    matrix = turner(p, me if p.swap else 0)
    for block in range(0, p.NB, 16):
        turn(p, lambda f, b: inner[f][b : b + 16, :], matrix, scale, offset, block,
             [(0, (R - 4) * CH, 0)], cells)
    clear_columns(p, cells, me)
    hidden = {r: (heven.at[k], hodd.at[k]) for k, r in enumerate((2, 3, R, R + 1))}
    for k in range(R - 4):
        hidden[4 + k] = (even.at[k], odd.at[k])
        pair_cells(p, cells[k], even.at[k], odd.at[k])
    first = {r: (feven_in.at[k], fodd_in.at[k]) for k, r in enumerate((0, 1, R, R + 1))}
    inside = {r: (feven.at[r - 2], fodd.at[r - 2]) for r in range(2, R)}
    conv_one(p, list(range(2, R)), hidden, w1, b1, me, my_row, inside)
    first.update(inside)

    for a in range(2):
        for b in range(2):
            acc = None
            for da in range(2):
                for db in range(2):
                    lhs = shifted(p, first, a + da, R, b + db, C // p.G)
                    u = dot(lhs, w2[((a * 2 + b) * 2 + da) * 2 + db])
                    acc = u if acc is None else acc + u
            phase[a, b] = (acc + b2[...]).astype(BF16).reshape(R, C * F, c2)

    q = p.q
    n = q * 2 * C
    i = lax.broadcasted_iota(jnp.int32, (n * F, n * F), 0)
    j = lax.broadcasted_iota(jnp.int32, (n * F, n * F), 1)
    source_cell = div(j, 2 * C * F) * (2 * C) + 2 * mod(div(j, F), C) + mod(div(j, C * F), 2)
    back = jnp.where((div(i, n) == mod(j, F)) & (mod(i, n) == source_cell), 1.0, 0.0).astype(BF16)
    for blk in range(2 * R // q):
        rows = range(blk * q, blk * q + q)
        x = jnp.concatenate([phase[o % 2, b, o // 2] for o in rows for b in range(2)], axis=0)
        turned = dot(back, x)
        second[:, blk * n : blk * n + n, :] = turned.astype(BF16).reshape(F, n, c2)
        act[:, blk * n : blk * n + n, :] = silu(turned).astype(BF16).reshape(F, n, c2)

    start[0] = 0

    def find(t, carry):
        start[t] = jnp.where(clip[t] == clip[t - 1], start[t - 1], t)
        return carry

    lax.fori_loop(1, F, find, 0)

    def temporal(t, carry):
        taps = [act[jnp.maximum(t - k * DILATION, start[t])] for k in range(TAPS)]
        lhs = jnp.concatenate(taps, axis=-1)
        out[t] = (dot(lhs, wt[...]) + second[t].astype(F32) + bt[...]).astype(BF16)
        return carry

    if F <= 8:
        for t in range(F):
            temporal(t, 0)
    else:
        lax.fori_loop(0, F, temporal, 0)


def outer_rows(p, got, face1, face2, sums2, gain, shift, w1, b1):
    F, C, CH, G, S, c1 = p.F, p.C, p.CH, p.G, p.S, p.c1
    vm = pl.BlockSpec(memory_space=pltpu.VMEM)
    pairs = lambda rows, cells: [(rows, cells // G, S, c1), (rows, max(1, cells // G - 1), S, c1)]
    return pl.pallas_call(
        functools.partial(outer_kernel, p, len(got)),
        out_shape=[jax.ShapeDtypeStruct((2, F, c1), F32)]
        + [jax.ShapeDtypeStruct(s, BF16) for s in pairs(4, CH) + pairs(4, C + 2)],
        in_specs=[vm] * (len(got) + 7),
        out_specs=[vm] * 5,
        scratch_shapes=[pltpu.VMEM((8, CH, F, c1), F32)] + [pltpu.VMEM(s, BF16) for s in pairs(4, CH)],
        compiler_params=pltpu.CompilerParams(vmem_limit_bytes=p.vmem),
        cost_estimate=pl.CostEstimate(
            flops=2 * 9 * 4 * (C + 2) * F * c1 * c1, transcendentals=8 * CH * F * c1,
            bytes_accessed=2 * 9 * c1 * c1,
        ),
    )(*got, face1, face2, sums2, gain, shift, w1, b1)


def inner_rows(p, clip, got, norm, hidden, first, w1, w2, wt, b1, b2, bt):
    F, R, C, CH, G, S, c1, c2 = p.F, p.R, p.C, p.CH, p.G, p.S, p.c1, p.c2
    vm = pl.BlockSpec(memory_space=pltpu.VMEM)
    sm = pl.BlockSpec(memory_space=pltpu.SMEM)
    pairs = lambda rows, cells: [(rows, cells // G, S, c1), (rows, max(1, cells // G - 1), S, c1)]
    return pl.pallas_call(
        functools.partial(inner_kernel, p, len(got)),
        out_shape=jax.ShapeDtypeStruct((F, p.cells, c2), BF16),
        in_specs=[sm] + [vm] * (len(got) + 11),
        out_specs=vm,
        scratch_shapes=[pltpu.VMEM((R - 4, CH, F, c1), F32)]
        + [pltpu.VMEM(s, BF16) for s in pairs(R - 4, CH) + pairs(R - 2, C + 2)]
        + [
            pltpu.VMEM((2, 2, R, C * F, c2), BF16),
            pltpu.VMEM((F, p.cells, c2), BF16),
            pltpu.VMEM((F, p.cells, c2), BF16),
            pltpu.SMEM((F,), jnp.int32),
        ],
        compiler_params=pltpu.CompilerParams(vmem_limit_bytes=p.vmem),
        cost_estimate=pl.CostEstimate(
            flops=2 * (9 * (R - 2) * (C + 2) * c1 + 16 * R * C * c2) * F * c1,
            transcendentals=p.cells * F * c2, bytes_accessed=34 * c1 * c1,
        ),
    )(clip, *got, norm, *hidden, *first, w1, w2, wt, b1, b2, bt)


def per_device(
    latent, norm_gain, norm_shift, conv_one_w, bias_one, conv_two, bias_two,
    temporal_weight, bias_temporal, clip_ids,
):
    _, height, width, c1 = latent.shape
    c2 = conv_two.shape[-1]
    peers, row_peers = lax.axis_size("frames"), lax.axis_size("rows")
    p = Plan(clip_ids.shape[0], height, width // peers, width, c1, c2, row_peers)
    got = list(pack(p, latent[0]))
    far = range(p.near, peers)

    def swap(v, s):
        return lax.ppermute(v, "frames", [(i, i ^ s) for i in range(peers)])

    def after(v, k):
        v, got[k] = lax.optimization_barrier((v, got[k]))
        return v

    if p.swap:
        near, one, two = got[: p.near], got[p.near : peers], got[peers:]
        got = near + [swap(v, s) for v, s in zip(one, far)]
        for s in range(1, p.near):
            got[s] = swap(near[s], s)
        two = [swap(after(v, s), s) for v, s in zip(two, far)]
        last = got[: p.near] + two
    else:
        got = [lax.all_to_all(got[0], "frames", split_axis=0, concat_axis=0, tiled=True)]
        last = got

    def over_rows(v, *pairs):
        return lax.ppermute(v, "rows", [(i, j) for a, b in pairs for i, j in ((a, b), (b, a))])

    assert row_peers == 4
    face1 = over_rows(face(p, got), (0, 1), (2, 3))
    face2, sums2 = face(p, got, face1)
    face2, sums2 = over_rows(face2, (1, 2)), over_rows(sums2, (0, 3))
    w1 = conv_one_w.reshape(3, 3, c1, c1)
    norm, *packed = outer_rows(
        p, got, face1, face2, sums2, norm_gain[None], norm_shift[None], w1, bias_one[None]
    )
    out = inner_rows(
        p, clip_ids, last, norm, packed[:2], packed[2:], w1,
        phase_weights(conv_two.reshape(9, c1, c2)), temporal_weight.reshape(TAPS * c2, c2),
        bias_one[None], bias_two[None], bias_temporal[None],
    )
    return out.reshape(p.F, 2 * height, 2 * p.C, c2)


def solution(mesh):
    in_specs = (P("frames", "rows", None, None), P(), P(), P(), P(), P(), P(), P(), P(), P())
    out_specs = P(None, "rows", "frames", None)
    return jax.shard_map(
        per_device, mesh=mesh, in_specs=in_specs, out_specs=out_specs, check_vma=False
    )
```

time: 75.3 us -> 62.4 us (0.83)
  the two profiles are of different devices: /device:TPU:0 before, /device:TPU:17 now
where the time goes in v3:
time: 62.4 us; the launch traced here: 62.2 us
  starting transfers between devices  21.8 us (35%)
  Pallas kernels  19.9 us (32%)
  waiting for transfers between devices  18.9 us (30%)
  local copies, waits for them, and re-layouts  1.43 us (2%)
    ppermute x11, waiting for transfers between devices, swap(): return lax.ppermute(v, 'frames', [(i, i ^ s) for i in range(peers)])  17.1 us
    ppermute x11, starting transfers between devices, swap(): return lax.ppermute(v, 'frames', [(i, i ^ s) for i in range(peers)])  16.9 us
    pallas_call x1, Pallas kernels, inner_rows(): pl.pallas_call(functools.partial(inner_kernel, p, len(got)), out_shape=ja...  13.9 us
    ppermute x3, starting transfers between devices, over_rows(): lax.ppermute(v, 'rows', [(i, j) for a, b in pairs for i, j in ((a, b), (b...  4.93 us
    pallas_call x1, Pallas kernels, outer_rows(): pl.pallas_call(functools.partial(outer_kernel, p, len(got)), out_shape=[j...  4.03 us
    ppermute x3, waiting for transfers between devices, over_rows(): lax.ppermute(v, 'rows', [(i, j) for a, b in pairs for i, j in ((a, b), (b...  1.8 us
    unnamed x20, local copies, waits for them, and re-layouts  1.43 us
    pallas_call x1, Pallas kernels, phase_weights(): pl.pallas_call(weights_kernel, grid=(c1 // step,), out_shape=jax.ShapeDty...  1.28 us
  transfers between devices with their start and end apart: 14, of which 7 were waited for; matrix products, arithmetic and copies ran while one was open for 0% of the time, Pallas kernels for 9%

profile of v3, /device:TPU:17, one launch (start us, length us, event | category | flops | bytes accessed | tf_op | source)
XLA Modules:
  0.0 62.2 jit_solution(8309280312610575192)
XLA Ops:
  0.0 1.4 %copy-done.1 = bf16[1,8,128,512]{3,2,1,0:T(8,128)(2,1)S(1)} copy-done((bf16[1,8,128,512]{3,2,1,0:T(8,128)(2,1)S(1)}, bf16[1,8,128,512]{3,2,1,0:T(8,128)(2,1)}, u32[]{:S(2)}) %copy-start.1) | copy-done | bytes 1048600
  1.4 0.6 shard_map.100
  2.0 0.1 collective-permute-start.3
  2.1 3.3 %collective-permute-start.5 = (bf16[88,512]{1,0:T(8,128)(2,1)S(1)}, bf16[88,512]{1,0:T(8,128)(2,1)S(1)}, u32[]{:S(2)}, u32[]{:S(2)}) collective-permute-start(bf16[88,512]{1,0:T(8,128)(2,1)S(1)} %get-tuple-element.40), channel_id=1, source_target_pairs={{0,20},{4,16},{8,28},{12,24},{16,4},{20,0},{24,12},{28,8},{1,21},{... | collective-permute-start | bytes 270344 | tf_op jit(solution)/shard_map/ppermute | solution.py:495
  5.4 0.3 collective-permute-start
  5.6 1.3 %collective-permute-start.1 = (bf16[168,512]{1,0:T(8,128)(2,1)S(1)}, bf16[168,512]{1,0:T(8,128)(2,1)S(1)}, u32[]{:S(2)}, u32[]{:S(2)}) collective-permute-start(bf16[168,512]{1,0:T(8,128)(2,1)S(1)} %get-tuple-element.34), channel_id=1, source_target_pairs={{0,8},{4,12},{8,0},{12,4},{16,24},{20,28},{24,16},{28,20},{1,9},{5... | collective-permute-start | bytes 516104 | tf_op jit(solution)/shard_map/ppermute | solution.py:495
  6.9 1.1 %collective-permute-start.2 = (bf16[168,512]{1,0:T(8,128)(2,1)S(1)}, bf16[168,512]{1,0:T(8,128)(2,1)S(1)}, u32[]{:S(2)}, u32[]{:S(2)}) collective-permute-start(bf16[168,512]{1,0:T(8,128)(2,1)S(1)} %get-tuple-element.35), channel_id=1, source_target_pairs={{0,12},{4,8},{8,4},{12,0},{16,28},{20,24},{24,20},{28,16},{1,13},{... | collective-permute-start | bytes 516104 | tf_op jit(solution)/shard_map/ppermute | solution.py:495
  8.0 2.5 %collective-permute-start.7 = (bf16[88,512]{1,0:T(8,128)(2,1)S(1)}, bf16[88,512]{1,0:T(8,128)(2,1)S(1)}, u32[]{:S(2)}, u32[]{:S(2)}) collective-permute-start(bf16[88,512]{1,0:T(8,128)(2,1)S(1)} %get-tuple-element.43), channel_id=1, source_target_pairs={{0,24},{4,28},{8,16},{12,20},{16,8},{20,12},{24,0},{28,4},{1,25},{... | collective-permute-start | bytes 270344 | tf_op jit(solution)/shard_map/ppermute | solution.py:495
  10.5 3.0 %collective-permute-start.9 = (bf16[88,512]{1,0:T(8,128)(2,1)S(1)}, bf16[88,512]{1,0:T(8,128)(2,1)S(1)}, u32[]{:S(2)}, u32[]{:S(2)}) collective-permute-start(bf16[88,512]{1,0:T(8,128)(2,1)S(1)} %get-tuple-element.46), channel_id=1, source_target_pairs={{0,28},{4,24},{8,20},{12,16},{16,12},{20,8},{24,4},{28,0},{1,29},{... | collective-permute-start | bytes 270344 | tf_op jit(solution)/shard_map/ppermute | solution.py:495
  13.5 1.7 %collective-permute-done.7.refs_6_ = bf16[88,512]{1,0:T(8,128)(2,1)S(1)} collective-permute-done((bf16[88,512]{1,0:T(8,128)(2,1)S(1)}, bf16[88,512]{1,0:T(8,128)(2,1)S(1)}, u32[]{:S(2)}, u32[]{:S(2)}) %collective-permute-start.7) | collective-permute-done | bytes 90144 | tf_op jit(solution)/shard_map/ppermute | solution.py:495
  15.3 6.7 %collective-permute-done.9.refs_7_ = bf16[88,512]{1,0:T(8,128)(2,1)S(1)} collective-permute-done((bf16[88,512]{1,0:T(8,128)(2,1)S(1)}, bf16[88,512]{1,0:T(8,128)(2,1)S(1)}, u32[]{:S(2)}, u32[]{:S(2)}) %collective-permute-start.9) | collective-permute-done | bytes 90144 | tf_op jit(solution)/shard_map/ppermute | solution.py:495
  22.1 0.0 copy-start.2
  22.1 0.0 copy-start.4
  22.1 0.0 copy-start.6
  22.1 0.8 %collective-permute-start.11 = (bf16[8,48,512]{2,1,0:T(8,128)(2,1)S(1)}, bf16[8,48,512]{2,1,0:T(8,128)(2,1)S(1)}, u32[]{:S(2)}, u32[]{:S(2)}) collective-permute-start(bf16[8,48,512]{2,1,0:T(8,128)(2,1)S(1)} %shard_map.101), channel_id=1, source_target_pairs={{0,1},{1,0},{2,3},{3,2},{4,5},{5,4},{6,7},{7,6},{8,9},{9,8},{10,11... | collective-permute-start | bytes 1179656 | tf_op jit(solution)/shard_map/ppermute | solution.py:513
  23.0 1.3 %collective-permute-done.11.refs_8_ = bf16[8,48,512]{2,1,0:T(8,128)(2,1)S(1)} collective-permute-done((bf16[8,48,512]{2,1,0:T(8,128)(2,1)S(1)}, bf16[8,48,512]{2,1,0:T(8,128)(2,1)S(1)}, u32[]{:S(2)}, u32[]{:S(2)}) %collective-permute-start.11) | collective-permute-done | bytes 393248 | tf_op jit(solution)/shard_map/ppermute | solution.py:513
  24.3 3.4 %collective-permute-start.12 = (bf16[8,56,512]{2,1,0:T(8,128)(2,1)S(1)}, bf16[8,56,512]{2,1,0:T(8,128)(2,1)S(1)}, u32[]{:S(2)}, u32[]{:S(2)}) collective-permute-start(bf16[8,56,512]{2,1,0:T(8,128)(2,1)S(1)} %get-tuple-element.52), channel_id=1, source_target_pairs={{1,2},{2,1},{5,6},{6,5},{9,10},{10,9},{13,14},{14,13},{17,18},{18,... | collective-permute-start | bytes 1376264 | tf_op jit(solution)/shard_map/ppermute | solution.py:513
  27.8 0.7 %collective-permute-start.13 = (bf16[8,16,512]{2,1,0:T(8,128)(2,1)S(1)}, bf16[8,16,512]{2,1,0:T(8,128)(2,1)S(1)}, u32[]{:S(2)}, u32[]{:S(2)}) collective-permute-start(bf16[8,16,512]{2,1,0:T(8,128)(2,1)S(1)} %get-tuple-element.53), channel_id=1, source_target_pairs={{0,3},{3,0},{4,7},{7,4},{8,11},{11,8},{12,15},{15,12},{16,19},{19,... | collective-permute-start | bytes 393224 | tf_op jit(solution)/shard_map/ppermute | solution.py:513
  28.5 1.3 %shard_map.104.refs_14_ = bf16[16,512,256]{2,1,0:T(8,128)(2,1)S(1)} custom-call(bf16[9,512,256]{2,1,0:T(8,128)(2,1)S(1)} %bitcast.9), custom_call_target="tpu_custom_call" | custom-call | flops 2621440 | bytes 6553600 | tf_op jit(solution)/shard_map/pallas_call | solution.py:164
  29.7 1.2 %collective-permute-start.4 = (bf16[80,512]{1,0:T(8,128)(2,1)S(1)}, bf16[80,512]{1,0:T(8,128)(2,1)S(1)}, u32[]{:S(2)}, u32[]{:S(2)}) collective-permute-start(bf16[80,512]{1,0:T(8,128)(2,1)S(1)} %get-tuple-element.38), channel_id=1, source_target_pairs={{0,16},{4,20},{8,24},{12,28},{16,0},{20,4},{24,8},{28,12},{1,17},{... | collective-permute-start | bytes 245768 | tf_op jit(solution)/shard_map/ppermute | solution.py:495
  30.9 2.1 %collective-permute-start.6 = (bf16[80,512]{1,0:T(8,128)(2,1)S(1)}, bf16[80,512]{1,0:T(8,128)(2,1)S(1)}, u32[]{:S(2)}, u32[]{:S(2)}) collective-permute-start(bf16[80,512]{1,0:T(8,128)(2,1)S(1)} %get-tuple-element.41), channel_id=1, source_target_pairs={{0,20},{4,16},{8,28},{12,24},{16,4},{20,0},{24,12},{28,8},{1,21},{... | collective-permute-start | bytes 245768 | tf_op jit(solution)/shard_map/ppermute | solution.py:495
  33.1 1.1 %collective-permute-start.8 = (bf16[80,512]{1,0:T(8,128)(2,1)S(1)}, bf16[80,512]{1,0:T(8,128)(2,1)S(1)}, u32[]{:S(2)}, u32[]{:S(2)}) collective-permute-start(bf16[80,512]{1,0:T(8,128)(2,1)S(1)} %get-tuple-element.44), channel_id=1, source_target_pairs={{0,24},{4,28},{8,16},{12,20},{16,8},{20,12},{24,0},{28,4},{1,25},{... | collective-permute-start | bytes 245768 | tf_op jit(solution)/shard_map/ppermute | solution.py:495
  34.2 0.9 %collective-permute-start.10 = (bf16[80,512]{1,0:T(8,128)(2,1)S(1)}, bf16[80,512]{1,0:T(8,128)(2,1)S(1)}, u32[]{:S(2)}, u32[]{:S(2)}) collective-permute-start(bf16[80,512]{1,0:T(8,128)(2,1)S(1)} %get-tuple-element.47), channel_id=1, source_target_pairs={{0,28},{4,24},{8,20},{12,16},{16,12},{20,8},{24,4},{28,0},{1,29},{... | collective-permute-start | bytes 245768 | tf_op jit(solution)/shard_map/ppermute | solution.py:495
  35.1 0.4 collective-permute-done.12.refs_9_
  35.6 0.0 copy-start.3
  35.6 0.0 copy-start.8
  35.6 0.0 copy-start.9
  35.6 4.0 %shard_map.103 = (f32[2,8,512]{2,1,0:T(8,128)S(1)}, bf16[4,10,16,512]{3,2,1,0:T(8,128)(2,1)S(1)}, bf16[4,9,16,512]{3,2,1,0:T(8,128)(2,1)S(1)}, bf16[4,9,16,512]{...) custom-call(bf16[168,512]{1,0:T(8,128)(2,1)S(1)} %get-tuple-element.32.refs_0_, ...), custom_call_target="tpu_custom_call" | custom-call | flops 2717908992 | bytes 4718592 | tf_op jit(solution)/shard_map/pallas_call | solution.py:442
  39.7 1.3 %collective-permute-done.6.refs_5_ = bf16[80,512]{1,0:T(8,128)(2,1)S(1)} collective-permute-done((bf16[80,512]{1,0:T(8,128)(2,1)S(1)}, bf16[80,512]{1,0:T(8,128)(2,1)S(1)}, u32[]{:S(2)}, u32[]{:S(2)}) %collective-permute-start.6) | collective-permute-done | bytes 81952 | tf_op jit(solution)/shard_map/ppermute | solution.py:495
  40.9 4.7 %collective-permute-done.8.refs_6_ = bf16[80,512]{1,0:T(8,128)(2,1)S(1)} collective-permute-done((bf16[80,512]{1,0:T(8,128)(2,1)S(1)}, bf16[80,512]{1,0:T(8,128)(2,1)S(1)}, u32[]{:S(2)}, u32[]{:S(2)}) %collective-permute-start.8) | collective-permute-done | bytes 81952 | tf_op jit(solution)/shard_map/ppermute | solution.py:495
  45.6 2.7 %collective-permute-done.10.refs_7_ = bf16[80,512]{1,0:T(8,128)(2,1)S(1)} collective-permute-done((bf16[80,512]{1,0:T(8,128)(2,1)S(1)}, bf16[80,512]{1,0:T(8,128)(2,1)S(1)}, u32[]{:S(2)}, u32[]{:S(2)}) %collective-permute-start.10) | collective-permute-done | bytes 81952 | tf_op jit(solution)/shard_map/ppermute | solution.py:495
  48.3 13.9 %shard_map.105 = bf16[8,512,256]{2,1,0:T(8,128)(2,1)} custom-call(s32[8]{0:T(128)S(1)} %copy-done.9, bf16[168,512]{1,0:T(8,128)(2,1)S(1)} %get-tuple-element.32.refs_0_, bf16[168,512]{1,0:T(8,128)(2,1)S(1)} %collective-permute-done.refs_1_, bf16[168,512]{1,0:T(8,128)(2,1)S(1)} %collective-permute-done.1.refs_2_, ...), custom_call_target="tpu_custom_call" | custom-call | flops 8371830784 | bytes 8912896 | tf_op jit(solution)/shard_map/pallas_call | solution.py:462
  (22 shorter events, 0.1 us)
Async XLA Ops:
  0.0 28.4 %copy-start = (bf16[3,3,512,256]{3,2,1,0:T(8,128)(2,1)S(1)}, bf16[3,3,512,256]{3,2,1,0:T(8,128)(2,1)}, u32[]{:S(2)}) copy-start(bf16[3,3,512,256]{3,2,1,0:T(8,128)(2,1)} %param.15) | copy-start | bytes 7077892
  0.0 1.4 %copy-start.1 = (bf16[1,8,128,512]{3,2,1,0:T(8,128)(2,1)S(1)}, bf16[1,8,128,512]{3,2,1,0:T(8,128)(2,1)}, u32[]{:S(2)}) copy-start(bf16[1,8,128,512]{3,2,1,0:T(8,128)(2,1)} %param.10) | copy-start | bytes 3145732
  2.0 6.0 %collective-permute-start.3 = (bf16[88,512]{1,0:T(8,128)(2,1)S(1)}, bf16[88,512]{1,0:T(8,128)(2,1)S(1)}, u32[]{:S(2)}, u32[]{:S(2)}) collective-permute-start(bf16[88,512]{1,0:T(8,128)(2,1)S(1)} %get-tuple-element.37), channel_id=1, source_target_pairs={{0,16},{4,20},{8,24},{12,28},{16,0},{20,4},{24,8},{28,12},{1,17},{... | collective-permute-start | bytes 270344 | tf_op jit(solution)/shard_map/ppermute | solution.py:495
  2.1 8.4 %collective-permute-start.5 = (bf16[88,512]{1,0:T(8,128)(2,1)S(1)}, bf16[88,512]{1,0:T(8,128)(2,1)S(1)}, u32[]{:S(2)}, u32[]{:S(2)}) collective-permute-start(bf16[88,512]{1,0:T(8,128)(2,1)S(1)} %get-tuple-element.40), channel_id=1, source_target_pairs={{0,20},{4,16},{8,28},{12,24},{16,4},{20,0},{24,12},{28,8},{1,21},{... | collective-permute-start | bytes 270344 | tf_op jit(solution)/shard_map/ppermute | solution.py:495
  5.4 16.6 %collective-permute-start = (bf16[168,512]{1,0:T(8,128)(2,1)S(1)}, bf16[168,512]{1,0:T(8,128)(2,1)S(1)}, u32[]{:S(2)}, u32[]{:S(2)}) collective-permute-start(bf16[168,512]{1,0:T(8,128)(2,1)S(1)} %get-tuple-element.33), channel_id=1, source_target_pairs={{0,4},{4,0},{8,12},{12,8},{16,20},{20,16},{24,28},{28,24},{1,5},{5... | collective-permute-start | bytes 516104 | tf_op jit(solution)/shard_map/ppermute | solution.py:495
  5.6 16.4 %collective-permute-start.1 = (bf16[168,512]{1,0:T(8,128)(2,1)S(1)}, bf16[168,512]{1,0:T(8,128)(2,1)S(1)}, u32[]{:S(2)}, u32[]{:S(2)}) collective-permute-start(bf16[168,512]{1,0:T(8,128)(2,1)S(1)} %get-tuple-element.34), channel_id=1, source_target_pairs={{0,8},{4,12},{8,0},{12,4},{16,24},{20,28},{24,16},{28,20},{1,9},{5... | collective-permute-start | bytes 516104 | tf_op jit(solution)/shard_map/ppermute | solution.py:495
  6.9 15.1 %collective-permute-start.2 = (bf16[168,512]{1,0:T(8,128)(2,1)S(1)}, bf16[168,512]{1,0:T(8,128)(2,1)S(1)}, u32[]{:S(2)}, u32[]{:S(2)}) collective-permute-start(bf16[168,512]{1,0:T(8,128)(2,1)S(1)} %get-tuple-element.35), channel_id=1, source_target_pairs={{0,12},{4,8},{8,4},{12,0},{16,28},{20,24},{24,20},{28,16},{1,13},{... | collective-permute-start | bytes 516104 | tf_op jit(solution)/shard_map/ppermute | solution.py:495
  8.0 7.3 %collective-permute-start.7 = (bf16[88,512]{1,0:T(8,128)(2,1)S(1)}, bf16[88,512]{1,0:T(8,128)(2,1)S(1)}, u32[]{:S(2)}, u32[]{:S(2)}) collective-permute-start(bf16[88,512]{1,0:T(8,128)(2,1)S(1)} %get-tuple-element.43), channel_id=1, source_target_pairs={{0,24},{4,28},{8,16},{12,20},{16,8},{20,12},{24,0},{28,4},{1,25},{... | collective-permute-start | bytes 270344 | tf_op jit(solution)/shard_map/ppermute | solution.py:495
  10.5 11.5 %collective-permute-start.9 = (bf16[88,512]{1,0:T(8,128)(2,1)S(1)}, bf16[88,512]{1,0:T(8,128)(2,1)S(1)}, u32[]{:S(2)}, u32[]{:S(2)}) collective-permute-start(bf16[88,512]{1,0:T(8,128)(2,1)S(1)} %get-tuple-element.46), channel_id=1, source_target_pairs={{0,28},{4,24},{8,20},{12,16},{16,12},{20,8},{24,4},{28,0},{1,29},{... | collective-permute-start | bytes 270344 | tf_op jit(solution)/shard_map/ppermute | solution.py:495
  22.1 13.5 %copy-start.2 = (bf16[3,3,512,512]{3,2,1,0:T(8,128)(2,1)S(1)}, bf16[3,3,512,512]{3,2,1,0:T(8,128)(2,1)}, u32[]{:S(2)}) copy-start(bf16[3,3,512,512]{3,2,1,0:T(8,128)(2,1)} %refs_13_.3) | copy-start | bytes 14155780
  22.1 13.5 %copy-start.4 = (f32[512]{0:T(512)S(1)}, f32[512]{0:T(512)}, u32[]{:S(2)}) copy-start(f32[512]{0:T(512)} %param.11) | copy-start | bytes 6148
  22.1 13.5 %copy-start.5 = (f32[512]{0:T(512)S(1)}, f32[512]{0:T(512)}, u32[]{:S(2)}) copy-start(f32[512]{0:T(512)} %param.12) | copy-start | bytes 6148
  22.1 13.5 %copy-start.6 = (f32[512]{0:T(512)S(1)}, f32[512]{0:T(512)}, u32[]{:S(2)}) copy-start(f32[512]{0:T(512)} %param.14) | copy-start | bytes 6148
  22.1 2.2 %collective-permute-start.11 = (bf16[8,48,512]{2,1,0:T(8,128)(2,1)S(1)}, bf16[8,48,512]{2,1,0:T(8,128)(2,1)S(1)}, u32[]{:S(2)}, u32[]{:S(2)}) collective-permute-start(bf16[8,48,512]{2,1,0:T(8,128)(2,1)S(1)} %shard_map.101), channel_id=1, source_target_pairs={{0,1},{1,0},{2,3},{3,2},{4,5},{5,4},{6,7},{7,6},{8,9},{9,8},{10,11... | collective-permute-start | bytes 1179656 | tf_op jit(solution)/shard_map/ppermute | solution.py:513
  24.3 11.2 %collective-permute-start.12 = (bf16[8,56,512]{2,1,0:T(8,128)(2,1)S(1)}, bf16[8,56,512]{2,1,0:T(8,128)(2,1)S(1)}, u32[]{:S(2)}, u32[]{:S(2)}) collective-permute-start(bf16[8,56,512]{2,1,0:T(8,128)(2,1)S(1)} %get-tuple-element.52), channel_id=1, source_target_pairs={{1,2},{2,1},{5,6},{6,5},{9,10},{10,9},{13,14},{14,13},{17,18},{18,... | collective-permute-start | bytes 1376264 | tf_op jit(solution)/shard_map/ppermute | solution.py:513
  27.8 6.4 %collective-permute-start.13 = (bf16[8,16,512]{2,1,0:T(8,128)(2,1)S(1)}, bf16[8,16,512]{2,1,0:T(8,128)(2,1)S(1)}, u32[]{:S(2)}, u32[]{:S(2)}) collective-permute-start(bf16[8,16,512]{2,1,0:T(8,128)(2,1)S(1)} %get-tuple-element.53), channel_id=1, source_target_pairs={{0,3},{3,0},{4,7},{7,4},{8,11},{11,8},{12,15},{15,12},{16,19},{19,... | collective-permute-start | bytes 393224 | tf_op jit(solution)/shard_map/ppermute | solution.py:513
  29.7 9.9 %collective-permute-start.4 = (bf16[80,512]{1,0:T(8,128)(2,1)S(1)}, bf16[80,512]{1,0:T(8,128)(2,1)S(1)}, u32[]{:S(2)}, u32[]{:S(2)}) collective-permute-start(bf16[80,512]{1,0:T(8,128)(2,1)S(1)} %get-tuple-element.38), channel_id=1, source_target_pairs={{0,16},{4,20},{8,24},{12,28},{16,0},{20,4},{24,8},{28,12},{1,17},{... | collective-permute-start | bytes 245768 | tf_op jit(solution)/shard_map/ppermute | solution.py:495
  30.9 10.0 %collective-permute-start.6 = (bf16[80,512]{1,0:T(8,128)(2,1)S(1)}, bf16[80,512]{1,0:T(8,128)(2,1)S(1)}, u32[]{:S(2)}, u32[]{:S(2)}) collective-permute-start(bf16[80,512]{1,0:T(8,128)(2,1)S(1)} %get-tuple-element.41), channel_id=1, source_target_pairs={{0,20},{4,16},{8,28},{12,24},{16,4},{20,0},{24,12},{28,8},{1,21},{... | collective-permute-start | bytes 245768 | tf_op jit(solution)/shard_map/ppermute | solution.py:495
  33.1 12.5 %collective-permute-start.8 = (bf16[80,512]{1,0:T(8,128)(2,1)S(1)}, bf16[80,512]{1,0:T(8,128)(2,1)S(1)}, u32[]{:S(2)}, u32[]{:S(2)}) collective-permute-start(bf16[80,512]{1,0:T(8,128)(2,1)S(1)} %get-tuple-element.44), channel_id=1, source_target_pairs={{0,24},{4,28},{8,16},{12,20},{16,8},{20,12},{24,0},{28,4},{1,25},{... | collective-permute-start | bytes 245768 | tf_op jit(solution)/shard_map/ppermute | solution.py:495
  34.2 14.2 %collective-permute-start.10 = (bf16[80,512]{1,0:T(8,128)(2,1)S(1)}, bf16[80,512]{1,0:T(8,128)(2,1)S(1)}, u32[]{:S(2)}, u32[]{:S(2)}) collective-permute-start(bf16[80,512]{1,0:T(8,128)(2,1)S(1)} %get-tuple-element.47), channel_id=1, source_target_pairs={{0,28},{4,24},{8,20},{12,16},{16,12},{20,8},{24,4},{28,0},{1,29},{... | collective-permute-start | bytes 245768 | tf_op jit(solution)/shard_map/ppermute | solution.py:495
  35.6 12.8 %copy-start.3 = (bf16[3,256,256]{2,1,0:T(8,128)(2,1)S(1)}, bf16[3,256,256]{2,1,0:T(8,128)(2,1)}, u32[]{:S(2)}) copy-start(bf16[3,256,256]{2,1,0:T(8,128)(2,1)} %param.17) | copy-start | bytes 1179652
  35.6 12.7 %copy-start.7 = (f32[256]{0:T(256)S(1)}, f32[256]{0:T(256)}, u32[]{:S(2)}) copy-start(f32[256]{0:T(256)} %param.16) | copy-start | bytes 3076
  35.6 12.7 %copy-start.8 = (f32[256]{0:T(256)S(1)}, f32[256]{0:T(256)}, u32[]{:S(2)}) copy-start(f32[256]{0:T(256)} %param.18) | copy-start | bytes 3076
  35.6 12.7 %copy-start.9 = (s32[8]{0:T(128)S(1)}, s32[8]{0:T(128)}, u32[]{:S(2)}) copy-start(s32[8]{0:T(128)} %clip.1) | copy-start | bytes 100

commit v4 on v3

--- a/solution.py
+++ b/solution.py
@@ -179,7 +179,7 @@
     T = p.T
     odd = lax.bitwise_and(lax.axis_index("rows"), 1)
     to_above = odd == (0 if second else 1)
-    out = refs[-2] if second else refs[-1]
+    out = refs[-1]
 
     @pl.when(to_above)
     def _():
@@ -197,23 +197,20 @@
         if second:
             theirs = refs[n][f, T : T + 8]
             out[f, T + 8 : T + 16] = theirs
-            refs[-1][f, 0:8] = sums
-            refs[-1][f, 8:16] = theirs
 
 
 def face(p, got, first=None):
     vm = pl.BlockSpec(memory_space=pltpu.VMEM)
-    rows = [p.T + 8] if first is None else [p.T + 16, 16]
+    rows = p.T + (8 if first is None else 16)
     args = list(got) + ([] if first is None else [first])
-    out = pl.pallas_call(
+    return pl.pallas_call(
         functools.partial(face_kernel, p, len(got), first is not None),
-        out_shape=[jax.ShapeDtypeStruct((p.F, r, p.c1), BF16) for r in rows],
+        out_shape=jax.ShapeDtypeStruct((p.F, rows, p.c1), BF16),
         in_specs=[vm] * len(args),
-        out_specs=[vm] * len(rows),
+        out_specs=vm,
         compiler_params=pltpu.CompilerParams(vmem_limit_bytes=16 * 2**20),
         cost_estimate=pl.CostEstimate(flops=1, transcendentals=0, bytes_accessed=1),
     )(*args)
-    return out[0] if first is None else out
 
 
 def turner(p, first):
@@ -296,7 +293,7 @@
 
 def outer_kernel(p, n, *refs):
     outer, _ = messages(p, list(refs[:n]) + [None] * (p.peers - p.near))
-    (face1, face2, sums2, gain, shift, w1, b1,
+    (face1, face2, gain, shift, w1, b1,
      norm, heven, hodd, feven, fodd, cells, teven, todd) = refs[n:]
     F, R, CH, T, c1 = p.F, p.R, p.CH, p.T, p.c1
     me = lax.axis_index("frames")
@@ -306,8 +303,7 @@
     parts = jnp.concatenate(
         [outer[f][T : T + 8, :].astype(F32) for f in range(F)]
         + [face1[f, T : T + 8, :].astype(F32) for f in range(F)]
-        + [face2[f, at : at + 8, :].astype(F32) for at in (T, T + 8) for f in range(F)]
-        + [sums2[f, at : at + 8, :].astype(F32) for at in (0, 8) for f in range(F)],
+        + [face2[f, at : at + 8, :].astype(F32) for at in (T, T + 8) for f in range(F)],
         axis=0,
     ).astype(BF16)
     i = lax.broadcasted_iota(jnp.int32, (2 * F, parts.shape[0]), 0)
@@ -372,7 +368,7 @@
     _, inner = messages(p, list(refs[: p.near]) + [None] * (p.peers - p.near) + list(refs[p.near : n])
                         if p.swap else refs[:n])
     (norm, heven, hodd, feven_in, fodd_in, w1, w2, wt, b1, b2, bt, out,
-     cells, even, odd, feven, fodd, phase, second, act, start) = refs[n:]
+     cells, even, odd, feven, fodd, phase, second, act, done, start, sems) = refs[n:]
     F, R, C, CH, S, c1, c2 = p.F, p.R, p.C, p.CH, p.S, p.c1, p.c2
     me = lax.axis_index("frames")
     my_row = lax.axis_index("rows")
@@ -425,17 +421,25 @@
     def temporal(t, carry):
         taps = [act[jnp.maximum(t - k * DILATION, start[t])] for k in range(TAPS)]
         lhs = jnp.concatenate(taps, axis=-1)
-        out[t] = (dot(lhs, wt[...]) + second[t].astype(F32) + bt[...]).astype(BF16)
+        done[t] = (dot(lhs, wt[...]) + second[t].astype(F32) + bt[...]).astype(BF16)
+        pltpu.make_async_copy(done.at[t], out.at[t], sems.at[t]).start()
+        return carry
+
+    def finish(t, carry):
+        pltpu.make_async_copy(done.at[t], out.at[t], sems.at[t]).wait()
         return carry
 
     if F <= 8:
         for t in range(F):
             temporal(t, 0)
+        for t in range(F):
+            finish(t, 0)
     else:
         lax.fori_loop(0, F, temporal, 0)
-
-
-def outer_rows(p, got, face1, face2, sums2, gain, shift, w1, b1):
+        lax.fori_loop(0, F, finish, 0)
+
+
+def outer_rows(p, got, face1, face2, gain, shift, w1, b1):
     F, C, CH, G, S, c1 = p.F, p.C, p.CH, p.G, p.S, p.c1
     vm = pl.BlockSpec(memory_space=pltpu.VMEM)
     pairs = lambda rows, cells: [(rows, cells // G, S, c1), (rows, max(1, cells // G - 1), S, c1)]
@@ -443,7 +447,7 @@
         functools.partial(outer_kernel, p, len(got)),
         out_shape=[jax.ShapeDtypeStruct((2, F, c1), F32)]
         + [jax.ShapeDtypeStruct(s, BF16) for s in pairs(4, CH) + pairs(4, C + 2)],
-        in_specs=[vm] * (len(got) + 7),
+        in_specs=[vm] * (len(got) + 6),
         out_specs=[vm] * 5,
         scratch_shapes=[pltpu.VMEM((8, CH, F, c1), F32)] + [pltpu.VMEM(s, BF16) for s in pairs(4, CH)],
         compiler_params=pltpu.CompilerParams(vmem_limit_bytes=p.vmem),
@@ -451,7 +455,7 @@
             flops=2 * 9 * 4 * (C + 2) * F * c1 * c1, transcendentals=8 * CH * F * c1,
             bytes_accessed=2 * 9 * c1 * c1,
         ),
-    )(*got, face1, face2, sums2, gain, shift, w1, b1)
+    )(*got, face1, face2, gain, shift, w1, b1)
 
 
 def inner_rows(p, clip, got, norm, hidden, first, w1, w2, wt, b1, b2, bt):
@@ -463,14 +467,16 @@
         functools.partial(inner_kernel, p, len(got)),
         out_shape=jax.ShapeDtypeStruct((F, p.cells, c2), BF16),
         in_specs=[sm] + [vm] * (len(got) + 11),
-        out_specs=vm,
+        out_specs=pl.BlockSpec(memory_space=pl.ANY),
         scratch_shapes=[pltpu.VMEM((R - 4, CH, F, c1), F32)]
         + [pltpu.VMEM(s, BF16) for s in pairs(R - 4, CH) + pairs(R - 2, C + 2)]
         + [
             pltpu.VMEM((2, 2, R, C * F, c2), BF16),
             pltpu.VMEM((F, p.cells, c2), BF16),
             pltpu.VMEM((F, p.cells, c2), BF16),
+            pltpu.VMEM((F, p.cells, c2), BF16),
             pltpu.SMEM((F,), jnp.int32),
+            pltpu.SemaphoreType.DMA((F,)),
         ],
         compiler_params=pltpu.CompilerParams(vmem_limit_bytes=p.vmem),
         cost_estimate=pl.CostEstimate(
@@ -513,16 +519,17 @@
         return lax.ppermute(v, "rows", [(i, j) for a, b in pairs for i, j in ((a, b), (b, a))])
 
     assert row_peers == 4
-    face1 = over_rows(face(p, got), (0, 1), (2, 3))
-    face2, sums2 = face(p, got, face1)
-    face2, sums2 = over_rows(face2, (1, 2)), over_rows(sums2, (0, 3))
+    w2 = phase_weights(conv_two.reshape(9, c1, c2))
+    face1, w2 = lax.optimization_barrier((face(p, got), w2))
+    face1 = over_rows(face1, (0, 1), (2, 3))
+    face2 = over_rows(face(p, got, face1), (1, 2), (0, 3))
     w1 = conv_one_w.reshape(3, 3, c1, c1)
     norm, *packed = outer_rows(
-        p, got, face1, face2, sums2, norm_gain[None], norm_shift[None], w1, bias_one[None]
+        p, got, face1, face2, norm_gain[None], norm_shift[None], w1, bias_one[None]
     )
     out = inner_rows(
         p, clip_ids, last, norm, packed[:2], packed[2:], w1,
-        phase_weights(conv_two.reshape(9, c1, c2)), temporal_weight.reshape(TAPS * c2, c2),
+        w2, temporal_weight.reshape(TAPS * c2, c2),
         bias_one[None], bias_two[None], bias_temporal[None],
     )
     return out.reshape(p.F, 2 * height, 2 * p.C, c2)

time: 62.4 us -> 57.9 us (0.928)
  waiting for transfers between devices: 18.9 us -> 16 us
  starting transfers between devices: 21.8 us -> 19.2 us
  local copies, waits for them, and re-layouts: 1.43 us -> 2.93 us
    ppermute x11, waiting for transfers between devices: 17.1 us -> 8.89 us  [swap(): return lax.ppermute(v, 'frames', [(i, i ^ s) for i in range(peers)])]
    ppermute x3 -> x2, waiting for transfers between devices: 1.8 us -> 7.14 us  [over_rows(): lax.ppermute(v, 'rows', [(i, j) for a, b in pairs for i, j in ((a, b), (b...]
    ppermute x3 -> x2, starting transfers between devices: 4.93 us -> 2.42 us  [over_rows(): lax.ppermute(v, 'rows', [(i, j) for a, b in pairs for i, j in ((a, b), (b...]
    unnamed x20, local copies, waits for them, and re-layouts: 1.43 us -> 2.93 us
  transfers between devices with their start and end apart: 14 -> 13, of which waited for: 7 -> 5; matrix products, arithmetic and copies ran while one was open for 0% -> 0% of each run, Pallas kernels for 9% -> 9%
where the time goes in v4:
time: 57.9 us; the launch traced here: 57.7 us
  Pallas kernels  19.4 us (34%)
  starting transfers between devices  19.2 us (33%)
  waiting for transfers between devices  16 us (28%)
  local copies, waits for them, and re-layouts  2.93 us (5%)
    ppermute x11, starting transfers between devices, swap(): return lax.ppermute(v, 'frames', [(i, i ^ s) for i in range(peers)])  16.7 us
    pallas_call x1, Pallas kernels, inner_rows(): pl.pallas_call(functools.partial(inner_kernel, p, len(got)), out_shape=ja...  13.4 us
    ppermute x11, waiting for transfers between devices, swap(): return lax.ppermute(v, 'frames', [(i, i ^ s) for i in range(peers)])  8.89 us
    ppermute x2, waiting for transfers between devices, over_rows(): lax.ppermute(v, 'rows', [(i, j) for a, b in pairs for i, j in ((a, b), (b...  7.14 us
    pallas_call x1, Pallas kernels, outer_rows(): pl.pallas_call(functools.partial(outer_kernel, p, len(got)), out_shape=[j...  4.03 us
    unnamed x20, local copies, waits for them, and re-layouts  2.93 us
    ppermute x2, starting transfers between devices, over_rows(): lax.ppermute(v, 'rows', [(i, j) for a, b in pairs for i, j in ((a, b), (b...  2.42 us
    pallas_call x1, Pallas kernels, phase_weights(): pl.pallas_call(weights_kernel, grid=(c1 // step,), out_shape=jax.ShapeDty...  1.28 us
  transfers between devices with their start and end apart: 13, of which 5 were waited for; matrix products, arithmetic and copies ran while one was open for 0% of the time, Pallas kernels for 9%

profile of v4, /device:TPU:17, one launch (start us, length us, event | category | flops | bytes accessed | tf_op | source)
XLA Modules:
  0.0 57.7 jit_solution(9507653916922413488)
XLA Ops:
  0.0 1.2 %copy-done.1 = bf16[1,8,128,512]{3,2,1,0:T(8,128)(2,1)S(1)} copy-done((bf16[1,8,128,512]{3,2,1,0:T(8,128)(2,1)S(1)}, bf16[1,8,128,512]{3,2,1,0:T(8,128)(2,1)}, u32[]{:S(2)}) %copy-start.1) | copy-done | bytes 1048600
  1.2 0.6 %shard_map.100 = (bf16[168,512]{1,0:T(8,128)(2,1)S(1)}, bf16[168,512]{1,0:T(8,128)(2,1)S(1)}, bf16[168,512]{1,0:T(8,128)(2,1)S(1)}, bf16[168,512]{1,0:T(8,128)(2...) custom-call(bf16[8,128,512]{2,1,0:T(8,128)(2,1)S(1)} %bitcast.10), custom_call_target="tpu_custom_call" | custom-call | tf_op jit(solution)/shard_map/pallas_call | solution.py:138
  1.8 0.1 collective-permute-start.3
  1.9 3.3 %collective-permute-start.5 = (bf16[88,512]{1,0:T(8,128)(2,1)S(1)}, bf16[88,512]{1,0:T(8,128)(2,1)S(1)}, u32[]{:S(2)}, u32[]{:S(2)}) collective-permute-start(bf16[88,512]{1,0:T(8,128)(2,1)S(1)} %get-tuple-element.40), channel_id=1, source_target_pairs={{0,20},{4,16},{8,28},{12,24},{16,4},{20,0},{24,12},{28,8},{1,21},{... | collective-permute-start | bytes 270344 | tf_op jit(solution)/shard_map/ppermute | solution.py:501
  5.2 0.3 collective-permute-start
  5.5 1.3 %collective-permute-start.1 = (bf16[168,512]{1,0:T(8,128)(2,1)S(1)}, bf16[168,512]{1,0:T(8,128)(2,1)S(1)}, u32[]{:S(2)}, u32[]{:S(2)}) collective-permute-start(bf16[168,512]{1,0:T(8,128)(2,1)S(1)} %get-tuple-element.34), channel_id=1, source_target_pairs={{0,8},{4,12},{8,0},{12,4},{16,24},{20,28},{24,16},{28,20},{1,9},{5... | collective-permute-start | bytes 516104 | tf_op jit(solution)/shard_map/ppermute | solution.py:501
  6.8 1.1 %collective-permute-start.2 = (bf16[168,512]{1,0:T(8,128)(2,1)S(1)}, bf16[168,512]{1,0:T(8,128)(2,1)S(1)}, u32[]{:S(2)}, u32[]{:S(2)}) collective-permute-start(bf16[168,512]{1,0:T(8,128)(2,1)S(1)} %get-tuple-element.35), channel_id=1, source_target_pairs={{0,12},{4,8},{8,4},{12,0},{16,28},{20,24},{24,20},{28,16},{1,13},{... | collective-permute-start | bytes 516104 | tf_op jit(solution)/shard_map/ppermute | solution.py:501
  7.9 0.0 collective-permute-done.3.refs_4_
  7.9 2.5 %collective-permute-start.7 = (bf16[88,512]{1,0:T(8,128)(2,1)S(1)}, bf16[88,512]{1,0:T(8,128)(2,1)S(1)}, u32[]{:S(2)}, u32[]{:S(2)}) collective-permute-start(bf16[88,512]{1,0:T(8,128)(2,1)S(1)} %get-tuple-element.43), channel_id=1, source_target_pairs={{0,24},{4,28},{8,16},{12,20},{16,8},{20,12},{24,0},{28,4},{1,25},{... | collective-permute-start | bytes 270344 | tf_op jit(solution)/shard_map/ppermute | solution.py:501
  10.3 3.0 %collective-permute-start.9 = (bf16[88,512]{1,0:T(8,128)(2,1)S(1)}, bf16[88,512]{1,0:T(8,128)(2,1)S(1)}, u32[]{:S(2)}, u32[]{:S(2)}) collective-permute-start(bf16[88,512]{1,0:T(8,128)(2,1)S(1)} %get-tuple-element.46), channel_id=1, source_target_pairs={{0,28},{4,24},{8,20},{12,16},{16,12},{20,8},{24,4},{28,0},{1,29},{... | collective-permute-start | bytes 270344 | tf_op jit(solution)/shard_map/ppermute | solution.py:501
  13.4 1.7 %copy-done = bf16[3,3,512,256]{3,2,1,0:T(8,128)(2,1)S(1)} copy-done((bf16[3,3,512,256]{3,2,1,0:T(8,128)(2,1)S(1)}, bf16[3,3,512,256]{3,2,1,0:T(8,128)(2,1)}, u32[]{:S(2)}) %copy-start) | copy-done | bytes 2359320
  15.1 1.3 %shard_map.102.refs_14_ = bf16[16,512,256]{2,1,0:T(8,128)(2,1)S(1)} custom-call(bf16[9,512,256]{2,1,0:T(8,128)(2,1)S(1)} %bitcast.9), custom_call_target="tpu_custom_call" | custom-call | flops 2621440 | bytes 6553600 | tf_op jit(solution)/shard_map/pallas_call | solution.py:164
  16.3 0.0 collective-permute-done.7.refs_6_
  16.4 5.5 %collective-permute-done.9.refs_7_ = bf16[88,512]{1,0:T(8,128)(2,1)S(1)} collective-permute-done((bf16[88,512]{1,0:T(8,128)(2,1)S(1)}, bf16[88,512]{1,0:T(8,128)(2,1)S(1)}, u32[]{:S(2)}, u32[]{:S(2)}) %collective-permute-start.9) | collective-permute-done | bytes 90144 | tf_op jit(solution)/shard_map/ppermute | solution.py:501
  21.8 0.0 collective-permute-done.refs_1_
  21.8 0.0 collective-permute-done.1.refs_2_
  21.9 0.8 %collective-permute-start.11 = (bf16[8,48,512]{2,1,0:T(8,128)(2,1)S(1)}, bf16[8,48,512]{2,1,0:T(8,128)(2,1)S(1)}, u32[]{:S(2)}, u32[]{:S(2)}) collective-permute-start(bf16[8,48,512]{2,1,0:T(8,128)(2,1)S(1)} %shard_map.101), channel_id=1, source_target_pairs={{0,1},{1,0},{2,3},{3,2},{4,5},{5,4},{6,7},{7,6},{8,9},{9,8},{10,11... | collective-permute-start | bytes 1179656 | tf_op jit(solution)/shard_map/ppermute | solution.py:519
  22.8 1.3 %collective-permute-done.11.refs_8_ = bf16[8,48,512]{2,1,0:T(8,128)(2,1)S(1)} collective-permute-done((bf16[8,48,512]{2,1,0:T(8,128)(2,1)S(1)}, bf16[8,48,512]{2,1,0:T(8,128)(2,1)S(1)}, u32[]{:S(2)}, u32[]{:S(2)}) %collective-permute-start.11) | collective-permute-done | bytes 393248 | tf_op jit(solution)/shard_map/ppermute | solution.py:519
  24.1 1.6 %collective-permute-start.12 = (bf16[8,56,512]{2,1,0:T(8,128)(2,1)S(1)}, bf16[8,56,512]{2,1,0:T(8,128)(2,1)S(1)}, u32[]{:S(2)}, u32[]{:S(2)}) collective-permute-start(bf16[8,56,512]{2,1,0:T(8,128)(2,1)S(1)} %shard_map.103), channel_id=1, source_target_pairs={{1,2},{2,1},{0,3},{3,0},{5,6},{6,5},{4,7},{7,4},{9,10},{10,9},{8,1... | collective-permute-start | bytes 1376264 | tf_op jit(solution)/shard_map/ppermute | solution.py:519
  25.7 1.1 %collective-permute-start.4 = (bf16[80,512]{1,0:T(8,128)(2,1)S(1)}, bf16[80,512]{1,0:T(8,128)(2,1)S(1)}, u32[]{:S(2)}, u32[]{:S(2)}) collective-permute-start(bf16[80,512]{1,0:T(8,128)(2,1)S(1)} %get-tuple-element.38), channel_id=1, source_target_pairs={{0,16},{4,20},{8,24},{12,28},{16,0},{20,4},{24,8},{28,12},{1,17},{... | collective-permute-start | bytes 245768 | tf_op jit(solution)/shard_map/ppermute | solution.py:501
  26.9 2.1 %collective-permute-start.6 = (bf16[80,512]{1,0:T(8,128)(2,1)S(1)}, bf16[80,512]{1,0:T(8,128)(2,1)S(1)}, u32[]{:S(2)}, u32[]{:S(2)}) collective-permute-start(bf16[80,512]{1,0:T(8,128)(2,1)S(1)} %get-tuple-element.41), channel_id=1, source_target_pairs={{0,20},{4,16},{8,28},{12,24},{16,4},{20,0},{24,12},{28,8},{1,21},{... | collective-permute-start | bytes 245768 | tf_op jit(solution)/shard_map/ppermute | solution.py:501
  29.0 1.0 %collective-permute-start.8 = (bf16[80,512]{1,0:T(8,128)(2,1)S(1)}, bf16[80,512]{1,0:T(8,128)(2,1)S(1)}, u32[]{:S(2)}, u32[]{:S(2)}) collective-permute-start(bf16[80,512]{1,0:T(8,128)(2,1)S(1)} %get-tuple-element.44), channel_id=1, source_target_pairs={{0,24},{4,28},{8,16},{12,20},{16,8},{20,12},{24,0},{28,4},{1,25},{... | collective-permute-start | bytes 245768 | tf_op jit(solution)/shard_map/ppermute | solution.py:501
  30.0 0.9 %collective-permute-start.10 = (bf16[80,512]{1,0:T(8,128)(2,1)S(1)}, bf16[80,512]{1,0:T(8,128)(2,1)S(1)}, u32[]{:S(2)}, u32[]{:S(2)}) collective-permute-start(bf16[80,512]{1,0:T(8,128)(2,1)S(1)} %get-tuple-element.47), channel_id=1, source_target_pairs={{0,28},{4,24},{8,20},{12,16},{16,12},{20,8},{24,4},{28,0},{1,29},{... | collective-permute-start | bytes 245768 | tf_op jit(solution)/shard_map/ppermute | solution.py:501
  30.9 5.8 %collective-permute-done.12.refs_9_ = bf16[8,56,512]{2,1,0:T(8,128)(2,1)S(1)} collective-permute-done((bf16[8,56,512]{2,1,0:T(8,128)(2,1)S(1)}, bf16[8,56,512]{2,1,0:T(8,128)(2,1)S(1)}, u32[]{:S(2)}, u32[]{:S(2)}) %collective-permute-start.12) | collective-permute-done | bytes 458784 | tf_op jit(solution)/shard_map/ppermute | solution.py:519
  36.7 0.0 copy-start.3
  36.7 0.0 copy-start.7
  36.8 0.0 copy-start.8
  36.8 0.0 copy-start.9
  36.8 4.0 %shard_map.104 = (f32[2,8,512]{2,1,0:T(8,128)S(1)}, bf16[4,10,16,512]{3,2,1,0:T(8,128)(2,1)S(1)}, bf16[4,9,16,512]{3,2,1,0:T(8,128)(2,1)S(1)}, bf16[4,9,16,512]{...) custom-call(bf16[168,512]{1,0:T(8,128)(2,1)S(1)} %get-tuple-element.32.refs_0_, ...), custom_call_target="tpu_custom_call" | custom-call | flops 2717908992 | bytes 4718592 | tf_op jit(solution)/shard_map/pallas_call | solution.py:446
  40.8 0.7 %collective-permute-done.8.refs_6_ = bf16[80,512]{1,0:T(8,128)(2,1)S(1)} collective-permute-done((bf16[80,512]{1,0:T(8,128)(2,1)S(1)}, bf16[80,512]{1,0:T(8,128)(2,1)S(1)}, u32[]{:S(2)}, u32[]{:S(2)}) %collective-permute-start.8) | collective-permute-done | bytes 81952 | tf_op jit(solution)/shard_map/ppermute | solution.py:501
  41.5 2.7 %collective-permute-done.10.refs_7_ = bf16[80,512]{1,0:T(8,128)(2,1)S(1)} collective-permute-done((bf16[80,512]{1,0:T(8,128)(2,1)S(1)}, bf16[80,512]{1,0:T(8,128)(2,1)S(1)}, u32[]{:S(2)}, u32[]{:S(2)}) %collective-permute-start.10) | collective-permute-done | bytes 81952 | tf_op jit(solution)/shard_map/ppermute | solution.py:501
  44.2 13.4 %shard_map.105 = bf16[8,512,256]{2,1,0:T(8,128)(2,1)} custom-call(s32[8]{0:T(128)S(1)} %copy-done.9, bf16[168,512]{1,0:T(8,128)(2,1)S(1)} %get-tuple-element.32.refs_0_, bf16[168,512]{1,0:T(8,128)(2,1)S(1)} %collective-permute-done.refs_1_, bf16[168,512]{1,0:T(8,128)(2,1)S(1)} %collective-permute-done.1.refs_2_, ...), custom_call_target="tpu_custom_call" | custom-call | flops 8371830784 | bytes 8912896 | tf_op jit(solution)/shard_map/pallas_call | solution.py:466
  (20 shorter events, 0.1 us)
Async XLA Ops:
  0.0 1.2 %copy-start.1 = (bf16[1,8,128,512]{3,2,1,0:T(8,128)(2,1)S(1)}, bf16[1,8,128,512]{3,2,1,0:T(8,128)(2,1)}, u32[]{:S(2)}) copy-start(bf16[1,8,128,512]{3,2,1,0:T(8,128)(2,1)} %param.10) | copy-start | bytes 3145732
  1.8 6.0 %collective-permute-start.3 = (bf16[88,512]{1,0:T(8,128)(2,1)S(1)}, bf16[88,512]{1,0:T(8,128)(2,1)S(1)}, u32[]{:S(2)}, u32[]{:S(2)}) collective-permute-start(bf16[88,512]{1,0:T(8,128)(2,1)S(1)} %get-tuple-element.37), channel_id=1, source_target_pairs={{0,16},{4,20},{8,24},{12,28},{16,0},{20,4},{24,8},{28,12},{1,17},{... | collective-permute-start | bytes 270344 | tf_op jit(solution)/shard_map/ppermute | solution.py:501
  1.9 8.4 %collective-permute-start.5 = (bf16[88,512]{1,0:T(8,128)(2,1)S(1)}, bf16[88,512]{1,0:T(8,128)(2,1)S(1)}, u32[]{:S(2)}, u32[]{:S(2)}) collective-permute-start(bf16[88,512]{1,0:T(8,128)(2,1)S(1)} %get-tuple-element.40), channel_id=1, source_target_pairs={{0,20},{4,16},{8,28},{12,24},{16,4},{20,0},{24,12},{28,8},{1,21},{... | collective-permute-start | bytes 270344 | tf_op jit(solution)/shard_map/ppermute | solution.py:501
  5.2 16.6 %collective-permute-start = (bf16[168,512]{1,0:T(8,128)(2,1)S(1)}, bf16[168,512]{1,0:T(8,128)(2,1)S(1)}, u32[]{:S(2)}, u32[]{:S(2)}) collective-permute-start(bf16[168,512]{1,0:T(8,128)(2,1)S(1)} %get-tuple-element.33), channel_id=1, source_target_pairs={{0,4},{4,0},{8,12},{12,8},{16,20},{20,16},{24,28},{28,24},{1,5},{5... | collective-permute-start | bytes 516104 | tf_op jit(solution)/shard_map/ppermute | solution.py:501
  5.5 16.4 %collective-permute-start.1 = (bf16[168,512]{1,0:T(8,128)(2,1)S(1)}, bf16[168,512]{1,0:T(8,128)(2,1)S(1)}, u32[]{:S(2)}, u32[]{:S(2)}) collective-permute-start(bf16[168,512]{1,0:T(8,128)(2,1)S(1)} %get-tuple-element.34), channel_id=1, source_target_pairs={{0,8},{4,12},{8,0},{12,4},{16,24},{20,28},{24,16},{28,20},{1,9},{5... | collective-permute-start | bytes 516104 | tf_op jit(solution)/shard_map/ppermute | solution.py:501
  6.8 15.1 %collective-permute-start.2 = (bf16[168,512]{1,0:T(8,128)(2,1)S(1)}, bf16[168,512]{1,0:T(8,128)(2,1)S(1)}, u32[]{:S(2)}, u32[]{:S(2)}) collective-permute-start(bf16[168,512]{1,0:T(8,128)(2,1)S(1)} %get-tuple-element.35), channel_id=1, source_target_pairs={{0,12},{4,8},{8,4},{12,0},{16,28},{20,24},{24,20},{28,16},{1,13},{... | collective-permute-start | bytes 516104 | tf_op jit(solution)/shard_map/ppermute | solution.py:501
  7.9 8.5 %collective-permute-start.7 = (bf16[88,512]{1,0:T(8,128)(2,1)S(1)}, bf16[88,512]{1,0:T(8,128)(2,1)S(1)}, u32[]{:S(2)}, u32[]{:S(2)}) collective-permute-start(bf16[88,512]{1,0:T(8,128)(2,1)S(1)} %get-tuple-element.43), channel_id=1, source_target_pairs={{0,24},{4,28},{8,16},{12,20},{16,8},{20,12},{24,0},{28,4},{1,25},{... | collective-permute-start | bytes 270344 | tf_op jit(solution)/shard_map/ppermute | solution.py:501
  10.3 11.5 %collective-permute-start.9 = (bf16[88,512]{1,0:T(8,128)(2,1)S(1)}, bf16[88,512]{1,0:T(8,128)(2,1)S(1)}, u32[]{:S(2)}, u32[]{:S(2)}) collective-permute-start(bf16[88,512]{1,0:T(8,128)(2,1)S(1)} %get-tuple-element.46), channel_id=1, source_target_pairs={{0,28},{4,24},{8,20},{12,16},{16,12},{20,8},{24,4},{28,0},{1,29},{... | collective-permute-start | bytes 270344 | tf_op jit(solution)/shard_map/ppermute | solution.py:501
  13.4 1.7 %copy-start = (bf16[3,3,512,256]{3,2,1,0:T(8,128)(2,1)S(1)}, bf16[3,3,512,256]{3,2,1,0:T(8,128)(2,1)}, u32[]{:S(2)}) copy-start(bf16[3,3,512,256]{3,2,1,0:T(8,128)(2,1)} %param.15) | copy-start | bytes 7077892
  15.1 21.7 %copy-start.2 = (bf16[3,3,512,512]{3,2,1,0:T(8,128)(2,1)S(1)}, bf16[3,3,512,512]{3,2,1,0:T(8,128)(2,1)}, u32[]{:S(2)}) copy-start(bf16[3,3,512,512]{3,2,1,0:T(8,128)(2,1)} %refs_13_.1) | copy-start | bytes 14155780
  15.1 21.7 %copy-start.4 = (f32[512]{0:T(512)S(1)}, f32[512]{0:T(512)}, u32[]{:S(2)}) copy-start(f32[512]{0:T(512)} %param.11) | copy-start | bytes 6148
  15.1 21.7 %copy-start.5 = (f32[512]{0:T(512)S(1)}, f32[512]{0:T(512)}, u32[]{:S(2)}) copy-start(f32[512]{0:T(512)} %param.12) | copy-start | bytes 6148
  15.1 21.7 %copy-start.6 = (f32[512]{0:T(512)S(1)}, f32[512]{0:T(512)}, u32[]{:S(2)}) copy-start(f32[512]{0:T(512)} %param.14) | copy-start | bytes 6148
  21.9 2.2 %collective-permute-start.11 = (bf16[8,48,512]{2,1,0:T(8,128)(2,1)S(1)}, bf16[8,48,512]{2,1,0:T(8,128)(2,1)S(1)}, u32[]{:S(2)}, u32[]{:S(2)}) collective-permute-start(bf16[8,48,512]{2,1,0:T(8,128)(2,1)S(1)} %shard_map.101), channel_id=1, source_target_pairs={{0,1},{1,0},{2,3},{3,2},{4,5},{5,4},{6,7},{7,6},{8,9},{9,8},{10,11... | collective-permute-start | bytes 1179656 | tf_op jit(solution)/shard_map/ppermute | solution.py:519
  24.1 12.6 %collective-permute-start.12 = (bf16[8,56,512]{2,1,0:T(8,128)(2,1)S(1)}, bf16[8,56,512]{2,1,0:T(8,128)(2,1)S(1)}, u32[]{:S(2)}, u32[]{:S(2)}) collective-permute-start(bf16[8,56,512]{2,1,0:T(8,128)(2,1)S(1)} %shard_map.103), channel_id=1, source_target_pairs={{1,2},{2,1},{0,3},{3,0},{5,6},{6,5},{4,7},{7,4},{9,10},{10,9},{8,1... | collective-permute-start | bytes 1376264 | tf_op jit(solution)/shard_map/ppermute | solution.py:519
  25.7 15.1 %collective-permute-start.4 = (bf16[80,512]{1,0:T(8,128)(2,1)S(1)}, bf16[80,512]{1,0:T(8,128)(2,1)S(1)}, u32[]{:S(2)}, u32[]{:S(2)}) collective-permute-start(bf16[80,512]{1,0:T(8,128)(2,1)S(1)} %get-tuple-element.38), channel_id=1, source_target_pairs={{0,16},{4,20},{8,24},{12,28},{16,0},{20,4},{24,8},{28,12},{1,17},{... | collective-permute-start | bytes 245768 | tf_op jit(solution)/shard_map/ppermute | solution.py:501
  26.9 14.0 %collective-permute-start.6 = (bf16[80,512]{1,0:T(8,128)(2,1)S(1)}, bf16[80,512]{1,0:T(8,128)(2,1)S(1)}, u32[]{:S(2)}, u32[]{:S(2)}) collective-permute-start(bf16[80,512]{1,0:T(8,128)(2,1)S(1)} %get-tuple-element.41), channel_id=1, source_target_pairs={{0,20},{4,16},{8,28},{12,24},{16,4},{20,0},{24,12},{28,8},{1,21},{... | collective-permute-start | bytes 245768 | tf_op jit(solution)/shard_map/ppermute | solution.py:501
  29.0 12.5 %collective-permute-start.8 = (bf16[80,512]{1,0:T(8,128)(2,1)S(1)}, bf16[80,512]{1,0:T(8,128)(2,1)S(1)}, u32[]{:S(2)}, u32[]{:S(2)}) collective-permute-start(bf16[80,512]{1,0:T(8,128)(2,1)S(1)} %get-tuple-element.44), channel_id=1, source_target_pairs={{0,24},{4,28},{8,16},{12,20},{16,8},{20,12},{24,0},{28,4},{1,25},{... | collective-permute-start | bytes 245768 | tf_op jit(solution)/shard_map/ppermute | solution.py:501
  30.0 14.2 %collective-permute-start.10 = (bf16[80,512]{1,0:T(8,128)(2,1)S(1)}, bf16[80,512]{1,0:T(8,128)(2,1)S(1)}, u32[]{:S(2)}, u32[]{:S(2)}) collective-permute-start(bf16[80,512]{1,0:T(8,128)(2,1)S(1)} %get-tuple-element.47), channel_id=1, source_target_pairs={{0,28},{4,24},{8,20},{12,16},{16,12},{20,8},{24,4},{28,0},{1,29},{... | collective-permute-start | bytes 245768 | tf_op jit(solution)/shard_map/ppermute | solution.py:501
  36.7 7.5 %copy-start.3 = (bf16[3,256,256]{2,1,0:T(8,128)(2,1)S(1)}, bf16[3,256,256]{2,1,0:T(8,128)(2,1)}, u32[]{:S(2)}) copy-start(bf16[3,256,256]{2,1,0:T(8,128)(2,1)} %param.17) | copy-start | bytes 1179652
  36.7 7.5 %copy-start.7 = (f32[256]{0:T(256)S(1)}, f32[256]{0:T(256)}, u32[]{:S(2)}) copy-start(f32[256]{0:T(256)} %param.16) | copy-start | bytes 3076
  36.8 7.5 %copy-start.8 = (f32[256]{0:T(256)S(1)}, f32[256]{0:T(256)}, u32[]{:S(2)}) copy-start(f32[256]{0:T(256)} %param.18) | copy-start | bytes 3076
  36.8 7.5 %copy-start.9 = (s32[8]{0:T(128)S(1)}, s32[8]{0:T(128)}, u32[]{:S(2)}) copy-start(s32[8]{0:T(128)} %clip.1) | copy-start | bytes 100

commit v5 on v4

--- a/solution.py
+++ b/solution.py
@@ -71,6 +71,15 @@
     )
 
 
+def in_three(total, square):
+    parts = []
+    for s in (total, square):
+        high = s.astype(BF16).astype(F32)
+        middle = (s - high).astype(BF16).astype(F32)
+        parts += [high, middle, s - high - middle]
+    return jnp.concatenate(parts + [jnp.zeros((2, s.shape[1]), F32)], axis=0).astype(BF16)
+
+
 def pack_kernel(p, lat, *refs):
     R, C, W, CH, T = p.R, p.C, p.W, p.CH, p.T
     outer, inner = messages(p, refs)
@@ -101,12 +110,7 @@
         x = lat[r].astype(F32)
         total = total + jnp.sum(x, axis=0, keepdims=True)
         square = square + jnp.sum(x * x, axis=0, keepdims=True)
-    parts = []
-    for s in (total, square):
-        high = s.astype(BF16).astype(F32)
-        middle = (s - high).astype(BF16).astype(F32)
-        parts += [high, middle, s - high - middle]
-    parts = jnp.concatenate(parts + [jnp.zeros((2, p.c1), F32)], axis=0).astype(BF16)
+    parts = in_three(total, square)
     me = lax.axis_index("frames")
     for s in range(p.peers):
         a, b = outer[s], inner[s]
@@ -193,15 +197,17 @@
 
     for f in range(p.F):
         sums = outer[f][T : T + 8, :]
+        if second:
+            both = sums.astype(F32) + refs[n][f, T : T + 8].astype(F32)
+            sums = in_three(
+                both[0:1] + both[1:2] + both[2:3], both[3:4] + both[4:5] + both[5:6]
+            )
         out[f, T : T + 8] = sums
-        if second:
-            theirs = refs[n][f, T : T + 8]
-            out[f, T + 8 : T + 16] = theirs
 
 
 def face(p, got, first=None):
     vm = pl.BlockSpec(memory_space=pltpu.VMEM)
-    rows = p.T + (8 if first is None else 16)
+    rows = p.T + 8
     args = list(got) + ([] if first is None else [first])
     return pl.pallas_call(
         functools.partial(face_kernel, p, len(got), first is not None),
@@ -303,7 +309,7 @@
     parts = jnp.concatenate(
         [outer[f][T : T + 8, :].astype(F32) for f in range(F)]
         + [face1[f, T : T + 8, :].astype(F32) for f in range(F)]
-        + [face2[f, at : at + 8, :].astype(F32) for at in (T, T + 8) for f in range(F)],
+        + [face2[f, T : T + 8, :].astype(F32) for f in range(F)],
         axis=0,
     ).astype(BF16)
     i = lax.broadcasted_iota(jnp.int32, (2 * F, parts.shape[0]), 0)

time: 57.9 us -> 57.9 us (level)
    ppermute x11, waiting for transfers between devices: 8.89 us -> 10.3 us  [swap(): return lax.ppermute(v, 'frames', [(i, i ^ s) for i in range(peers)])]
    ppermute x2, waiting for transfers between devices: 7.14 us -> 5.73 us  [over_rows(): lax.ppermute(v, 'rows', [(i, j) for a, b in pairs for i, j in ((a, b), (b...]
where the time goes in v5:
time: 57.9 us; the launch traced here: 57.8 us
  Pallas kernels  19.5 us (34%)
  starting transfers between devices  19.2 us (33%)
  waiting for transfers between devices  16 us (28%)
  local copies, waits for them, and re-layouts  2.93 us (5%)
    ppermute x11, starting transfers between devices, swap(): return lax.ppermute(v, 'frames', [(i, i ^ s) for i in range(peers)])  16.7 us
    pallas_call x1, Pallas kernels, inner_rows(): pl.pallas_call(functools.partial(inner_kernel, p, len(got)), out_shape=ja...  13.4 us
    ppermute x11, waiting for transfers between devices, swap(): return lax.ppermute(v, 'frames', [(i, i ^ s) for i in range(peers)])  10.3 us
    ppermute x2, waiting for transfers between devices, over_rows(): lax.ppermute(v, 'rows', [(i, j) for a, b in pairs for i, j in ((a, b), (b...  5.73 us
    pallas_call x1, Pallas kernels, outer_rows(): pl.pallas_call(functools.partial(outer_kernel, p, len(got)), out_shape=[j...  4.01 us
    unnamed x20, local copies, waits for them, and re-layouts  2.93 us
    ppermute x2, starting transfers between devices, over_rows(): lax.ppermute(v, 'rows', [(i, j) for a, b in pairs for i, j in ((a, b), (b...  2.42 us
    pallas_call x1, Pallas kernels, phase_weights(): pl.pallas_call(weights_kernel, grid=(c1 // step,), out_shape=jax.ShapeDty...  1.28 us
  transfers between devices with their start and end apart: 13, of which 5 were waited for; matrix products, arithmetic and copies ran while one was open for 0% of the time, Pallas kernels for 9%

profile of v5, /device:TPU:17, one launch (start us, length us, event | category | flops | bytes accessed | tf_op | source)
XLA Modules:
  0.0 57.8 jit_solution(16312547192096367487)
XLA Ops:
  0.0 1.2 %copy-done.1 = bf16[1,8,128,512]{3,2,1,0:T(8,128)(2,1)S(1)} copy-done((bf16[1,8,128,512]{3,2,1,0:T(8,128)(2,1)S(1)}, bf16[1,8,128,512]{3,2,1,0:T(8,128)(2,1)}, u32[]{:S(2)}) %copy-start.1) | copy-done | bytes 1048600
  1.2 0.6 %shard_map.100 = (bf16[168,512]{1,0:T(8,128)(2,1)S(1)}, bf16[168,512]{1,0:T(8,128)(2,1)S(1)}, bf16[168,512]{1,0:T(8,128)(2,1)S(1)}, bf16[168,512]{1,0:T(8,128)(2...) custom-call(bf16[8,128,512]{2,1,0:T(8,128)(2,1)S(1)} %bitcast.10), custom_call_target="tpu_custom_call" | custom-call | tf_op jit(solution)/shard_map/pallas_call | solution.py:142
  1.8 0.1 collective-permute-start.3
  1.9 3.3 %collective-permute-start.5 = (bf16[88,512]{1,0:T(8,128)(2,1)S(1)}, bf16[88,512]{1,0:T(8,128)(2,1)S(1)}, u32[]{:S(2)}, u32[]{:S(2)}) collective-permute-start(bf16[88,512]{1,0:T(8,128)(2,1)S(1)} %get-tuple-element.40), channel_id=1, source_target_pairs={{0,20},{4,16},{8,28},{12,24},{16,4},{20,0},{24,12},{28,8},{1,21},{... | collective-permute-start | bytes 270344 | tf_op jit(solution)/shard_map/ppermute | solution.py:507
  5.2 0.3 collective-permute-start
  5.5 1.3 %collective-permute-start.1 = (bf16[168,512]{1,0:T(8,128)(2,1)S(1)}, bf16[168,512]{1,0:T(8,128)(2,1)S(1)}, u32[]{:S(2)}, u32[]{:S(2)}) collective-permute-start(bf16[168,512]{1,0:T(8,128)(2,1)S(1)} %get-tuple-element.34), channel_id=1, source_target_pairs={{0,8},{4,12},{8,0},{12,4},{16,24},{20,28},{24,16},{28,20},{1,9},{5... | collective-permute-start | bytes 516104 | tf_op jit(solution)/shard_map/ppermute | solution.py:507
  6.8 1.1 %collective-permute-start.2 = (bf16[168,512]{1,0:T(8,128)(2,1)S(1)}, bf16[168,512]{1,0:T(8,128)(2,1)S(1)}, u32[]{:S(2)}, u32[]{:S(2)}) collective-permute-start(bf16[168,512]{1,0:T(8,128)(2,1)S(1)} %get-tuple-element.35), channel_id=1, source_target_pairs={{0,12},{4,8},{8,4},{12,0},{16,28},{20,24},{24,20},{28,16},{1,13},{... | collective-permute-start | bytes 516104 | tf_op jit(solution)/shard_map/ppermute | solution.py:507
  7.9 0.0 collective-permute-done.3.refs_4_
  7.9 2.5 %collective-permute-start.7 = (bf16[88,512]{1,0:T(8,128)(2,1)S(1)}, bf16[88,512]{1,0:T(8,128)(2,1)S(1)}, u32[]{:S(2)}, u32[]{:S(2)}) collective-permute-start(bf16[88,512]{1,0:T(8,128)(2,1)S(1)} %get-tuple-element.43), channel_id=1, source_target_pairs={{0,24},{4,28},{8,16},{12,20},{16,8},{20,12},{24,0},{28,4},{1,25},{... | collective-permute-start | bytes 270344 | tf_op jit(solution)/shard_map/ppermute | solution.py:507
  10.3 0.0 collective-permute-done.5.refs_5_
  10.3 3.0 %collective-permute-start.9 = (bf16[88,512]{1,0:T(8,128)(2,1)S(1)}, bf16[88,512]{1,0:T(8,128)(2,1)S(1)}, u32[]{:S(2)}, u32[]{:S(2)}) collective-permute-start(bf16[88,512]{1,0:T(8,128)(2,1)S(1)} %get-tuple-element.46), channel_id=1, source_target_pairs={{0,28},{4,24},{8,20},{12,16},{16,12},{20,8},{24,4},{28,0},{1,29},{... | collective-permute-start | bytes 270344 | tf_op jit(solution)/shard_map/ppermute | solution.py:507
  13.4 1.7 %copy-done = bf16[3,3,512,256]{3,2,1,0:T(8,128)(2,1)S(1)} copy-done((bf16[3,3,512,256]{3,2,1,0:T(8,128)(2,1)S(1)}, bf16[3,3,512,256]{3,2,1,0:T(8,128)(2,1)}, u32[]{:S(2)}) %copy-start) | copy-done | bytes 2359320
  15.1 1.3 %shard_map.102.refs_14_ = bf16[16,512,256]{2,1,0:T(8,128)(2,1)S(1)} custom-call(bf16[9,512,256]{2,1,0:T(8,128)(2,1)S(1)} %bitcast.9), custom_call_target="tpu_custom_call" | custom-call | flops 2621440 | bytes 6553600 | tf_op jit(solution)/shard_map/pallas_call | solution.py:168
  16.4 5.5 %collective-permute-done.9.refs_7_ = bf16[88,512]{1,0:T(8,128)(2,1)S(1)} collective-permute-done((bf16[88,512]{1,0:T(8,128)(2,1)S(1)}, bf16[88,512]{1,0:T(8,128)(2,1)S(1)}, u32[]{:S(2)}, u32[]{:S(2)}) %collective-permute-start.9) | collective-permute-done | bytes 90144 | tf_op jit(solution)/shard_map/ppermute | solution.py:507
  21.8 0.0 collective-permute-done.refs_1_
  21.9 0.8 %collective-permute-start.11 = (bf16[8,48,512]{2,1,0:T(8,128)(2,1)S(1)}, bf16[8,48,512]{2,1,0:T(8,128)(2,1)S(1)}, u32[]{:S(2)}, u32[]{:S(2)}) collective-permute-start(bf16[8,48,512]{2,1,0:T(8,128)(2,1)S(1)} %shard_map.101), channel_id=1, source_target_pairs={{0,1},{1,0},{2,3},{3,2},{4,5},{5,4},{6,7},{7,6},{8,9},{9,8},{10,11... | collective-permute-start | bytes 1179656 | tf_op jit(solution)/shard_map/ppermute | solution.py:525
  22.8 1.3 %collective-permute-done.11.refs_8_ = bf16[8,48,512]{2,1,0:T(8,128)(2,1)S(1)} collective-permute-done((bf16[8,48,512]{2,1,0:T(8,128)(2,1)S(1)}, bf16[8,48,512]{2,1,0:T(8,128)(2,1)S(1)}, u32[]{:S(2)}, u32[]{:S(2)}) %collective-permute-start.11) | collective-permute-done | bytes 393248 | tf_op jit(solution)/shard_map/ppermute | solution.py:525
  24.1 0.1 shard_map.103
  24.2 1.6 %collective-permute-start.12 = (bf16[8,48,512]{2,1,0:T(8,128)(2,1)S(1)}, bf16[8,48,512]{2,1,0:T(8,128)(2,1)S(1)}, u32[]{:S(2)}, u32[]{:S(2)}) collective-permute-start(bf16[8,48,512]{2,1,0:T(8,128)(2,1)S(1)} %shard_map.103), channel_id=1, source_target_pairs={{1,2},{2,1},{0,3},{3,0},{5,6},{6,5},{4,7},{7,4},{9,10},{10,9},{8,1... | collective-permute-start | bytes 1179656 | tf_op jit(solution)/shard_map/ppermute | solution.py:525
  25.8 1.1 %collective-permute-start.4 = (bf16[80,512]{1,0:T(8,128)(2,1)S(1)}, bf16[80,512]{1,0:T(8,128)(2,1)S(1)}, u32[]{:S(2)}, u32[]{:S(2)}) collective-permute-start(bf16[80,512]{1,0:T(8,128)(2,1)S(1)} %get-tuple-element.38), channel_id=1, source_target_pairs={{0,16},{4,20},{8,24},{12,28},{16,0},{20,4},{24,8},{28,12},{1,17},{... | collective-permute-start | bytes 245768 | tf_op jit(solution)/shard_map/ppermute | solution.py:507
  26.9 2.1 %collective-permute-start.6 = (bf16[80,512]{1,0:T(8,128)(2,1)S(1)}, bf16[80,512]{1,0:T(8,128)(2,1)S(1)}, u32[]{:S(2)}, u32[]{:S(2)}) collective-permute-start(bf16[80,512]{1,0:T(8,128)(2,1)S(1)} %get-tuple-element.41), channel_id=1, source_target_pairs={{0,20},{4,16},{8,28},{12,24},{16,4},{20,0},{24,12},{28,8},{1,21},{... | collective-permute-start | bytes 245768 | tf_op jit(solution)/shard_map/ppermute | solution.py:507
  29.1 1.0 %collective-permute-start.8 = (bf16[80,512]{1,0:T(8,128)(2,1)S(1)}, bf16[80,512]{1,0:T(8,128)(2,1)S(1)}, u32[]{:S(2)}, u32[]{:S(2)}) collective-permute-start(bf16[80,512]{1,0:T(8,128)(2,1)S(1)} %get-tuple-element.44), channel_id=1, source_target_pairs={{0,24},{4,28},{8,16},{12,20},{16,8},{20,12},{24,0},{28,4},{1,25},{... | collective-permute-start | bytes 245768 | tf_op jit(solution)/shard_map/ppermute | solution.py:507
  30.1 0.9 %collective-permute-start.10 = (bf16[80,512]{1,0:T(8,128)(2,1)S(1)}, bf16[80,512]{1,0:T(8,128)(2,1)S(1)}, u32[]{:S(2)}, u32[]{:S(2)}) collective-permute-start(bf16[80,512]{1,0:T(8,128)(2,1)S(1)} %get-tuple-element.47), channel_id=1, source_target_pairs={{0,28},{4,24},{8,20},{12,16},{16,12},{20,8},{24,4},{28,0},{1,29},{... | collective-permute-start | bytes 245768 | tf_op jit(solution)/shard_map/ppermute | solution.py:507
  31.0 4.4 %collective-permute-done.12.refs_9_ = bf16[8,48,512]{2,1,0:T(8,128)(2,1)S(1)} collective-permute-done((bf16[8,48,512]{2,1,0:T(8,128)(2,1)S(1)}, bf16[8,48,512]{2,1,0:T(8,128)(2,1)S(1)}, u32[]{:S(2)}, u32[]{:S(2)}) %collective-permute-start.12) | collective-permute-done | bytes 393248 | tf_op jit(solution)/shard_map/ppermute | solution.py:525
  35.4 0.0 copy-start.3
  35.4 0.0 copy-start.7
  35.4 0.0 copy-start.8
  35.5 0.0 copy-start.9
  35.5 4.0 %shard_map.104 = (f32[2,8,512]{2,1,0:T(8,128)S(1)}, bf16[4,10,16,512]{3,2,1,0:T(8,128)(2,1)S(1)}, bf16[4,9,16,512]{3,2,1,0:T(8,128)(2,1)S(1)}, bf16[4,9,16,512]{...) custom-call(bf16[168,512]{1,0:T(8,128)(2,1)S(1)} %get-tuple-element.32.refs_0_, ...), custom_call_target="tpu_custom_call" | custom-call | flops 2717908992 | bytes 4718592 | tf_op jit(solution)/shard_map/pallas_call | solution.py:452
  39.5 2.1 %collective-permute-done.8.refs_6_ = bf16[80,512]{1,0:T(8,128)(2,1)S(1)} collective-permute-done((bf16[80,512]{1,0:T(8,128)(2,1)S(1)}, bf16[80,512]{1,0:T(8,128)(2,1)S(1)}, u32[]{:S(2)}, u32[]{:S(2)}) %collective-permute-start.8) | collective-permute-done | bytes 81952 | tf_op jit(solution)/shard_map/ppermute | solution.py:507
  41.6 2.7 %collective-permute-done.10.refs_7_ = bf16[80,512]{1,0:T(8,128)(2,1)S(1)} collective-permute-done((bf16[80,512]{1,0:T(8,128)(2,1)S(1)}, bf16[80,512]{1,0:T(8,128)(2,1)S(1)}, u32[]{:S(2)}, u32[]{:S(2)}) %collective-permute-start.10) | collective-permute-done | bytes 81952 | tf_op jit(solution)/shard_map/ppermute | solution.py:507
  44.3 13.4 %shard_map.105 = bf16[8,512,256]{2,1,0:T(8,128)(2,1)} custom-call(s32[8]{0:T(128)S(1)} %copy-done.9, bf16[168,512]{1,0:T(8,128)(2,1)S(1)} %get-tuple-element.32.refs_0_, bf16[168,512]{1,0:T(8,128)(2,1)S(1)} %collective-permute-done.refs_1_, bf16[168,512]{1,0:T(8,128)(2,1)S(1)} %collective-permute-done.1.refs_2_, ...), custom_call_target="tpu_custom_call" | custom-call | flops 8371830784 | bytes 8912896 | tf_op jit(solution)/shard_map/pallas_call | solution.py:472
  (20 shorter events, 0.1 us)
Async XLA Ops:
  0.0 1.2 %copy-start.1 = (bf16[1,8,128,512]{3,2,1,0:T(8,128)(2,1)S(1)}, bf16[1,8,128,512]{3,2,1,0:T(8,128)(2,1)}, u32[]{:S(2)}) copy-start(bf16[1,8,128,512]{3,2,1,0:T(8,128)(2,1)} %param.10) | copy-start | bytes 3145732
  1.8 6.0 %collective-permute-start.3 = (bf16[88,512]{1,0:T(8,128)(2,1)S(1)}, bf16[88,512]{1,0:T(8,128)(2,1)S(1)}, u32[]{:S(2)}, u32[]{:S(2)}) collective-permute-start(bf16[88,512]{1,0:T(8,128)(2,1)S(1)} %get-tuple-element.37), channel_id=1, source_target_pairs={{0,16},{4,20},{8,24},{12,28},{16,0},{20,4},{24,8},{28,12},{1,17},{... | collective-permute-start | bytes 270344 | tf_op jit(solution)/shard_map/ppermute | solution.py:507
  1.9 8.4 %collective-permute-start.5 = (bf16[88,512]{1,0:T(8,128)(2,1)S(1)}, bf16[88,512]{1,0:T(8,128)(2,1)S(1)}, u32[]{:S(2)}, u32[]{:S(2)}) collective-permute-start(bf16[88,512]{1,0:T(8,128)(2,1)S(1)} %get-tuple-element.40), channel_id=1, source_target_pairs={{0,20},{4,16},{8,28},{12,24},{16,4},{20,0},{24,12},{28,8},{1,21},{... | collective-permute-start | bytes 270344 | tf_op jit(solution)/shard_map/ppermute | solution.py:507
  5.2 16.6 %collective-permute-start = (bf16[168,512]{1,0:T(8,128)(2,1)S(1)}, bf16[168,512]{1,0:T(8,128)(2,1)S(1)}, u32[]{:S(2)}, u32[]{:S(2)}) collective-permute-start(bf16[168,512]{1,0:T(8,128)(2,1)S(1)} %get-tuple-element.33), channel_id=1, source_target_pairs={{0,4},{4,0},{8,12},{12,8},{16,20},{20,16},{24,28},{28,24},{1,5},{5... | collective-permute-start | bytes 516104 | tf_op jit(solution)/shard_map/ppermute | solution.py:507
  5.5 16.4 %collective-permute-start.1 = (bf16[168,512]{1,0:T(8,128)(2,1)S(1)}, bf16[168,512]{1,0:T(8,128)(2,1)S(1)}, u32[]{:S(2)}, u32[]{:S(2)}) collective-permute-start(bf16[168,512]{1,0:T(8,128)(2,1)S(1)} %get-tuple-element.34), channel_id=1, source_target_pairs={{0,8},{4,12},{8,0},{12,4},{16,24},{20,28},{24,16},{28,20},{1,9},{5... | collective-permute-start | bytes 516104 | tf_op jit(solution)/shard_map/ppermute | solution.py:507
  6.8 15.1 %collective-permute-start.2 = (bf16[168,512]{1,0:T(8,128)(2,1)S(1)}, bf16[168,512]{1,0:T(8,128)(2,1)S(1)}, u32[]{:S(2)}, u32[]{:S(2)}) collective-permute-start(bf16[168,512]{1,0:T(8,128)(2,1)S(1)} %get-tuple-element.35), channel_id=1, source_target_pairs={{0,12},{4,8},{8,4},{12,0},{16,28},{20,24},{24,20},{28,16},{1,13},{... | collective-permute-start | bytes 516104 | tf_op jit(solution)/shard_map/ppermute | solution.py:507
  7.9 8.5 %collective-permute-start.7 = (bf16[88,512]{1,0:T(8,128)(2,1)S(1)}, bf16[88,512]{1,0:T(8,128)(2,1)S(1)}, u32[]{:S(2)}, u32[]{:S(2)}) collective-permute-start(bf16[88,512]{1,0:T(8,128)(2,1)S(1)} %get-tuple-element.43), channel_id=1, source_target_pairs={{0,24},{4,28},{8,16},{12,20},{16,8},{20,12},{24,0},{28,4},{1,25},{... | collective-permute-start | bytes 270344 | tf_op jit(solution)/shard_map/ppermute | solution.py:507
  10.3 11.5 %collective-permute-start.9 = (bf16[88,512]{1,0:T(8,128)(2,1)S(1)}, bf16[88,512]{1,0:T(8,128)(2,1)S(1)}, u32[]{:S(2)}, u32[]{:S(2)}) collective-permute-start(bf16[88,512]{1,0:T(8,128)(2,1)S(1)} %get-tuple-element.46), channel_id=1, source_target_pairs={{0,28},{4,24},{8,20},{12,16},{16,12},{20,8},{24,4},{28,0},{1,29},{... | collective-permute-start | bytes 270344 | tf_op jit(solution)/shard_map/ppermute | solution.py:507
  13.4 1.7 %copy-start = (bf16[3,3,512,256]{3,2,1,0:T(8,128)(2,1)S(1)}, bf16[3,3,512,256]{3,2,1,0:T(8,128)(2,1)}, u32[]{:S(2)}) copy-start(bf16[3,3,512,256]{3,2,1,0:T(8,128)(2,1)} %param.15) | copy-start | bytes 7077892
  15.1 20.3 %copy-start.2 = (bf16[3,3,512,512]{3,2,1,0:T(8,128)(2,1)S(1)}, bf16[3,3,512,512]{3,2,1,0:T(8,128)(2,1)}, u32[]{:S(2)}) copy-start(bf16[3,3,512,512]{3,2,1,0:T(8,128)(2,1)} %refs_13_.1) | copy-start | bytes 14155780
  15.1 20.3 %copy-start.4 = (f32[512]{0:T(512)S(1)}, f32[512]{0:T(512)}, u32[]{:S(2)}) copy-start(f32[512]{0:T(512)} %param.11) | copy-start | bytes 6148
  15.1 20.3 %copy-start.5 = (f32[512]{0:T(512)S(1)}, f32[512]{0:T(512)}, u32[]{:S(2)}) copy-start(f32[512]{0:T(512)} %param.12) | copy-start | bytes 6148
  15.1 20.4 %copy-start.6 = (f32[512]{0:T(512)S(1)}, f32[512]{0:T(512)}, u32[]{:S(2)}) copy-start(f32[512]{0:T(512)} %param.14) | copy-start | bytes 6148
  21.9 2.2 %collective-permute-start.11 = (bf16[8,48,512]{2,1,0:T(8,128)(2,1)S(1)}, bf16[8,48,512]{2,1,0:T(8,128)(2,1)S(1)}, u32[]{:S(2)}, u32[]{:S(2)}) collective-permute-start(bf16[8,48,512]{2,1,0:T(8,128)(2,1)S(1)} %shard_map.101), channel_id=1, source_target_pairs={{0,1},{1,0},{2,3},{3,2},{4,5},{5,4},{6,7},{7,6},{8,9},{9,8},{10,11... | collective-permute-start | bytes 1179656 | tf_op jit(solution)/shard_map/ppermute | solution.py:525
  24.2 11.2 %collective-permute-start.12 = (bf16[8,48,512]{2,1,0:T(8,128)(2,1)S(1)}, bf16[8,48,512]{2,1,0:T(8,128)(2,1)S(1)}, u32[]{:S(2)}, u32[]{:S(2)}) collective-permute-start(bf16[8,48,512]{2,1,0:T(8,128)(2,1)S(1)} %shard_map.103), channel_id=1, source_target_pairs={{1,2},{2,1},{0,3},{3,0},{5,6},{6,5},{4,7},{7,4},{9,10},{10,9},{8,1... | collective-permute-start | bytes 1179656 | tf_op jit(solution)/shard_map/ppermute | solution.py:525
  25.8 13.7 %collective-permute-start.4 = (bf16[80,512]{1,0:T(8,128)(2,1)S(1)}, bf16[80,512]{1,0:T(8,128)(2,1)S(1)}, u32[]{:S(2)}, u32[]{:S(2)}) collective-permute-start(bf16[80,512]{1,0:T(8,128)(2,1)S(1)} %get-tuple-element.38), channel_id=1, source_target_pairs={{0,16},{4,20},{8,24},{12,28},{16,0},{20,4},{24,8},{28,12},{1,17},{... | collective-permute-start | bytes 245768 | tf_op jit(solution)/shard_map/ppermute | solution.py:507
  26.9 12.6 %collective-permute-start.6 = (bf16[80,512]{1,0:T(8,128)(2,1)S(1)}, bf16[80,512]{1,0:T(8,128)(2,1)S(1)}, u32[]{:S(2)}, u32[]{:S(2)}) collective-permute-start(bf16[80,512]{1,0:T(8,128)(2,1)S(1)} %get-tuple-element.41), channel_id=1, source_target_pairs={{0,20},{4,16},{8,28},{12,24},{16,4},{20,0},{24,12},{28,8},{1,21},{... | collective-permute-start | bytes 245768 | tf_op jit(solution)/shard_map/ppermute | solution.py:507
  29.1 12.5 %collective-permute-start.8 = (bf16[80,512]{1,0:T(8,128)(2,1)S(1)}, bf16[80,512]{1,0:T(8,128)(2,1)S(1)}, u32[]{:S(2)}, u32[]{:S(2)}) collective-permute-start(bf16[80,512]{1,0:T(8,128)(2,1)S(1)} %get-tuple-element.44), channel_id=1, source_target_pairs={{0,24},{4,28},{8,16},{12,20},{16,8},{20,12},{24,0},{28,4},{1,25},{... | collective-permute-start | bytes 245768 | tf_op jit(solution)/shard_map/ppermute | solution.py:507
  30.1 14.2 %collective-permute-start.10 = (bf16[80,512]{1,0:T(8,128)(2,1)S(1)}, bf16[80,512]{1,0:T(8,128)(2,1)S(1)}, u32[]{:S(2)}, u32[]{:S(2)}) collective-permute-start(bf16[80,512]{1,0:T(8,128)(2,1)S(1)} %get-tuple-element.47), channel_id=1, source_target_pairs={{0,28},{4,24},{8,20},{12,16},{16,12},{20,8},{24,4},{28,0},{1,29},{... | collective-permute-start | bytes 245768 | tf_op jit(solution)/shard_map/ppermute | solution.py:507
  35.4 8.9 %copy-start.3 = (bf16[3,256,256]{2,1,0:T(8,128)(2,1)S(1)}, bf16[3,256,256]{2,1,0:T(8,128)(2,1)}, u32[]{:S(2)}) copy-start(bf16[3,256,256]{2,1,0:T(8,128)(2,1)} %param.17) | copy-start | bytes 1179652
  35.4 8.9 %copy-start.7 = (f32[256]{0:T(256)S(1)}, f32[256]{0:T(256)}, u32[]{:S(2)}) copy-start(f32[256]{0:T(256)} %param.16) | copy-start | bytes 3076
  35.4 8.9 %copy-start.8 = (f32[256]{0:T(256)S(1)}, f32[256]{0:T(256)}, u32[]{:S(2)}) copy-start(f32[256]{0:T(256)} %param.18) | copy-start | bytes 3076
  35.5 8.9 %copy-start.9 = (s32[8]{0:T(128)S(1)}, s32[8]{0:T(128)}, u32[]{:S(2)}) copy-start(s32[8]{0:T(128)} %clip.1) | copy-start | bytes 100

commit v6 on v4

--- a/solution.py
+++ b/solution.py
@@ -387,6 +387,19 @@
     conv_one(p, list(range(2, R)), hidden, w1, b1, me, my_row, inside)
     first.update(inside)
 
+    q = p.q
+    n = q * 2 * C
+    i = lax.broadcasted_iota(jnp.int32, (n * F, n * F), 0)
+    j = lax.broadcasted_iota(jnp.int32, (n * F, n * F), 1)
+    source_cell = div(j, 2 * C * F) * (2 * C) + 2 * mod(div(j, F), C) + mod(div(j, C * F), 2)
+    back = jnp.where((div(i, n) == mod(j, F)) & (mod(i, n) == source_cell), 1.0, 0.0).astype(BF16)
+    def to_frames(blk):
+        rows = range(blk * q, blk * q + q)
+        x = jnp.concatenate([phase[o % 2, b, o // 2] for o in rows for b in range(2)], axis=0)
+        turned = dot(back, x)
+        second[:, blk * n : blk * n + n, :] = turned.astype(BF16).reshape(F, n, c2)
+        act[:, blk * n : blk * n + n, :] = silu(turned).astype(BF16).reshape(F, n, c2)
+
     for a in range(2):
         for b in range(2):
             acc = None
@@ -396,19 +409,12 @@
                     u = dot(lhs, w2[((a * 2 + b) * 2 + da) * 2 + db])
                     acc = u if acc is None else acc + u
             phase[a, b] = (acc + b2[...]).astype(BF16).reshape(R, C * F, c2)
-
-    q = p.q
-    n = q * 2 * C
-    i = lax.broadcasted_iota(jnp.int32, (n * F, n * F), 0)
-    j = lax.broadcasted_iota(jnp.int32, (n * F, n * F), 1)
-    source_cell = div(j, 2 * C * F) * (2 * C) + 2 * mod(div(j, F), C) + mod(div(j, C * F), 2)
-    back = jnp.where((div(i, n) == mod(j, F)) & (mod(i, n) == source_cell), 1.0, 0.0).astype(BF16)
-    for blk in range(2 * R // q):
-        rows = range(blk * q, blk * q + q)
-        x = jnp.concatenate([phase[o % 2, b, o // 2] for o in rows for b in range(2)], axis=0)
-        turned = dot(back, x)
-        second[:, blk * n : blk * n + n, :] = turned.astype(BF16).reshape(F, n, c2)
-        act[:, blk * n : blk * n + n, :] = silu(turned).astype(BF16).reshape(F, n, c2)
+        if q == 1:
+            for o in range(a, 2 * R, 2):
+                to_frames(o)
+    if q > 1:
+        for blk in range(2 * R // q):
+            to_frames(blk)
 
     start[0] = 0
 

time: 57.9 us -> 58.1 us (level)
  no operation moved by 1% of the time
where the time goes in v6:
time: 58.1 us; the launch traced here: 57.9 us
  Pallas kernels  19.5 us (34%)
  starting transfers between devices  19.2 us (33%)
  waiting for transfers between devices  16 us (28%)
  local copies, waits for them, and re-layouts  2.93 us (5%)
    ppermute x11, starting transfers between devices, swap(): return lax.ppermute(v, 'frames', [(i, i ^ s) for i in range(peers)])  16.7 us
    pallas_call x1, Pallas kernels, inner_rows(): pl.pallas_call(functools.partial(inner_kernel, p, len(got)), out_shape=ja...  13.5 us
    ppermute x11, waiting for transfers between devices, swap(): return lax.ppermute(v, 'frames', [(i, i ^ s) for i in range(peers)])  8.89 us
    ppermute x2, waiting for transfers between devices, over_rows(): lax.ppermute(v, 'rows', [(i, j) for a, b in pairs for i, j in ((a, b), (b...  7.14 us
    pallas_call x1, Pallas kernels, outer_rows(): pl.pallas_call(functools.partial(outer_kernel, p, len(got)), out_shape=[j...  4.03 us
    unnamed x20, local copies, waits for them, and re-layouts  2.93 us
    ppermute x2, starting transfers between devices, over_rows(): lax.ppermute(v, 'rows', [(i, j) for a, b in pairs for i, j in ((a, b), (b...  2.42 us
    pallas_call x1, Pallas kernels, phase_weights(): pl.pallas_call(weights_kernel, grid=(c1 // step,), out_shape=jax.ShapeDty...  1.28 us
  transfers between devices with their start and end apart: 13, of which 5 were waited for; matrix products, arithmetic and copies ran while one was open for 0% of the time, Pallas kernels for 9%

profile of v6, /device:TPU:17, one launch (start us, length us, event | category | flops | bytes accessed | tf_op | source)
XLA Modules:
  0.0 57.9 jit_solution(17584060825070031439)
XLA Ops:
  0.0 1.2 %copy-done.1 = bf16[1,8,128,512]{3,2,1,0:T(8,128)(2,1)S(1)} copy-done((bf16[1,8,128,512]{3,2,1,0:T(8,128)(2,1)S(1)}, bf16[1,8,128,512]{3,2,1,0:T(8,128)(2,1)}, u32[]{:S(2)}) %copy-start.1) | copy-done | bytes 1048600
  1.2 0.6 %shard_map.100 = (bf16[168,512]{1,0:T(8,128)(2,1)S(1)}, bf16[168,512]{1,0:T(8,128)(2,1)S(1)}, bf16[168,512]{1,0:T(8,128)(2,1)S(1)}, bf16[168,512]{1,0:T(8,128)(2...) custom-call(bf16[8,128,512]{2,1,0:T(8,128)(2,1)S(1)} %bitcast.10), custom_call_target="tpu_custom_call" | custom-call | tf_op jit(solution)/shard_map/pallas_call | solution.py:138
  1.8 0.1 collective-permute-start.3
  1.9 3.3 %collective-permute-start.5 = (bf16[88,512]{1,0:T(8,128)(2,1)S(1)}, bf16[88,512]{1,0:T(8,128)(2,1)S(1)}, u32[]{:S(2)}, u32[]{:S(2)}) collective-permute-start(bf16[88,512]{1,0:T(8,128)(2,1)S(1)} %get-tuple-element.40), channel_id=1, source_target_pairs={{0,20},{4,16},{8,28},{12,24},{16,4},{20,0},{24,12},{28,8},{1,21},{... | collective-permute-start | bytes 270344 | tf_op jit(solution)/shard_map/ppermute | solution.py:507
  5.2 0.3 collective-permute-start
  5.5 1.3 %collective-permute-start.1 = (bf16[168,512]{1,0:T(8,128)(2,1)S(1)}, bf16[168,512]{1,0:T(8,128)(2,1)S(1)}, u32[]{:S(2)}, u32[]{:S(2)}) collective-permute-start(bf16[168,512]{1,0:T(8,128)(2,1)S(1)} %get-tuple-element.34), channel_id=1, source_target_pairs={{0,8},{4,12},{8,0},{12,4},{16,24},{20,28},{24,16},{28,20},{1,9},{5... | collective-permute-start | bytes 516104 | tf_op jit(solution)/shard_map/ppermute | solution.py:507
  6.8 1.1 %collective-permute-start.2 = (bf16[168,512]{1,0:T(8,128)(2,1)S(1)}, bf16[168,512]{1,0:T(8,128)(2,1)S(1)}, u32[]{:S(2)}, u32[]{:S(2)}) collective-permute-start(bf16[168,512]{1,0:T(8,128)(2,1)S(1)} %get-tuple-element.35), channel_id=1, source_target_pairs={{0,12},{4,8},{8,4},{12,0},{16,28},{20,24},{24,20},{28,16},{1,13},{... | collective-permute-start | bytes 516104 | tf_op jit(solution)/shard_map/ppermute | solution.py:507
  7.9 0.0 collective-permute-done.3.refs_4_
  7.9 2.5 %collective-permute-start.7 = (bf16[88,512]{1,0:T(8,128)(2,1)S(1)}, bf16[88,512]{1,0:T(8,128)(2,1)S(1)}, u32[]{:S(2)}, u32[]{:S(2)}) collective-permute-start(bf16[88,512]{1,0:T(8,128)(2,1)S(1)} %get-tuple-element.43), channel_id=1, source_target_pairs={{0,24},{4,28},{8,16},{12,20},{16,8},{20,12},{24,0},{28,4},{1,25},{... | collective-permute-start | bytes 270344 | tf_op jit(solution)/shard_map/ppermute | solution.py:507
  10.3 0.0 collective-permute-done.5.refs_5_
  10.3 3.0 %collective-permute-start.9 = (bf16[88,512]{1,0:T(8,128)(2,1)S(1)}, bf16[88,512]{1,0:T(8,128)(2,1)S(1)}, u32[]{:S(2)}, u32[]{:S(2)}) collective-permute-start(bf16[88,512]{1,0:T(8,128)(2,1)S(1)} %get-tuple-element.46), channel_id=1, source_target_pairs={{0,28},{4,24},{8,20},{12,16},{16,12},{20,8},{24,4},{28,0},{1,29},{... | collective-permute-start | bytes 270344 | tf_op jit(solution)/shard_map/ppermute | solution.py:507
  13.4 1.7 %copy-done = bf16[3,3,512,256]{3,2,1,0:T(8,128)(2,1)S(1)} copy-done((bf16[3,3,512,256]{3,2,1,0:T(8,128)(2,1)S(1)}, bf16[3,3,512,256]{3,2,1,0:T(8,128)(2,1)}, u32[]{:S(2)}) %copy-start) | copy-done | bytes 2359320
  15.1 1.3 %shard_map.102.refs_14_ = bf16[16,512,256]{2,1,0:T(8,128)(2,1)S(1)} custom-call(bf16[9,512,256]{2,1,0:T(8,128)(2,1)S(1)} %bitcast.9), custom_call_target="tpu_custom_call" | custom-call | flops 2621440 | bytes 6553600 | tf_op jit(solution)/shard_map/pallas_call | solution.py:164
  16.3 0.0 collective-permute-done.7.refs_6_
  16.4 5.5 %collective-permute-done.9.refs_7_ = bf16[88,512]{1,0:T(8,128)(2,1)S(1)} collective-permute-done((bf16[88,512]{1,0:T(8,128)(2,1)S(1)}, bf16[88,512]{1,0:T(8,128)(2,1)S(1)}, u32[]{:S(2)}, u32[]{:S(2)}) %collective-permute-start.9) | collective-permute-done | bytes 90144 | tf_op jit(solution)/shard_map/ppermute | solution.py:507
  21.9 0.8 %collective-permute-start.11 = (bf16[8,48,512]{2,1,0:T(8,128)(2,1)S(1)}, bf16[8,48,512]{2,1,0:T(8,128)(2,1)S(1)}, u32[]{:S(2)}, u32[]{:S(2)}) collective-permute-start(bf16[8,48,512]{2,1,0:T(8,128)(2,1)S(1)} %shard_map.101), channel_id=1, source_target_pairs={{0,1},{1,0},{2,3},{3,2},{4,5},{5,4},{6,7},{7,6},{8,9},{9,8},{10,11... | collective-permute-start | bytes 1179656 | tf_op jit(solution)/shard_map/ppermute | solution.py:525
  22.8 1.3 %collective-permute-done.11.refs_8_ = bf16[8,48,512]{2,1,0:T(8,128)(2,1)S(1)} collective-permute-done((bf16[8,48,512]{2,1,0:T(8,128)(2,1)S(1)}, bf16[8,48,512]{2,1,0:T(8,128)(2,1)S(1)}, u32[]{:S(2)}, u32[]{:S(2)}) %collective-permute-start.11) | collective-permute-done | bytes 393248 | tf_op jit(solution)/shard_map/ppermute | solution.py:525
  24.1 1.6 %collective-permute-start.12 = (bf16[8,56,512]{2,1,0:T(8,128)(2,1)S(1)}, bf16[8,56,512]{2,1,0:T(8,128)(2,1)S(1)}, u32[]{:S(2)}, u32[]{:S(2)}) collective-permute-start(bf16[8,56,512]{2,1,0:T(8,128)(2,1)S(1)} %shard_map.103), channel_id=1, source_target_pairs={{1,2},{2,1},{0,3},{3,0},{5,6},{6,5},{4,7},{7,4},{9,10},{10,9},{8,1... | collective-permute-start | bytes 1376264 | tf_op jit(solution)/shard_map/ppermute | solution.py:525
  25.7 1.1 %collective-permute-start.4 = (bf16[80,512]{1,0:T(8,128)(2,1)S(1)}, bf16[80,512]{1,0:T(8,128)(2,1)S(1)}, u32[]{:S(2)}, u32[]{:S(2)}) collective-permute-start(bf16[80,512]{1,0:T(8,128)(2,1)S(1)} %get-tuple-element.38), channel_id=1, source_target_pairs={{0,16},{4,20},{8,24},{12,28},{16,0},{20,4},{24,8},{28,12},{1,17},{... | collective-permute-start | bytes 245768 | tf_op jit(solution)/shard_map/ppermute | solution.py:507
  26.9 2.1 %collective-permute-start.6 = (bf16[80,512]{1,0:T(8,128)(2,1)S(1)}, bf16[80,512]{1,0:T(8,128)(2,1)S(1)}, u32[]{:S(2)}, u32[]{:S(2)}) collective-permute-start(bf16[80,512]{1,0:T(8,128)(2,1)S(1)} %get-tuple-element.41), channel_id=1, source_target_pairs={{0,20},{4,16},{8,28},{12,24},{16,4},{20,0},{24,12},{28,8},{1,21},{... | collective-permute-start | bytes 245768 | tf_op jit(solution)/shard_map/ppermute | solution.py:507
  29.0 1.0 %collective-permute-start.8 = (bf16[80,512]{1,0:T(8,128)(2,1)S(1)}, bf16[80,512]{1,0:T(8,128)(2,1)S(1)}, u32[]{:S(2)}, u32[]{:S(2)}) collective-permute-start(bf16[80,512]{1,0:T(8,128)(2,1)S(1)} %get-tuple-element.44), channel_id=1, source_target_pairs={{0,24},{4,28},{8,16},{12,20},{16,8},{20,12},{24,0},{28,4},{1,25},{... | collective-permute-start | bytes 245768 | tf_op jit(solution)/shard_map/ppermute | solution.py:507
  30.0 0.9 %collective-permute-start.10 = (bf16[80,512]{1,0:T(8,128)(2,1)S(1)}, bf16[80,512]{1,0:T(8,128)(2,1)S(1)}, u32[]{:S(2)}, u32[]{:S(2)}) collective-permute-start(bf16[80,512]{1,0:T(8,128)(2,1)S(1)} %get-tuple-element.47), channel_id=1, source_target_pairs={{0,28},{4,24},{8,20},{12,16},{16,12},{20,8},{24,4},{28,0},{1,29},{... | collective-permute-start | bytes 245768 | tf_op jit(solution)/shard_map/ppermute | solution.py:507
  30.9 5.8 %collective-permute-done.12.refs_9_ = bf16[8,56,512]{2,1,0:T(8,128)(2,1)S(1)} collective-permute-done((bf16[8,56,512]{2,1,0:T(8,128)(2,1)S(1)}, bf16[8,56,512]{2,1,0:T(8,128)(2,1)S(1)}, u32[]{:S(2)}, u32[]{:S(2)}) %collective-permute-start.12) | collective-permute-done | bytes 458784 | tf_op jit(solution)/shard_map/ppermute | solution.py:525
  36.7 0.0 copy-start.3
  36.7 0.0 copy-start.7
  36.8 0.0 copy-start.8
  36.8 0.0 copy-start.9
  36.8 4.0 %shard_map.104 = (f32[2,8,512]{2,1,0:T(8,128)S(1)}, bf16[4,10,16,512]{3,2,1,0:T(8,128)(2,1)S(1)}, bf16[4,9,16,512]{3,2,1,0:T(8,128)(2,1)S(1)}, bf16[4,9,16,512]{...) custom-call(bf16[168,512]{1,0:T(8,128)(2,1)S(1)} %get-tuple-element.32.refs_0_, ...), custom_call_target="tpu_custom_call" | custom-call | flops 2717908992 | bytes 4718592 | tf_op jit(solution)/shard_map/pallas_call | solution.py:452
  40.8 0.0 collective-permute-done.6.refs_5_
  40.8 0.7 %collective-permute-done.8.refs_6_ = bf16[80,512]{1,0:T(8,128)(2,1)S(1)} collective-permute-done((bf16[80,512]{1,0:T(8,128)(2,1)S(1)}, bf16[80,512]{1,0:T(8,128)(2,1)S(1)}, u32[]{:S(2)}, u32[]{:S(2)}) %collective-permute-start.8) | collective-permute-done | bytes 81952 | tf_op jit(solution)/shard_map/ppermute | solution.py:507
  41.5 2.7 %collective-permute-done.10.refs_7_ = bf16[80,512]{1,0:T(8,128)(2,1)S(1)} collective-permute-done((bf16[80,512]{1,0:T(8,128)(2,1)S(1)}, bf16[80,512]{1,0:T(8,128)(2,1)S(1)}, u32[]{:S(2)}, u32[]{:S(2)}) %collective-permute-start.10) | collective-permute-done | bytes 81952 | tf_op jit(solution)/shard_map/ppermute | solution.py:507
  44.2 13.5 %shard_map.105 = bf16[8,512,256]{2,1,0:T(8,128)(2,1)} custom-call(s32[8]{0:T(128)S(1)} %copy-done.9, bf16[168,512]{1,0:T(8,128)(2,1)S(1)} %get-tuple-element.32.refs_0_, bf16[168,512]{1,0:T(8,128)(2,1)S(1)} %collective-permute-done.refs_1_, bf16[168,512]{1,0:T(8,128)(2,1)S(1)} %collective-permute-done.1.refs_2_, ...), custom_call_target="tpu_custom_call" | custom-call | flops 8371830784 | bytes 8912896 | tf_op jit(solution)/shard_map/pallas_call | solution.py:472
  (20 shorter events, 0.1 us)
Async XLA Ops:
  0.0 1.2 %copy-start.1 = (bf16[1,8,128,512]{3,2,1,0:T(8,128)(2,1)S(1)}, bf16[1,8,128,512]{3,2,1,0:T(8,128)(2,1)}, u32[]{:S(2)}) copy-start(bf16[1,8,128,512]{3,2,1,0:T(8,128)(2,1)} %param.10) | copy-start | bytes 3145732
  1.8 6.0 %collective-permute-start.3 = (bf16[88,512]{1,0:T(8,128)(2,1)S(1)}, bf16[88,512]{1,0:T(8,128)(2,1)S(1)}, u32[]{:S(2)}, u32[]{:S(2)}) collective-permute-start(bf16[88,512]{1,0:T(8,128)(2,1)S(1)} %get-tuple-element.37), channel_id=1, source_target_pairs={{0,16},{4,20},{8,24},{12,28},{16,0},{20,4},{24,8},{28,12},{1,17},{... | collective-permute-start | bytes 270344 | tf_op jit(solution)/shard_map/ppermute | solution.py:507
  1.9 8.4 %collective-permute-start.5 = (bf16[88,512]{1,0:T(8,128)(2,1)S(1)}, bf16[88,512]{1,0:T(8,128)(2,1)S(1)}, u32[]{:S(2)}, u32[]{:S(2)}) collective-permute-start(bf16[88,512]{1,0:T(8,128)(2,1)S(1)} %get-tuple-element.40), channel_id=1, source_target_pairs={{0,20},{4,16},{8,28},{12,24},{16,4},{20,0},{24,12},{28,8},{1,21},{... | collective-permute-start | bytes 270344 | tf_op jit(solution)/shard_map/ppermute | solution.py:507
  5.2 16.6 %collective-permute-start = (bf16[168,512]{1,0:T(8,128)(2,1)S(1)}, bf16[168,512]{1,0:T(8,128)(2,1)S(1)}, u32[]{:S(2)}, u32[]{:S(2)}) collective-permute-start(bf16[168,512]{1,0:T(8,128)(2,1)S(1)} %get-tuple-element.33), channel_id=1, source_target_pairs={{0,4},{4,0},{8,12},{12,8},{16,20},{20,16},{24,28},{28,24},{1,5},{5... | collective-permute-start | bytes 516104 | tf_op jit(solution)/shard_map/ppermute | solution.py:507
  5.5 16.4 %collective-permute-start.1 = (bf16[168,512]{1,0:T(8,128)(2,1)S(1)}, bf16[168,512]{1,0:T(8,128)(2,1)S(1)}, u32[]{:S(2)}, u32[]{:S(2)}) collective-permute-start(bf16[168,512]{1,0:T(8,128)(2,1)S(1)} %get-tuple-element.34), channel_id=1, source_target_pairs={{0,8},{4,12},{8,0},{12,4},{16,24},{20,28},{24,16},{28,20},{1,9},{5... | collective-permute-start | bytes 516104 | tf_op jit(solution)/shard_map/ppermute | solution.py:507
  6.8 15.1 %collective-permute-start.2 = (bf16[168,512]{1,0:T(8,128)(2,1)S(1)}, bf16[168,512]{1,0:T(8,128)(2,1)S(1)}, u32[]{:S(2)}, u32[]{:S(2)}) collective-permute-start(bf16[168,512]{1,0:T(8,128)(2,1)S(1)} %get-tuple-element.35), channel_id=1, source_target_pairs={{0,12},{4,8},{8,4},{12,0},{16,28},{20,24},{24,20},{28,16},{1,13},{... | collective-permute-start | bytes 516104 | tf_op jit(solution)/shard_map/ppermute | solution.py:507
  7.9 8.5 %collective-permute-start.7 = (bf16[88,512]{1,0:T(8,128)(2,1)S(1)}, bf16[88,512]{1,0:T(8,128)(2,1)S(1)}, u32[]{:S(2)}, u32[]{:S(2)}) collective-permute-start(bf16[88,512]{1,0:T(8,128)(2,1)S(1)} %get-tuple-element.43), channel_id=1, source_target_pairs={{0,24},{4,28},{8,16},{12,20},{16,8},{20,12},{24,0},{28,4},{1,25},{... | collective-permute-start | bytes 270344 | tf_op jit(solution)/shard_map/ppermute | solution.py:507
  10.3 11.5 %collective-permute-start.9 = (bf16[88,512]{1,0:T(8,128)(2,1)S(1)}, bf16[88,512]{1,0:T(8,128)(2,1)S(1)}, u32[]{:S(2)}, u32[]{:S(2)}) collective-permute-start(bf16[88,512]{1,0:T(8,128)(2,1)S(1)} %get-tuple-element.46), channel_id=1, source_target_pairs={{0,28},{4,24},{8,20},{12,16},{16,12},{20,8},{24,4},{28,0},{1,29},{... | collective-permute-start | bytes 270344 | tf_op jit(solution)/shard_map/ppermute | solution.py:507
  13.4 1.7 %copy-start = (bf16[3,3,512,256]{3,2,1,0:T(8,128)(2,1)S(1)}, bf16[3,3,512,256]{3,2,1,0:T(8,128)(2,1)}, u32[]{:S(2)}) copy-start(bf16[3,3,512,256]{3,2,1,0:T(8,128)(2,1)} %param.15) | copy-start | bytes 7077892
  15.1 21.7 %copy-start.2 = (bf16[3,3,512,512]{3,2,1,0:T(8,128)(2,1)S(1)}, bf16[3,3,512,512]{3,2,1,0:T(8,128)(2,1)}, u32[]{:S(2)}) copy-start(bf16[3,3,512,512]{3,2,1,0:T(8,128)(2,1)} %refs_13_.1) | copy-start | bytes 14155780
  15.1 21.7 %copy-start.4 = (f32[512]{0:T(512)S(1)}, f32[512]{0:T(512)}, u32[]{:S(2)}) copy-start(f32[512]{0:T(512)} %param.11) | copy-start | bytes 6148
  15.1 21.7 %copy-start.5 = (f32[512]{0:T(512)S(1)}, f32[512]{0:T(512)}, u32[]{:S(2)}) copy-start(f32[512]{0:T(512)} %param.12) | copy-start | bytes 6148
  15.1 21.7 %copy-start.6 = (f32[512]{0:T(512)S(1)}, f32[512]{0:T(512)}, u32[]{:S(2)}) copy-start(f32[512]{0:T(512)} %param.14) | copy-start | bytes 6148
  21.9 2.2 %collective-permute-start.11 = (bf16[8,48,512]{2,1,0:T(8,128)(2,1)S(1)}, bf16[8,48,512]{2,1,0:T(8,128)(2,1)S(1)}, u32[]{:S(2)}, u32[]{:S(2)}) collective-permute-start(bf16[8,48,512]{2,1,0:T(8,128)(2,1)S(1)} %shard_map.101), channel_id=1, source_target_pairs={{0,1},{1,0},{2,3},{3,2},{4,5},{5,4},{6,7},{7,6},{8,9},{9,8},{10,11... | collective-permute-start | bytes 1179656 | tf_op jit(solution)/shard_map/ppermute | solution.py:525
  24.1 12.6 %collective-permute-start.12 = (bf16[8,56,512]{2,1,0:T(8,128)(2,1)S(1)}, bf16[8,56,512]{2,1,0:T(8,128)(2,1)S(1)}, u32[]{:S(2)}, u32[]{:S(2)}) collective-permute-start(bf16[8,56,512]{2,1,0:T(8,128)(2,1)S(1)} %shard_map.103), channel_id=1, source_target_pairs={{1,2},{2,1},{0,3},{3,0},{5,6},{6,5},{4,7},{7,4},{9,10},{10,9},{8,1... | collective-permute-start | bytes 1376264 | tf_op jit(solution)/shard_map/ppermute | solution.py:525
  25.7 15.1 %collective-permute-start.4 = (bf16[80,512]{1,0:T(8,128)(2,1)S(1)}, bf16[80,512]{1,0:T(8,128)(2,1)S(1)}, u32[]{:S(2)}, u32[]{:S(2)}) collective-permute-start(bf16[80,512]{1,0:T(8,128)(2,1)S(1)} %get-tuple-element.38), channel_id=1, source_target_pairs={{0,16},{4,20},{8,24},{12,28},{16,0},{20,4},{24,8},{28,12},{1,17},{... | collective-permute-start | bytes 245768 | tf_op jit(solution)/shard_map/ppermute | solution.py:507
  26.9 14.0 %collective-permute-start.6 = (bf16[80,512]{1,0:T(8,128)(2,1)S(1)}, bf16[80,512]{1,0:T(8,128)(2,1)S(1)}, u32[]{:S(2)}, u32[]{:S(2)}) collective-permute-start(bf16[80,512]{1,0:T(8,128)(2,1)S(1)} %get-tuple-element.41), channel_id=1, source_target_pairs={{0,20},{4,16},{8,28},{12,24},{16,4},{20,0},{24,12},{28,8},{1,21},{... | collective-permute-start | bytes 245768 | tf_op jit(solution)/shard_map/ppermute | solution.py:507
  29.0 12.5 %collective-permute-start.8 = (bf16[80,512]{1,0:T(8,128)(2,1)S(1)}, bf16[80,512]{1,0:T(8,128)(2,1)S(1)}, u32[]{:S(2)}, u32[]{:S(2)}) collective-permute-start(bf16[80,512]{1,0:T(8,128)(2,1)S(1)} %get-tuple-element.44), channel_id=1, source_target_pairs={{0,24},{4,28},{8,16},{12,20},{16,8},{20,12},{24,0},{28,4},{1,25},{... | collective-permute-start | bytes 245768 | tf_op jit(solution)/shard_map/ppermute | solution.py:507
  30.0 14.2 %collective-permute-start.10 = (bf16[80,512]{1,0:T(8,128)(2,1)S(1)}, bf16[80,512]{1,0:T(8,128)(2,1)S(1)}, u32[]{:S(2)}, u32[]{:S(2)}) collective-permute-start(bf16[80,512]{1,0:T(8,128)(2,1)S(1)} %get-tuple-element.47), channel_id=1, source_target_pairs={{0,28},{4,24},{8,20},{12,16},{16,12},{20,8},{24,4},{28,0},{1,29},{... | collective-permute-start | bytes 245768 | tf_op jit(solution)/shard_map/ppermute | solution.py:507
  36.7 7.5 %copy-start.3 = (bf16[3,256,256]{2,1,0:T(8,128)(2,1)S(1)}, bf16[3,256,256]{2,1,0:T(8,128)(2,1)}, u32[]{:S(2)}) copy-start(bf16[3,256,256]{2,1,0:T(8,128)(2,1)} %param.17) | copy-start | bytes 1179652
  36.7 7.5 %copy-start.7 = (f32[256]{0:T(256)S(1)}, f32[256]{0:T(256)}, u32[]{:S(2)}) copy-start(f32[256]{0:T(256)} %param.16) | copy-start | bytes 3076
  36.8 7.5 %copy-start.8 = (f32[256]{0:T(256)S(1)}, f32[256]{0:T(256)}, u32[]{:S(2)}) copy-start(f32[256]{0:T(256)} %param.18) | copy-start | bytes 3076
  36.8 7.5 %copy-start.9 = (s32[8]{0:T(128)S(1)}, s32[8]{0:T(128)}, u32[]{:S(2)}) copy-start(s32[8]{0:T(128)} %clip.1) | copy-start | bytes 100
